TPU v7x, 512 devices: a whole 4x8x8 slice. The times are simulated.
512 devices in a mesh: dp: 16 (over y, z_lo), fsdp: 32 (over x, z_hi, core).
Axes of the slice: x: 4, y: 8, z: 8 (z_hi: 4, z_lo: 2; z = z_hi * 2 + z_lo), core: 2. Of those that a mesh axis runs over, the one named last changes fastest.
Arguments:
- signal: bfloat16 [131072, 1024], P(('dp', 'fsdp')), may hold values from -6 to 6
- grad_gated: bfloat16 [131072, 512], P(('dp', 'fsdp')), may hold values from -24 to 24
- conv_weight: bfloat16 [1024, 3072], P('fsdp'), may hold values from -0.109375 to 0.109375
- source_seg: int32 [512, 32], P(('dp', 'fsdp')), may hold values from -1 to 1023, as said below
Outputs:
- gated_out: bfloat16 [131072, 512], P(('dp', 'fsdp'))
- grad_in: bfloat16 [131072, 1024], P(('dp', 'fsdp'))
- grad_weight: float32 [1024, 3072], P('fsdp')
Inputs may be any that keep to these rules, and one draw needn't show every extreme that they name: `source_seg`: -1 where a stream begins. The preceding segment holds the same position on its device as g on its own, no two segments of one device take their left context from the same device, and every segment precedes at most one segment.
All inputs are finite; a program needn't handle non-finite values.
Results may differ from a plain program's by a relative error of at most 0.0049.
Values may be sent and summed in bfloat16 or wider, within the bound.
A program may use at most 64 MiB of HBM per device.

v0:
```python
import math

import jax
import jax.numpy as jnp
from jax import lax
from jax.sharding import PartitionSpec as P

C = 1024
H = 512
DILATION_SIZE = 4


def tap_starts(context_row_block):
    return [context_row_block - (2 - selected_index) * DILATION_SIZE for selected_index in range(3)]


def per_device(signal, grad_gated, conv_weight, source_seg):
    peer_count = lax.axis_size("fsdp")
    seg_count = source_seg.shape[1]
    row_count = signal.shape[0]
    seg_rows = row_count // seg_count
    context_row_block = 2 * DILATION_SIZE
    starts = tap_starts(context_row_block)
    segments = signal.reshape(seg_count, seg_rows, C)
    sources = source_seg[0]
    source_dev = jnp.where(sources >= 0, sources // seg_count, -1)
    peers = jnp.arange(peer_count, dtype=jnp.int32)
    request_mask = (source_dev[None, :] == peers[:, None]).astype(jnp.int32)
    asked = lax.all_to_all(request_mask, "fsdp", split_axis=0, concat_axis=0, tiled=True)
    send_table = asked.astype(jnp.bfloat16)
    recv_table = (source_dev[:, None] == peers[None, :]).astype(jnp.bfloat16)
    outgoing = jnp.einsum(
        "ns,slc->nlc", send_table, segments, preferred_element_type=jnp.float32
    ).astype(jnp.bfloat16)
    incoming = lax.all_to_all(outgoing, "fsdp", split_axis=0, concat_axis=0, tiled=True)
    carries = jnp.einsum(
        "sn,nlc->slc", recv_table, incoming, preferred_element_type=jnp.float32
    ).astype(jnp.bfloat16)
    extended = jnp.concatenate([carries, segments], axis=1)
    full_weight = lax.all_gather(conv_weight, "fsdp", axis=0, tiled=True)
    contract_final_axis = (((1,), (1,)), ((), ()))
    contract_first = (((0,), (0,)), ((), ()))
    windows = [extended[:, start : start + seg_rows, :].reshape(row_count, C) for start in starts]
    preact = sum(
        (
            lax.dot_general(
                windows[selected_index],
                full_weight[:, selected_index * C : (selected_index + 1) * C],
                contract_final_axis,
                preferred_element_type=jnp.float32,
            )
            for selected_index in range(3)
        )
    )
    filter_act = jnp.tanh(preact[:, :H])
    gate_act = jax.nn.sigmoid(preact[:, H:])
    gated_out = (filter_act * gate_act).astype(jnp.bfloat16)
    upstream_wide = grad_gated.astype(jnp.float32)
    grad_pre = jnp.concatenate(
        [
            upstream_wide * gate_act * (1.0 - filter_act * filter_act),
            upstream_wide * filter_act * gate_act * (1.0 - gate_act),
        ],
        axis=1,
    ).astype(jnp.bfloat16)
    partial_value = jnp.concatenate(
        [
            lax.dot_general(
                grad_pre,
                windows[selected_index],
                contract_first,
                preferred_element_type=jnp.float32,
            ).astype(jnp.bfloat16)
            for selected_index in range(3)
        ],
        axis=1,
    )
    arrived = lax.all_to_all(partial_value, "fsdp", split_axis=0, concat_axis=0, tiled=True)
    shard_sum = jnp.sum(arrived.reshape(peer_count, -1, 3 * C), axis=0, dtype=jnp.float32)
    group_total = lax.psum(shard_sum, "dp")
    total_token_count = row_count * peer_count * lax.axis_size("dp")
    grad_weight = group_total * (1.0 / math.sqrt(total_token_count))
    back_proj = jnp.dot(grad_pre, full_weight, preferred_element_type=jnp.float32)
    back_proj = back_proj.reshape(seg_count, seg_rows, 3 * C)
    grad_ext = jnp.zeros((seg_count, context_row_block + seg_rows, C), jnp.float32)
    for selected_index, start in enumerate(starts):
        grad_ext = grad_ext.at[:, start : start + seg_rows, :].add(
            back_proj[:, :, selected_index * C : (selected_index + 1) * C]
        )
    outgoing_grad = jnp.einsum(
        "sn,slc->nlc",
        recv_table.astype(jnp.float32),
        grad_ext[:, :context_row_block, :],
        precision=lax.Precision.HIGHEST,
    )
    incoming_grad = lax.all_to_all(outgoing_grad, "fsdp", split_axis=0, concat_axis=0, tiled=True)
    tail_grad = jnp.einsum(
        "ns,nlc->slc",
        send_table.astype(jnp.float32),
        incoming_grad,
        precision=lax.Precision.HIGHEST,
    )
    grad_in = (
        grad_ext[:, context_row_block:, :].at[:, seg_rows - context_row_block :, :].add(tail_grad)
    )
    grad_in = grad_in.reshape(row_count, C).astype(jnp.bfloat16)
    return (gated_out, grad_in, grad_weight)


def solution(mesh):
    placed = (
        P(("dp", "fsdp"), None),
        P(("dp", "fsdp"), None),
        P("fsdp", None),
        P(("dp", "fsdp"), None),
    )
    return jax.shard_map(
        per_device,
        mesh=mesh,
        in_specs=placed,
        out_specs=(P(("dp", "fsdp"), None), P(("dp", "fsdp"), None), P("fsdp", None)),
        check_vma=False,
    )
```

profile of v0, /device:TPU:6, one launch (start us, length us, event | category | flops | bytes accessed | tf_op | source)
XLA Modules:
  0.0 440.8 jit_solution(733692016285793341)
XLA Ops:
  8.6 21.1 %all_to_all.25 = s32[32,1,32]{2,1,0:T(1,128)S(1)} all-to-all(s32[32,1,32]{2,1,0:T(1,128)S(1)} %compare_convert_fusion), channel_id=1, replica_groups=mesh['dp'=16,'fsdp'=32] {'fsdp'}, dimensions={0} | all-to-all | bytes 8192 | tf_op jit(solution)/shard_map/all_to_all | solution.py:29
  29.7 1.8 convolution_convert_fusion.4
  31.6 1.1 copy.20
  32.7 5.8 %all-to-all-start.1 = ((bf16[32,8,1024]{2,1,0:T(8,128)(2,1)}), bf16[32,8,1024]{2,1,0:T(8,128)(2,1)S(1)}, u32[]{:S(2)}, u32[]{:S(2)}) async-start(bf16[32,8,1024]{2,1,0:T(8,128)(2,1)} %copy.20), calls=%async_computation.1 | async-start | bytes 1048576 | tf_op jit(solution)/shard_map/all_to_all | solution.py:35
  38.4 1.3 copy.19
  39.8 16.9 %all-to-all-done.1 = bf16[32,8,1024]{2,1,0:T(8,128)(2,1)S(1)} async-done(((bf16[32,8,1024]{2,1,0:T(8,128)(2,1)}), bf16[32,8,1024]{2,1,0:T(8,128)(2,1)S(1)}, u32[]{:S(2)}, u32[]{:S(2)}) %all-to-all-start.1) | async-done | bytes 524320 | tf_op jit(solution)/shard_map/all_to_all | solution.py:35
  57.5 39.6 %all-gather.2.cloned.1.call-done = bf16[1024,3072]{1,0:T(8,128)(2,1)} async-done(((bf16[32,3072]{1,0:T(8,128)(2,1)}), bf16[1024,3072]{1,0:T(8,128)(2,1)}) %all-gather.2.cloned.1.call-update) | async-done | bytes 6291472 | tf_op jit(solution)/shard_map/all_gather | solution.py:40
  97.0 2.3 fusion
  99.4 2.5 fusion.2
  101.9 2.5 fusion.9
  107.8 13.4 %pad_maximum_fusion = bf16[1024,3072]{0,1:T(8,128)(2,1)} fusion(bf16[1024,1024]{0,1:T(8,128)(2,1)S(1)} %convolution_convert_fusion, bf16[1024,1024]{0,1:T(8,128)(2,1)S(1)} %convolution_convert_fusion.1, bf16[1024,1024]{0,1:T(8,128)(2,1)S(1)} %convolution_convert_fusion.2), kind=kLoop, calls=%fused_computation.1 | loop fusion | flops 18874368 | bytes 12582912 | tf_op jit(solution)/shard_map/concatenate | solution.py:66
  121.2 8.6 %copy.33 = bf16[1024,3072]{1,0:T(8,128)(2,1)} copy(bf16[1024,3072]{0,1:T(8,128)(2,1)} %pad_maximum_fusion) | data formatting | bytes 12582912 | tf_op jit(solution)/shard_map/concatenate | solution.py:66
  129.9 6.9 %all-to-all-start.3 = ((bf16[32,32,3072]{2,1,0:T(8,128)(2,1)}), bf16[32,32,3072]{2,1,0:T(8,128)(2,1)}, u32[]{:S(2)}, u32[]{:S(2)}) async-start(bf16[32,32,3072]{2,1,0:T(8,128)(2,1)} %bitcast.44), calls=%async_computation.3 | async-start | bytes 12582912 | tf_op jit(solution)/shard_map/all_to_all | solution.py:78
  136.7 4.6 %convolution_bitcast_fusion = f32[32,8,3072]{2,1,0:T(8,128)S(1)} fusion(bf16[1024,3072]{1,0:T(8,128)(2,1)} %all-gather.2.cloned.1.call-done, bf16[256,512]{1,0:T(8,128)(2,1)S(1)} %get-tuple-element.63, bf16[256,512]{1,0:T(8,128)(2,1)S(1)} %get-tuple-element.62), kind=kOutput, calls=%fused_computation.2 | convolution fusion | flops 1611661312 | bytes 9961472 | tf_op jit(solution)/shard_map/dot_general | solution.py:83
  141.3 1.4 fusion.45
  145.1 1.6 copy.29
  146.7 130.7 %all-to-all-done.3 = bf16[32,32,3072]{2,1,0:T(8,128)(2,1)} async-done(((bf16[32,32,3072]{2,1,0:T(8,128)(2,1)}), bf16[32,32,3072]{2,1,0:T(8,128)(2,1)}, u32[]{:S(2)}, u32[]{:S(2)}) %all-to-all-start.3) | async-done | bytes 6291488 | tf_op jit(solution)/shard_map/all_to_all | solution.py:78
  277.4 8.2 %all-to-all-start.2 = ((f32[32,8,1024]{2,1,0:T(8,128)}), f32[32,8,1024]{2,1,0:T(8,128)S(1)}, u32[]{:S(2)}, u32[]{:S(2)}) async-start(f32[32,8,1024]{2,1,0:T(8,128)} %copy.29), calls=%async_computation.2 | async-start | bytes 2097152 | tf_op jit(solution)/shard_map/all_to_all | solution.py:96
  285.6 4.8 %convert_reduce_fusion = f32[32,3072]{1,0:T(8,128)} fusion(bf16[32,32,3072]{2,1,0:T(8,128)(2,1)} %all-to-all-done.3), kind=kLoop, calls=%fused_computation | loop fusion | flops 6193152 | bytes 6684672 | tf_op jit(solution)/shard_map/reduce_sum | solution.py:79
  290.4 20.9 %all-to-all-done.2 = f32[32,8,1024]{2,1,0:T(8,128)S(1)} async-done(((f32[32,8,1024]{2,1,0:T(8,128)}), f32[32,8,1024]{2,1,0:T(8,128)S(1)}, u32[]{:S(2)}, u32[]{:S(2)}) %all-to-all-start.2) | async-done | bytes 1048608 | tf_op jit(solution)/shard_map/all_to_all | solution.py:96
  311.3 3.0 fusion.12
  314.4 1.1 copy.68
  315.4 116.8 %all-reduce.3.cloned.1.call-done = f32[32,3072]{1,0:T(8,128)} async-done(((f32[32,3072]{1,0:T(8,128)}), f32[32,3072]{1,0:T(8,128)}) %all-reduce.3.cloned.1.call-update) | async-done | bytes 393232 | tf_op jit(solution)/shard_map/psum | solution.py:80
  432.2 1.8 broadcast_multiply_fusion
  (23 shorter events, 8.2 us)
Async XLA Ops:
  7.2 32.6 %copy-start.2 = (s32[1,32]{1,0:T(1,128)S(1)}, s32[1,32]{1,0:T(1,128)}, u32[]{:S(2)}) copy-start(s32[1,32]{1,0:T(1,128)} %param.17) | copy-start | bytes 388
  7.2 89.9 %copy-start = (bf16[256,1024]{1,0:T(8,128)(2,1)S(1)}, bf16[256,1024]{1,0:T(8,128)(2,1)}, u32[]{:S(2)}) copy-start(bf16[256,1024]{1,0:T(8,128)(2,1)} %param.14) | copy-start | bytes 1572868
  7.2 89.9 %all-gather.2.cloned.1.call-start = ((), (), s32[]{:S(2)}) async-start(), calls=%async_computation.4 | async-start | bytes 6488064 | tf_op jit(solution)/shard_map/all_gather | solution.py:40
  32.7 24.0 %all-to-all-start.1 = ((bf16[32,8,1024]{2,1,0:T(8,128)(2,1)}), bf16[32,8,1024]{2,1,0:T(8,128)(2,1)S(1)}, u32[]{:S(2)}, u32[]{:S(2)}) async-start(bf16[32,8,1024]{2,1,0:T(8,128)(2,1)} %copy.20), calls=%async_computation.1 | async-start | bytes 1048576 | tf_op jit(solution)/shard_map/all_to_all | solution.py:35
  99.4 5.0 %copy-start.1 = (bf16[256,512]{1,0:T(8,128)(2,1)S(1)}, bf16[256,512]{1,0:T(8,128)(2,1)}, u32[]{:S(2)}) copy-start(bf16[256,512]{1,0:T(8,128)(2,1)} %param.15) | copy-start | bytes 786436
  129.9 147.5 %all-to-all-start.3 = ((bf16[32,32,3072]{2,1,0:T(8,128)(2,1)}), bf16[32,32,3072]{2,1,0:T(8,128)(2,1)}, u32[]{:S(2)}, u32[]{:S(2)}) async-start(bf16[32,32,3072]{2,1,0:T(8,128)(2,1)} %bitcast.44), calls=%async_computation.3 | async-start | bytes 12582912 | tf_op jit(solution)/shard_map/all_to_all | solution.py:78
  277.4 33.9 %all-to-all-start.2 = ((f32[32,8,1024]{2,1,0:T(8,128)}), f32[32,8,1024]{2,1,0:T(8,128)S(1)}, u32[]{:S(2)}, u32[]{:S(2)}) async-start(f32[32,8,1024]{2,1,0:T(8,128)} %copy.29), calls=%async_computation.2 | async-start | bytes 2097152 | tf_op jit(solution)/shard_map/all_to_all | solution.py:96
  285.6 146.6 %all-reduce.3.cloned.1.call-start = ((), (), s32[]{:S(2)}) async-start(), calls=%async_computation.5 | async-start | bytes 786432 | tf_op jit(solution)/shard_map/psum | solution.py:80
Sparse Core Ops, SparseCore 0:
  11.1 85.8 all-gather.1
  290.6 141.6 all-reduce.2
where the time goes:
time: 442 us; the launch traced here: 441 us
  waiting for transfers between devices  325 us (74%)
  other arithmetic  22.7 us (5%)
  blocking collectives  21.1 us (5%)
  starting transfers between devices  20.9 us (5%)
  matrix products  20.5 us (5%)
  local copies, waits for them, and re-layouts  16 us (4%)
  between operations  14.2 us (3%)
    all_to_all x1, waiting for transfers between devices, per_device(): lax.all_to_all(partial_value, 'fsdp', split_axis=0, concat_axis=0, tiled=...  131 us
    psum x1, waiting for transfers between devices, per_device(): group_total = lax.psum(shard_sum, 'dp')  117 us
    all_gather x1, waiting for transfers between devices, per_device(): full_weight = lax.all_gather(conv_weight, 'fsdp', axis=0, tiled=True)  39.6 us
    all_to_all x1, blocking collectives, per_device(): lax.all_to_all(request_mask, 'fsdp', split_axis=0, concat_axis=0, tiled=T...  21.1 us
    all_to_all x1, waiting for transfers between devices, per_device(): lax.all_to_all(outgoing_grad, 'fsdp', split_axis=0, concat_axis=0, tiled=...  20.9 us
    all_to_all x1, waiting for transfers between devices, per_device(): lax.all_to_all(outgoing, 'fsdp', split_axis=0, concat_axis=0, tiled=True)  16.9 us
    concatenate x1, other arithmetic, per_device(): jnp.concatenate([lax.dot_general(grad_pre, windows[selected_index], contr...  13.4 us
  transfers between devices with their start and end apart: 5, of which 5 were waited for; matrix products, arithmetic and copies ran while one was open for 6% of the time, Pallas kernels for 0%

commit v1 on v0

--- a/solution.py
+++ b/solution.py
@@ -1,13 +1,106 @@
+import functools
 import math
 
 import jax
 import jax.numpy as jnp
 from jax import lax
+from jax.experimental import pallas as pl
+from jax.experimental.pallas import tpu as pltpu
 from jax.sharding import PartitionSpec as P
+
+MESH = pl.DeviceIdType.MESH
 
 C = 1024
 H = 512
 DILATION_SIZE = 4
+
+
+def all_reduce_kernel(axis, n, x_ref, out_ref, gathered, summed, send_sems, recv_sems, out_send, out_recv):
+    me = lax.axis_index(axis)
+    barrier = pltpu.get_barrier_semaphore()
+    for k in range(1, n):
+        peer = lax.rem(me + k, n)
+        pl.semaphore_signal(barrier, inc=1, device_id={axis: peer}, device_id_type=MESH)
+    pl.semaphore_wait(barrier, n - 1)
+    sends = []
+    for k in range(1, n):
+        peer = lax.rem(me + k, n)
+        copy = pltpu.make_async_remote_copy(
+            src_ref=x_ref.at[peer],
+            dst_ref=gathered.at[me],
+            send_sem=send_sems.at[peer],
+            recv_sem=recv_sems.at[me],
+            device_id={axis: peer},
+            device_id_type=MESH,
+        )
+        copy.start()
+        sends.append(copy)
+    gathered[me] = x_ref[me]
+    for k in range(1, n):
+        peer = lax.rem(me + k, n)
+        pltpu.make_async_remote_copy(
+            src_ref=x_ref.at[peer],
+            dst_ref=gathered.at[peer],
+            send_sem=send_sems.at[peer],
+            recv_sem=recv_sems.at[peer],
+            device_id={axis: peer},
+            device_id_type=MESH,
+        ).wait_recv()
+    for copy in sends:
+        copy.wait_send()
+    total = gathered[0]
+    for k in range(1, n):
+        total = total + gathered[k]
+    summed[...] = total
+    out_ref[me] = total
+    shares = []
+    for k in range(1, n):
+        peer = lax.rem(me + k, n)
+        copy = pltpu.make_async_remote_copy(
+            src_ref=summed,
+            dst_ref=out_ref.at[me],
+            send_sem=out_send.at[peer],
+            recv_sem=out_recv.at[me],
+            device_id={axis: peer},
+            device_id_type=MESH,
+        )
+        copy.start()
+        shares.append(copy)
+    for k in range(1, n):
+        peer = lax.rem(me + k, n)
+        pltpu.make_async_remote_copy(
+            src_ref=summed,
+            dst_ref=out_ref.at[peer],
+            send_sem=out_send.at[peer],
+            recv_sem=out_recv.at[peer],
+            device_id={axis: peer},
+            device_id_type=MESH,
+        ).wait_recv()
+    for copy in shares:
+        copy.wait_send()
+
+
+def all_reduce(x, axis):
+    n = lax.axis_size(axis)
+    shape = x.shape
+    blocks = x.reshape(n, -1, 128)
+    block_shape = blocks.shape[1:]
+    out = pl.pallas_call(
+        functools.partial(all_reduce_kernel, axis, n),
+        out_shape=jax.ShapeDtypeStruct(blocks.shape, x.dtype),
+        in_specs=[pl.BlockSpec(memory_space=pltpu.VMEM)],
+        out_specs=pl.BlockSpec(memory_space=pltpu.VMEM),
+        scratch_shapes=[
+            pltpu.VMEM(blocks.shape, x.dtype),
+            pltpu.VMEM(block_shape, x.dtype),
+            pltpu.SemaphoreType.DMA((n,)),
+            pltpu.SemaphoreType.DMA((n,)),
+            pltpu.SemaphoreType.DMA((n,)),
+            pltpu.SemaphoreType.DMA((n,)),
+        ],
+        compiler_params=pltpu.CompilerParams(collective_id=0, has_side_effects=True),
+    )(blocks)
+    return out.reshape(shape)
 
 
 def tap_starts(context_row_block):
@@ -77,7 +170,7 @@
     )
     arrived = lax.all_to_all(partial_value, "fsdp", split_axis=0, concat_axis=0, tiled=True)
     shard_sum = jnp.sum(arrived.reshape(peer_count, -1, 3 * C), axis=0, dtype=jnp.float32)
-    group_total = lax.psum(shard_sum, "dp")
+    group_total = all_reduce(shard_sum, "dp")
     total_token_count = row_count * peer_count * lax.axis_size("dp")
     grad_weight = group_total * (1.0 / math.sqrt(total_token_count))
     back_proj = jnp.dot(grad_pre, full_weight, preferred_element_type=jnp.float32)

time: 442 us -> 341 us (0.77)
  waiting for transfers between devices: 325 us -> 195 us
  Pallas kernels: 0 us -> 28.6 us
    psum x1 -> x0, waiting for transfers between devices: 117 us -> none  [per_device(): group_total = lax.psum(shard_sum, 'dp')]
    pallas_call x0 -> x1, Pallas kernels: none -> 28.6 us  [all_reduce(): pl.pallas_call(functools.partial(all_reduce_kernel, axis, n), out_shape=j...]
    all_to_all x1, waiting for transfers between devices: 20.9 us -> 1.31 us  [per_device(): lax.all_to_all(outgoing_grad, 'fsdp', split_axis=0, concat_axis=0, tiled=...]
    all_to_all x1, waiting for transfers between devices: 131 us -> 137 us  [per_device(): lax.all_to_all(partial_value, 'fsdp', split_axis=0, concat_axis=0, tiled=...]
  transfers between devices with their start and end apart: 5 -> 4, of which waited for: 5 -> 4; matrix products, arithmetic and copies ran while one was open for 6% -> 11% of each run, Pallas kernels for 0% -> 0%
where the time goes in v1:
time: 341 us; the launch traced here: 338 us
  waiting for transfers between devices  195 us (57%)
  Pallas kernels  28.6 us (8%)
  starting transfers between devices  21.3 us (6%)
  other arithmetic  21.2 us (6%)
  blocking collectives  21.1 us (6%)
  matrix products  18.4 us (5%)
  local copies, waits for them, and re-layouts  17.6 us (5%)
  between operations  14.3 us (4%)
    all_to_all x1, waiting for transfers between devices, per_device(): lax.all_to_all(partial_value, 'fsdp', split_axis=0, concat_axis=0, tiled=...  137 us
    all_gather x1, waiting for transfers between devices, per_device(): full_weight = lax.all_gather(conv_weight, 'fsdp', axis=0, tiled=True)  39.5 us
    pallas_call x1, Pallas kernels, all_reduce(): pl.pallas_call(functools.partial(all_reduce_kernel, axis, n), out_shape=j...  28.6 us
    all_to_all x1, blocking collectives, per_device(): lax.all_to_all(request_mask, 'fsdp', split_axis=0, concat_axis=0, tiled=T...  21.1 us
    all_to_all x1, waiting for transfers between devices, per_device(): lax.all_to_all(outgoing, 'fsdp', split_axis=0, concat_axis=0, tiled=True)  16.9 us
    concatenate x1, other arithmetic, per_device(): jnp.concatenate([lax.dot_general(grad_pre, windows[selected_index], contr...  13.4 us
    all_to_all x1, starting transfers between devices, per_device(): lax.all_to_all(partial_value, 'fsdp', split_axis=0, concat_axis=0, tiled=...  8.66 us
    concatenate x1, local copies, waits for them, and re-layouts, per_device(): jnp.concatenate([lax.dot_general(grad_pre, windows[selected_index], contr...  8.66 us
  transfers between devices with their start and end apart: 4, of which 4 were waited for; matrix products, arithmetic and copies ran while one was open for 11% of the time, Pallas kernels for 0%

profile of v1, /device:TPU:6, one launch (start us, length us, event | category | flops | bytes accessed | tf_op | source)
XLA Modules:
  0.0 337.5 jit_solution(10109041193145346631)
XLA Ops:
  8.6 21.1 %all_to_all.25 = s32[32,1,32]{2,1,0:T(1,128)S(1)} all-to-all(s32[32,1,32]{2,1,0:T(1,128)S(1)} %compare_convert_fusion), channel_id=1, replica_groups=mesh['dp'=16,'fsdp'=32] {'fsdp'}, dimensions={0} | all-to-all | bytes 8192 | tf_op jit(solution)/shard_map/all_to_all | solution.py:122
  29.7 1.8 convolution_convert_fusion.4
  31.6 1.1 copy.20
  32.7 5.8 %all-to-all-start.1 = ((bf16[32,8,1024]{2,1,0:T(8,128)(2,1)}), bf16[32,8,1024]{2,1,0:T(8,128)(2,1)S(1)}, u32[]{:S(2)}, u32[]{:S(2)}) async-start(bf16[32,8,1024]{2,1,0:T(8,128)(2,1)} %copy.20), calls=%async_computation.1 | async-start | bytes 1048576 | tf_op jit(solution)/shard_map/all_to_all | solution.py:128
  38.4 1.3 copy.19
  39.8 16.9 %all-to-all-done.1 = bf16[32,8,1024]{2,1,0:T(8,128)(2,1)S(1)} async-done(((bf16[32,8,1024]{2,1,0:T(8,128)(2,1)}), bf16[32,8,1024]{2,1,0:T(8,128)(2,1)S(1)}, u32[]{:S(2)}, u32[]{:S(2)}) %all-to-all-start.1) | async-done | bytes 524320 | tf_op jit(solution)/shard_map/all_to_all | solution.py:128
  57.5 39.5 %all-gather.2.cloned.1.call-done = bf16[1024,3072]{1,0:T(8,128)(2,1)} async-done(((bf16[32,3072]{1,0:T(8,128)(2,1)}), bf16[1024,3072]{1,0:T(8,128)(2,1)}) %all-gather.2.cloned.1.call-update) | async-done | bytes 6291472 | tf_op jit(solution)/shard_map/all_gather | solution.py:133
  97.0 2.5 fusion
  99.5 2.5 fusion.2
  104.0 1.8 convolution_bitcast_fusion
  105.8 1.3 fusion.45
  109.5 1.6 copy.29
  111.1 6.9 %all-to-all-start.2 = ((f32[32,8,1024]{2,1,0:T(8,128)}), f32[32,8,1024]{2,1,0:T(8,128)}, u32[]{:S(2)}, u32[]{:S(2)}) async-start(f32[32,8,1024]{2,1,0:T(8,128)} %copy.29), calls=%async_computation.2 | async-start | bytes 2097152 | tf_op jit(solution)/shard_map/all_to_all | solution.py:189
  118.0 1.9 convolution_convert_fusion.2
  119.9 2.0 convolution_convert_fusion.1
  122.6 13.4 %pad_maximum_fusion = bf16[1024,3072]{0,1:T(8,128)(2,1)} fusion(bf16[1024,1024]{0,1:T(8,128)(2,1)S(1)} %convolution_convert_fusion, bf16[1024,1024]{0,1:T(8,128)(2,1)S(1)} %convolution_convert_fusion.1, bf16[1024,1024]{0,1:T(8,128)(2,1)S(1)} %convolution_convert_fusion.2), kind=kLoop, calls=%fused_computation.1 | loop fusion | flops 18874368 | bytes 12582912 | tf_op jit(solution)/shard_map/concatenate | solution.py:159
  136.0 8.7 %copy.33 = bf16[1024,3072]{1,0:T(8,128)(2,1)} copy(bf16[1024,3072]{0,1:T(8,128)(2,1)} %pad_maximum_fusion) | data formatting | bytes 12582912 | tf_op jit(solution)/shard_map/concatenate | solution.py:159
  144.6 1.3 all-to-all-done.2
  145.9 8.7 %all-to-all-start.3 = ((bf16[32,32,3072]{2,1,0:T(8,128)(2,1)}), bf16[32,32,3072]{2,1,0:T(8,128)(2,1)}, u32[]{:S(2)}, u32[]{:S(2)}) async-start(bf16[32,32,3072]{2,1,0:T(8,128)(2,1)} %bitcast.44), calls=%async_computation.3 | async-start | bytes 12582912 | tf_op jit(solution)/shard_map/all_to_all | solution.py:171
  154.6 3.0 fusion.12
  157.6 1.1 copy.68
  158.7 136.6 %all-to-all-done.3 = bf16[32,32,3072]{2,1,0:T(8,128)(2,1)} async-done(((bf16[32,32,3072]{2,1,0:T(8,128)(2,1)}), bf16[32,32,3072]{2,1,0:T(8,128)(2,1)}, u32[]{:S(2)}, u32[]{:S(2)}) %all-to-all-start.3) | async-done | bytes 6291488 | tf_op jit(solution)/shard_map/all_to_all | solution.py:171
  295.3 4.0 %convert_reduce_fusion = f32[32,3072]{1,0:T(8,128)S(1)} fusion(bf16[32,32,3072]{2,1,0:T(8,128)(2,1)} %all-to-all-done.3), kind=kLoop, calls=%fused_computation | loop fusion | flops 6193152 | bytes 6684672 | tf_op jit(solution)/shard_map/reduce_sum | solution.py:172
  300.2 28.6 %shard_map.72 = f32[16,48,128]{2,1,0:T(8,128)} custom-call(f32[16,48,128]{2,1,0:T(8,128)} %reshape.227.x_ref), custom_call_target="tpu_custom_call" | custom-call | tf_op jit(solution)/shard_map/pallas_call | solution.py:88
  (33 shorter events, 10.0 us)
Async XLA Ops:
  7.2 32.6 %copy-start.7 = (s32[1,32]{1,0:T(1,128)S(1)}, s32[1,32]{1,0:T(1,128)}, u32[]{:S(2)}) copy-start(s32[1,32]{1,0:T(1,128)} %param.17) | copy-start | bytes 388
  7.2 89.9 %copy-start = (bf16[256,1024]{1,0:T(8,128)(2,1)S(1)}, bf16[256,1024]{1,0:T(8,128)(2,1)}, u32[]{:S(2)}) copy-start(bf16[256,1024]{1,0:T(8,128)(2,1)} %param.14) | copy-start | bytes 1572868
  7.2 89.8 %all-gather.2.cloned.1.call-start = ((), (), s32[]{:S(2)}) async-start(), calls=%async_computation.4 | async-start | bytes 6488064 | tf_op jit(solution)/shard_map/all_gather | solution.py:133
  32.7 24.0 %all-to-all-start.1 = ((bf16[32,8,1024]{2,1,0:T(8,128)(2,1)}), bf16[32,8,1024]{2,1,0:T(8,128)(2,1)S(1)}, u32[]{:S(2)}, u32[]{:S(2)}) async-start(bf16[32,8,1024]{2,1,0:T(8,128)(2,1)} %copy.20), calls=%async_computation.1 | async-start | bytes 1048576 | tf_op jit(solution)/shard_map/all_to_all | solution.py:128
  57.5 42.0 %copy-start.4 = (bf16[32,8,1024]{2,0,1:T(8,128)(2,1)}, bf16[32,8,1024]{2,0,1:T(8,128)(2,1)S(1)}, u32[]{:S(2)}) copy-start(bf16[32,8,1024]{2,0,1:T(8,128)(2,1)S(1)} %pad_maximum_fusion.1) | copy-start | bytes 1572868
  97.0 5.0 %copy-start.5 = (bf16[1024,3072]{1,0:T(8,128)(2,1)S(1)}, bf16[1024,3072]{1,0:T(8,128)(2,1)}, u32[]{:S(2)}) copy-start(bf16[1024,3072]{1,0:T(8,128)(2,1)} %all-gather.2.cloned.1.call-done) | copy-start | bytes 18874372
  99.5 3.4 %copy-start.6 = (bf16[256,512]{1,0:T(8,128)(2,1)S(1)}, bf16[256,512]{1,0:T(8,128)(2,1)}, u32[]{:S(2)}) copy-start(bf16[256,512]{1,0:T(8,128)(2,1)} %param.15) | copy-start | bytes 786436
  103.9 1.8 copy-start.2
  111.1 34.8 %all-to-all-start.2 = ((f32[32,8,1024]{2,1,0:T(8,128)}), f32[32,8,1024]{2,1,0:T(8,128)}, u32[]{:S(2)}, u32[]{:S(2)}) async-start(f32[32,8,1024]{2,1,0:T(8,128)} %copy.29), calls=%async_computation.2 | async-start | bytes 2097152 | tf_op jit(solution)/shard_map/all_to_all | solution.py:189
  118.0 3.9 %copy-start.3 = (bf16[256,512]{1,0:T(8,128)(2,1)S(1)}, bf16[256,512]{1,0:T(8,128)(2,1)}, u32[]{:S(2)}) copy-start(bf16[256,512]{1,0:T(8,128)(2,1)} %copy-done.2) | copy-start | bytes 786436
  145.9 8.7 %copy-start.1 = (f32[32,8,1024]{2,1,0:T(8,128)S(1)}, f32[32,8,1024]{2,1,0:T(8,128)}, u32[]{:S(2)}) copy-start(f32[32,8,1024]{2,1,0:T(8,128)} %get-tuple-element.59) | copy-start | bytes 3145732
  145.9 149.4 %all-to-all-start.3 = ((bf16[32,32,3072]{2,1,0:T(8,128)(2,1)}), bf16[32,32,3072]{2,1,0:T(8,128)(2,1)}, u32[]{:S(2)}, u32[]{:S(2)}) async-start(bf16[32,32,3072]{2,1,0:T(8,128)(2,1)} %bitcast.44), calls=%async_computation.3 | async-start | bytes 12582912 | tf_op jit(solution)/shard_map/all_to_all | solution.py:171
Sparse Core Ops, SparseCore 0:
  11.1 85.8 all-gather.1

commit v2 on v1

--- a/solution.py
+++ b/solution.py
@@ -13,6 +13,7 @@
 C = 1024
 H = 512
 DILATION_SIZE = 4
+Z_HI = 4
 
 
 def all_reduce_kernel(axis, n, x_ref, out_ref, gathered, summed, send_sems, recv_sems, out_send, out_recv):
@@ -101,6 +102,150 @@
         compiler_params=pltpu.CompilerParams(collective_id=0, has_side_effects=True),
     )(blocks)
     return out.reshape(shape)
+
+
+def grad_reduce_kernel(z_hi, scale, p_ref, out_ref, recv_c, s1b, recv_x, s2, recv_z, s3, recv_y, g16,
+                       core_sems, x_send, x_recv, z_send, z_recv, y_send, y_recv, g_send, g_recv, pair_sems):
+    n_x = recv_x.shape[0]
+    n_z = 2 * z_hi
+    n_y = recv_y.shape[0]
+    band = recv_c.shape[1]
+    half = s2.shape[1]
+    width = recv_y.shape[2]
+    f = lax.axis_index("fsdp")
+    d = lax.axis_index("dp")
+    c = lax.rem(f, 2)
+    zh = lax.rem(f // 2, z_hi)
+    x = f // (2 * z_hi)
+    zl = lax.rem(d, 2)
+    y = d // 2
+    z = zh * 2 + zl
+
+    def device(x_, zh_, c_, y_, zl_):
+        return {"dp": y_ * 2 + zl_, "fsdp": (x_ * z_hi + zh_) * 2 + c_}
+
+    partner = device(x, zh, 1 - c, y, zl)
+    x_peers = [lax.rem(x + k, n_x) for k in range(1, n_x)]
+    z_peers = [lax.rem(z + k, n_z) for k in range(1, n_z)]
+    y_peers = [lax.rem(y + k, n_y) for k in range(1, n_y)]
+    everyone = [partner]
+    everyone += [device(xp, zh, c, y, zl) for xp in x_peers]
+    everyone += [device(x, zp // 2, c, y, lax.rem(zp, 2)) for zp in z_peers]
+    everyone += [device(x, zh, c, yp, zl) for yp in y_peers]
+    barrier = pltpu.get_barrier_semaphore()
+    for peer in everyone:
+        pl.semaphore_signal(barrier, inc=1, device_id=peer, device_id_type=MESH)
+    pl.semaphore_wait(barrier, len(everyone))
+
+    def exchange(src_of, dst_of, send_sems, recv_sems, peers, mine, device_of):
+        sends = []
+        for p in peers:
+            copy = pltpu.make_async_remote_copy(
+                src_ref=src_of(p), dst_ref=dst_of(mine), send_sem=send_sems.at[p],
+                recv_sem=recv_sems.at[mine], device_id=device_of(p), device_id_type=MESH)
+            copy.start()
+            sends.append(copy)
+        for p in peers:
+            pltpu.make_async_remote_copy(
+                src_ref=src_of(p), dst_ref=dst_of(p), send_sem=send_sems.at[p],
+                recv_sem=recv_sems.at[p], device_id=device_of(p), device_id_type=MESH).wait_recv()
+        for copy in sends:
+            copy.wait_send()
+
+    core_copy = pltpu.make_async_remote_copy(
+        src_ref=p_ref.at[1 - c], dst_ref=recv_c, send_sem=core_sems.at[0],
+        recv_sem=core_sems.at[1], device_id=partner, device_id_type=MESH)
+    core_copy.start()
+    core_copy.wait()
+
+    rows = 32
+    chunks = band // rows
+
+    def round_two_sums(i, carry):
+        xi, r = i // chunks, lax.rem(i, chunks)
+        at = pl.ds(pl.multiple_of(r * rows, rows), rows)
+        both = p_ref[c, xi, at, :].astype(jnp.float32) + recv_c[xi, at, :].astype(jnp.float32)
+        s1b[xi, at, :] = both.astype(s1b.dtype)
+        return carry
+
+    lax.fori_loop(0, n_x * chunks, round_two_sums, 0)
+    exchange(lambda p: s1b.at[p], lambda p: recv_x.at[p], x_send, x_recv, x_peers, x,
+             lambda p: device(p, zh, c, y, zl))
+
+    def sum_x(j, carry):
+        at = pl.ds(pl.multiple_of(j * half, half), half)
+        total = p_ref[c, x, at, :].astype(jnp.float32) + recv_c[x, at, :].astype(jnp.float32)
+        for p in x_peers:
+            total = total + recv_x[p, at, :].astype(jnp.float32)
+        s2[j] = total
+        return carry
+
+    lax.fori_loop(0, n_z, sum_x, 0)
+    exchange(lambda p: s2.at[p], lambda p: recv_z.at[p], z_send, z_recv, z_peers, z,
+             lambda p: device(x, p // 2, c, y, lax.rem(p, 2)))
+    total = s2[z]
+    for p in z_peers:
+        total = total + recv_z[p]
+    s3[...] = total
+
+    def cols(p):
+        return pl.ds(pl.multiple_of(p * width, 128), width)
+
+    exchange(lambda p: s3.at[:, cols(p)], lambda p: recv_y.at[p], y_send, y_recv, y_peers, y,
+             lambda p: device(x, zh, c, p, zl))
+    total = s3[:, cols(y)]
+    for p in y_peers:
+        total = total + recv_y[p]
+    g16[:, cols(y)] = total * scale
+    exchange(lambda p: g16.at[:, cols(y)], lambda p: g16.at[:, cols(p)], g_send, g_recv, y_peers, y,
+             lambda p: device(x, zh, c, p, zl))
+    out_ref[zl] = g16[...]
+    pair_copy = pltpu.make_async_remote_copy(
+        src_ref=g16, dst_ref=out_ref.at[zl], send_sem=pair_sems.at[0], recv_sem=pair_sems.at[1],
+        device_id=device(x, zh, c, y, 1 - zl), device_id_type=MESH)
+    pair_copy.start()
+    pltpu.make_async_remote_copy(
+        src_ref=g16, dst_ref=out_ref.at[1 - zl], send_sem=pair_sems.at[0], recv_sem=pair_sems.at[1],
+        device_id=device(x, zh, c, y, 1 - zl), device_id_type=MESH).wait_recv()
+    pair_copy.wait_send()
+
+
+def grad_reduce(partial_rows, z_hi, scale):
+    n_x = partial_rows.shape[1]
+    n_y = lax.axis_size("dp") // 2
+    cols = partial_rows.shape[3]
+    shard = partial_rows.shape[2] // z_hi
+    half = shard // 2
+    band = partial_rows.shape[2]
+    f32 = jnp.float32
+    return pl.pallas_call(
+        functools.partial(grad_reduce_kernel, z_hi, scale),
+        out_shape=jax.ShapeDtypeStruct((2, half, cols), f32),
+        in_specs=[pl.BlockSpec(memory_space=pltpu.VMEM)],
+        out_specs=pl.BlockSpec(memory_space=pltpu.VMEM),
+        scratch_shapes=[
+            pltpu.VMEM((n_x, band, cols), partial_rows.dtype),
+            pltpu.VMEM((n_x, band, cols), partial_rows.dtype),
+            pltpu.VMEM((n_x, band, cols), partial_rows.dtype),
+            pltpu.VMEM((2 * z_hi, half, cols), f32),
+            pltpu.VMEM((2 * z_hi, half, cols), f32),
+            pltpu.VMEM((half, cols), f32),
+            pltpu.VMEM((n_y, half, cols // n_y), f32),
+            pltpu.VMEM((half, cols), f32),
+            pltpu.SemaphoreType.DMA((2,)),
+            pltpu.SemaphoreType.DMA((n_x,)),
+            pltpu.SemaphoreType.DMA((n_x,)),
+            pltpu.SemaphoreType.DMA((2 * z_hi,)),
+            pltpu.SemaphoreType.DMA((2 * z_hi,)),
+            pltpu.SemaphoreType.DMA((n_y,)),
+            pltpu.SemaphoreType.DMA((n_y,)),
+            pltpu.SemaphoreType.DMA((n_y,)),
+            pltpu.SemaphoreType.DMA((n_y,)),
+            pltpu.SemaphoreType.DMA((2,)),
+        ],
+        compiler_params=pltpu.CompilerParams(
+            collective_id=1, has_side_effects=True, vmem_limit_bytes=48 * 1024 * 1024),
+    )(partial_rows)
 
 
 def tap_starts(context_row_block):
@@ -156,10 +301,18 @@
         ],
         axis=1,
     ).astype(jnp.bfloat16)
+    z_hi = Z_HI
+    n_x = peer_count // (2 * z_hi)
+    shard = conv_weight.shape[0]
+    routed = (
+        grad_pre.reshape(row_count, n_x, z_hi, 2, shard)
+        .transpose(0, 3, 1, 2, 4)
+        .reshape(row_count, 2 * H)
+    )
     partial_value = jnp.concatenate(
         [
             lax.dot_general(
-                grad_pre,
+                routed,
                 windows[selected_index],
                 contract_first,
                 preferred_element_type=jnp.float32,
@@ -168,11 +321,11 @@
         ],
         axis=1,
     )
-    arrived = lax.all_to_all(partial_value, "fsdp", split_axis=0, concat_axis=0, tiled=True)
-    shard_sum = jnp.sum(arrived.reshape(peer_count, -1, 3 * C), axis=0, dtype=jnp.float32)
-    group_total = all_reduce(shard_sum, "dp")
     total_token_count = row_count * peer_count * lax.axis_size("dp")
-    grad_weight = group_total * (1.0 / math.sqrt(total_token_count))
+    reduced = grad_reduce(
+        partial_value.reshape(2, n_x, z_hi * shard, 3 * C), z_hi, 1.0 / math.sqrt(total_token_count)
+    )
+    grad_weight = reduced.reshape(shard, 3 * C)
     back_proj = jnp.dot(grad_pre, full_weight, preferred_element_type=jnp.float32)
     back_proj = back_proj.reshape(seg_count, seg_rows, 3 * C)
     grad_ext = jnp.zeros((seg_count, context_row_block + seg_rows, C), jnp.float32)

time: 341 us -> 270 us (0.79)
  waiting for transfers between devices: 195 us -> 58.1 us
  Pallas kernels: 28.6 us -> 108 us
  starting transfers between devices: 21.3 us -> 12.7 us
  other arithmetic: 21.2 us -> 17.1 us
    all_to_all x1 -> x0, waiting for transfers between devices: 137 us -> none  [per_device(): lax.all_to_all(partial_value, 'fsdp', split_axis=0, concat_axis=0, tiled=...]
    pallas_call x1, Pallas kernels: 28.6 us -> 108 us  [grad_reduce(): pl.pallas_call(functools.partial(grad_reduce_kernel, z_hi, scale), out_sh...]
    all_to_all x1 -> x0, starting transfers between devices: 8.66 us -> none  [per_device(): lax.all_to_all(partial_value, 'fsdp', split_axis=0, concat_axis=0, tiled=...]
    reduce_sum x1 -> x0, other arithmetic: 4.03 us -> none  [per_device(): jnp.sum(arrived.reshape(peer_count, -1, 3 * C), axis=0, dtype=jnp.float32)]
  transfers between devices with their start and end apart: 4 -> 3, of which waited for: 4 -> 2; matrix products, arithmetic and copies ran while one was open for 11% -> 13% of each run, Pallas kernels for 0% -> 40%
where the time goes in v2:
time: 270 us; the launch traced here: 267 us
  Pallas kernels  108 us (40%)
  waiting for transfers between devices  58.1 us (22%)
  blocking collectives  21.1 us (8%)
  local copies, waits for them, and re-layouts  18.6 us (7%)
  matrix products  17.3 us (6%)
  other arithmetic  17.1 us (6%)
  between operations  14.3 us (5%)
  starting transfers between devices  12.7 us (5%)
    pallas_call x1, Pallas kernels, grad_reduce(): pl.pallas_call(functools.partial(grad_reduce_kernel, z_hi, scale), out_sh...  108 us
    all_gather x1, waiting for transfers between devices, per_device(): full_weight = lax.all_gather(conv_weight, 'fsdp', axis=0, tiled=True)  39.5 us
    all_to_all x1, blocking collectives, per_device(): lax.all_to_all(request_mask, 'fsdp', split_axis=0, concat_axis=0, tiled=T...  21.1 us
    all_to_all x1, waiting for transfers between devices, per_device(): lax.all_to_all(outgoing, 'fsdp', split_axis=0, concat_axis=0, tiled=True)  17.9 us
    concatenate x1, other arithmetic, per_device(): jnp.concatenate([lax.dot_general(routed, windows[selected_index], contrac...  13.4 us
    concatenate x1, local copies, waits for them, and re-layouts, per_device(): jnp.concatenate([lax.dot_general(routed, windows[selected_index], contrac...  8.62 us
    all_to_all x1, starting transfers between devices, per_device(): lax.all_to_all(outgoing_grad, 'fsdp', split_axis=0, concat_axis=0, tiled=...  6.86 us
    dot_general x3, matrix products, per_device(): lax.dot_general(windows[selected_index], full_weight[:, selected_index *...  5.83 us
  transfers between devices with their start and end apart: 3, of which 2 were waited for; matrix products, arithmetic and copies ran while one was open for 13% of the time, Pallas kernels for 40%

profile of v2, /device:TPU:6, one launch (start us, length us, event | category | flops | bytes accessed | tf_op | source)
XLA Modules:
  0.0 266.9 jit_solution(4094425554194627193)
XLA Ops:
  8.6 21.1 %all_to_all.16 = s32[32,1,32]{2,1,0:T(1,128)S(1)} all-to-all(s32[32,1,32]{2,1,0:T(1,128)S(1)} %compare_convert_fusion), channel_id=1, replica_groups=mesh['dp'=16,'fsdp'=32] {'fsdp'}, dimensions={0} | all-to-all | bytes 8192 | tf_op jit(solution)/shard_map/all_to_all | solution.py:267
  29.7 1.8 convolution_convert_fusion.4
  31.6 1.1 copy.24
  32.7 5.8 %all-to-all-start.1 = ((bf16[32,8,1024]{2,1,0:T(8,128)(2,1)}), bf16[32,8,1024]{2,1,0:T(8,128)(2,1)S(1)}, u32[]{:S(2)}, u32[]{:S(2)}) async-start(bf16[32,8,1024]{2,1,0:T(8,128)(2,1)} %copy.24), calls=%async_computation.1 | async-start | bytes 1048576 | tf_op jit(solution)/shard_map/all_to_all | solution.py:273
  38.8 17.9 %all-to-all-done.1 = bf16[32,8,1024]{2,1,0:T(8,128)(2,1)S(1)} async-done(((bf16[32,8,1024]{2,1,0:T(8,128)(2,1)}), bf16[32,8,1024]{2,1,0:T(8,128)(2,1)S(1)}, u32[]{:S(2)}, u32[]{:S(2)}) %all-to-all-start.1) | async-done | bytes 524320 | tf_op jit(solution)/shard_map/all_to_all | solution.py:273
  57.5 39.5 %all-gather.2.cloned.1.call-done = bf16[1024,3072]{1,0:T(8,128)(2,1)} async-done(((bf16[32,3072]{1,0:T(8,128)(2,1)}), bf16[1024,3072]{1,0:T(8,128)(2,1)}) %all-gather.2.cloned.1.call-update) | async-done | bytes 6291472 | tf_op jit(solution)/shard_map/all_gather | solution.py:278
  97.0 2.5 fusion
  99.5 2.4 fusion.2
  102.0 0.9 fusion.9
  102.9 1.0 fusion.18
  104.0 1.8 convolution_bitcast_fusion
  105.8 1.4 fusion.49
  108.0 1.0 fusion.15
  109.6 1.6 copy.33
  111.2 6.9 %all-to-all-start.2 = ((f32[32,8,1024]{2,1,0:T(8,128)}), f32[32,8,1024]{2,1,0:T(8,128)}, u32[]{:S(2)}, u32[]{:S(2)}) async-start(f32[32,8,1024]{2,1,0:T(8,128)} %copy.33), calls=%async_computation.2 | async-start | bytes 2097152 | tf_op jit(solution)/shard_map/all_to_all | solution.py:342
  118.1 1.1 copy.37
  119.2 1.8 copy.38
  121.0 1.0 maximum_bitcast_fusion
  122.0 1.9 convolution_convert_fusion.1
  125.5 13.4 %pad_maximum_fusion = bf16[1024,3072]{0,1:T(8,128)(2,1)} fusion(bf16[1024,1024]{0,1:T(8,128)(2,1)S(1)} %convolution_convert_fusion, bf16[1024,1024]{0,1:T(8,128)(2,1)S(1)} %convolution_convert_fusion.1, bf16[1024,1024]{0,1:T(8,128)(2,1)S(1)} %convolution_convert_fusion.2), kind=kLoop, calls=%fused_computation | loop fusion | flops 18874368 | bytes 12582912 | tf_op jit(solution)/shard_map/concatenate | solution.py:312
  138.9 8.6 %copy.40 = bf16[1024,3072]{1,0:T(8,128)(2,1)} copy(bf16[1024,3072]{0,1:T(8,128)(2,1)} %pad_maximum_fusion) | data formatting | bytes 12582912 | tf_op jit(solution)/shard_map/concatenate | solution.py:312
  147.6 107.7 %shard_map.72 = f32[2,16,3072]{2,1,0:T(8,128)S(1)} custom-call(bf16[2,4,128,3072]{3,2,1,0:T(8,128)(2,1)} %bitcast.54), custom_call_target="tpu_custom_call" | custom-call | tf_op jit(solution)/shard_map/pallas_call | solution.py:221
  255.3 3.0 %fusion.12 = bf16[32,8,1024]{2,0,1:T(8,128)(2,1)S(1)} fusion(f32[32,16,1024]{2,0,1:T(8,128)S(1)} %fusion.15, f32[32,8,1024]{2,1,0:T(8,128)S(1)} %copy-done.1, f32[32,8,1024]{2,1,0:T(8,128)} %all-to-all-done.2, s32[32,1,32]{2,0,1:T(8,128)S(1)} %bitcast.64), kind=kOutput, calls=%fused_computation.16 | convolution fusion | flops 101450752 | bytes 3674112 | tf_op jit(solution)/shard_map/ns,nlc->slc/dot_general | solution.py:343
  258.3 1.1 copy.75
  (36 shorter events, 6.4 us)
Async XLA Ops:
  7.2 31.6 %copy-start.9 = (s32[1,32]{1,0:T(1,128)S(1)}, s32[1,32]{1,0:T(1,128)}, u32[]{:S(2)}) copy-start(s32[1,32]{1,0:T(1,128)} %param.17) | copy-start | bytes 388
  7.2 31.3 %copy-start = (bf16[256,1024]{1,0:T(8,128)(2,1)S(1)}, bf16[256,1024]{1,0:T(8,128)(2,1)}, u32[]{:S(2)}) copy-start(bf16[256,1024]{1,0:T(8,128)(2,1)} %param.14) | copy-start | bytes 1572868
  7.2 89.8 %all-gather.2.cloned.1.call-start = ((), (), s32[]{:S(2)}) async-start(), calls=%async_computation.3 | async-start | bytes 6488064 | tf_op jit(solution)/shard_map/all_gather | solution.py:278
  32.7 24.0 %all-to-all-start.1 = ((bf16[32,8,1024]{2,1,0:T(8,128)(2,1)}), bf16[32,8,1024]{2,1,0:T(8,128)(2,1)S(1)}, u32[]{:S(2)}, u32[]{:S(2)}) async-start(bf16[32,8,1024]{2,1,0:T(8,128)(2,1)} %copy.24), calls=%async_computation.1 | async-start | bytes 1048576 | tf_op jit(solution)/shard_map/all_to_all | solution.py:273
  38.8 18.7 %copy-start.7 = (s32[32]{0:T(128)}, s32[32]{0:T(128)S(1)}, u32[]{:S(2)}) copy-start(s32[32]{0:T(128)S(1)} %compare_select_fusion.1) | copy-start | bytes 388
  57.5 48.3 %copy-start.2 = (bf16[32,8,1024]{2,0,1:T(8,128)(2,1)}, bf16[32,8,1024]{2,0,1:T(8,128)(2,1)S(1)}, u32[]{:S(2)}) copy-start(bf16[32,8,1024]{2,0,1:T(8,128)(2,1)S(1)} %pad_maximum_fusion.1) | copy-start | bytes 1572868
  97.0 4.9 %copy-start.5 = (bf16[1024,3072]{1,0:T(8,128)(2,1)S(1)}, bf16[1024,3072]{1,0:T(8,128)(2,1)}, u32[]{:S(2)}) copy-start(bf16[1024,3072]{1,0:T(8,128)(2,1)} %all-gather.2.cloned.1.call-done) | copy-start | bytes 18874372
  102.0 1.0 copy-start.6
  104.0 1.8 copy-start.3
  104.0 1.8 copy-start.4
  107.8 1.2 copy-start.8
  111.2 144.0 %all-to-all-start.2 = ((f32[32,8,1024]{2,1,0:T(8,128)}), f32[32,8,1024]{2,1,0:T(8,128)}, u32[]{:S(2)}, u32[]{:S(2)}) async-start(f32[32,8,1024]{2,1,0:T(8,128)} %copy.33), calls=%async_computation.2 | async-start | bytes 2097152 | tf_op jit(solution)/shard_map/all_to_all | solution.py:342
  147.6 107.7 %copy-start.1 = (f32[32,8,1024]{2,1,0:T(8,128)S(1)}, f32[32,8,1024]{2,1,0:T(8,128)}, u32[]{:S(2)}) copy-start(f32[32,8,1024]{2,1,0:T(8,128)} %get-tuple-element.59) | copy-start | bytes 3145732
Sparse Core Ops, SparseCore 0:
  11.1 85.8 all-gather.1

commit v3 on v2

--- a/solution.py
+++ b/solution.py
@@ -104,7 +104,7 @@
     return out.reshape(shape)
 
 
-def grad_reduce_kernel(z_hi, scale, p_ref, out_ref, recv_c, s1b, recv_x, s2, recv_z, s3, recv_y, g16,
+def grad_reduce_kernel(z_hi, scale, p_ref, out_ref, recv_c, s1b, recv_x, s2, own, recv_z, s3, recv_y, g16,
                        core_sems, x_send, x_recv, z_send, z_recv, y_send, y_recv, g_send, g_recv, pair_sems):
     n_x = recv_x.shape[0]
     n_z = 2 * z_hi
@@ -177,15 +177,16 @@
         total = p_ref[c, x, at, :].astype(jnp.float32) + recv_c[x, at, :].astype(jnp.float32)
         for p in x_peers:
             total = total + recv_x[p, at, :].astype(jnp.float32)
-        s2[j] = total
+        s2[j] = total.astype(s2.dtype)
+        own[j] = total
         return carry
 
     lax.fori_loop(0, n_z, sum_x, 0)
     exchange(lambda p: s2.at[p], lambda p: recv_z.at[p], z_send, z_recv, z_peers, z,
              lambda p: device(x, p // 2, c, y, lax.rem(p, 2)))
-    total = s2[z]
+    total = own[z]
     for p in z_peers:
-        total = total + recv_z[p]
+        total = total + recv_z[p].astype(jnp.float32)
     s3[...] = total
 
     def cols(p):
@@ -227,8 +228,9 @@
             pltpu.VMEM((n_x, band, cols), partial_rows.dtype),
             pltpu.VMEM((n_x, band, cols), partial_rows.dtype),
             pltpu.VMEM((n_x, band, cols), partial_rows.dtype),
+            pltpu.VMEM((2 * z_hi, half, cols), partial_rows.dtype),
             pltpu.VMEM((2 * z_hi, half, cols), f32),
-            pltpu.VMEM((2 * z_hi, half, cols), f32),
+            pltpu.VMEM((2 * z_hi, half, cols), partial_rows.dtype),
             pltpu.VMEM((half, cols), f32),
             pltpu.VMEM((n_y, half, cols // n_y), f32),
             pltpu.VMEM((half, cols), f32),
@@ -309,18 +311,10 @@
         .transpose(0, 3, 1, 2, 4)
         .reshape(row_count, 2 * H)
     )
-    partial_value = jnp.concatenate(
-        [
-            lax.dot_general(
-                routed,
-                windows[selected_index],
-                contract_first,
-                preferred_element_type=jnp.float32,
-            ).astype(jnp.bfloat16)
-            for selected_index in range(3)
-        ],
-        axis=1,
-    )
+    stacked = jnp.concatenate(windows, axis=1)
+    partial_value = lax.dot_general(
+        routed, stacked, contract_first, preferred_element_type=jnp.float32
+    ).astype(jnp.bfloat16)
     total_token_count = row_count * peer_count * lax.axis_size("dp")
     reduced = grad_reduce(
         partial_value.reshape(2, n_x, z_hi * shard, 3 * C), z_hi, 1.0 / math.sqrt(total_token_count)

time: 270 us -> 235 us (0.87)
  Pallas kernels: 108 us -> 90.7 us
  other arithmetic: 17.1 us -> 2.78 us
  local copies, waits for them, and re-layouts: 18.6 us -> 11.3 us
    pallas_call x1, Pallas kernels: 108 us -> 90.7 us  [grad_reduce(): pl.pallas_call(functools.partial(grad_reduce_kernel, z_hi, scale), out_sh...]
    concatenate x1 -> x0, other arithmetic: 13.4 us -> none  [per_device(): jnp.concatenate([lax.dot_general(routed, windows[selected_index], contrac...]
    concatenate x1 -> x0, local copies, waits for them, and re-layouts: 8.62 us -> none  [per_device(): jnp.concatenate([lax.dot_general(routed, windows[selected_index], contrac...]
    dot_general x3 -> x1, matrix products: 3.49 us -> 5.66 us  [per_device(): lax.dot_general(routed, stacked, contract_first, preferred_element_type=j...]
  transfers between devices with their start and end apart: 3 -> 3, of which waited for: 2 -> 2; matrix products, arithmetic and copies ran while one was open for 13% -> 6% of each run, Pallas kernels for 40% -> 39%
where the time goes in v3:
time: 235 us; the launch traced here: 230 us
  Pallas kernels  90.7 us (39%)
  waiting for transfers between devices  58.1 us (25%)
  blocking collectives  21.1 us (9%)
  matrix products  19.4 us (8%)
  between operations  14.3 us (6%)
  starting transfers between devices  12.7 us (5%)
  local copies, waits for them, and re-layouts  11.3 us (5%)
  other arithmetic  2.78 us (1%)
    pallas_call x1, Pallas kernels, grad_reduce(): pl.pallas_call(functools.partial(grad_reduce_kernel, z_hi, scale), out_sh...  90.7 us
    all_gather x1, waiting for transfers between devices, per_device(): full_weight = lax.all_gather(conv_weight, 'fsdp', axis=0, tiled=True)  39.5 us
    all_to_all x1, blocking collectives, per_device(): lax.all_to_all(request_mask, 'fsdp', split_axis=0, concat_axis=0, tiled=T...  21.1 us
    all_to_all x1, waiting for transfers between devices, per_device(): lax.all_to_all(outgoing, 'fsdp', split_axis=0, concat_axis=0, tiled=True)  17.9 us
    all_to_all x1, starting transfers between devices, per_device(): lax.all_to_all(outgoing_grad, 'fsdp', split_axis=0, concat_axis=0, tiled=...  6.86 us
    dot_general x3, matrix products, per_device(): lax.dot_general(windows[selected_index], full_weight[:, selected_index *...  5.83 us
    all_to_all x1, starting transfers between devices, per_device(): lax.all_to_all(outgoing, 'fsdp', split_axis=0, concat_axis=0, tiled=True)  5.78 us
    dot_general x1, matrix products, per_device(): lax.dot_general(routed, stacked, contract_first, preferred_element_type=j...  5.66 us
  transfers between devices with their start and end apart: 3, of which 2 were waited for; matrix products, arithmetic and copies ran while one was open for 6% of the time, Pallas kernels for 39%

profile of v3, /device:TPU:6, one launch (start us, length us, event | category | flops | bytes accessed | tf_op | source)
XLA Modules:
  0.0 230.3 jit_solution(16008189906208734412)
XLA Ops:
  8.6 21.1 %all_to_all.16 = s32[32,1,32]{2,1,0:T(1,128)S(1)} all-to-all(s32[32,1,32]{2,1,0:T(1,128)S(1)} %compare_convert_fusion), channel_id=1, replica_groups=mesh['dp'=16,'fsdp'=32] {'fsdp'}, dimensions={0} | all-to-all | bytes 8192 | tf_op jit(solution)/shard_map/all_to_all | solution.py:269
  29.7 1.8 convolution_convert_fusion.2
  31.6 1.1 copy.22
  32.7 5.8 %all-to-all-start.1 = ((bf16[32,8,1024]{2,1,0:T(8,128)(2,1)}), bf16[32,8,1024]{2,1,0:T(8,128)(2,1)S(1)}, u32[]{:S(2)}, u32[]{:S(2)}) async-start(bf16[32,8,1024]{2,1,0:T(8,128)(2,1)} %copy.22), calls=%async_computation.1 | async-start | bytes 1048576 | tf_op jit(solution)/shard_map/all_to_all | solution.py:275
  38.8 17.9 %all-to-all-done.1 = bf16[32,8,1024]{2,1,0:T(8,128)(2,1)S(1)} async-done(((bf16[32,8,1024]{2,1,0:T(8,128)(2,1)}), bf16[32,8,1024]{2,1,0:T(8,128)(2,1)S(1)}, u32[]{:S(2)}, u32[]{:S(2)}) %all-to-all-start.1) | async-done | bytes 524320 | tf_op jit(solution)/shard_map/all_to_all | solution.py:275
  56.7 0.8 convolution_convert_fusion.1
  57.5 39.5 %all-gather.2.cloned.1.call-done = bf16[1024,3072]{1,0:T(8,128)(2,1)} async-done(((bf16[32,3072]{1,0:T(8,128)(2,1)}), bf16[1024,3072]{1,0:T(8,128)(2,1)}) %all-gather.2.cloned.1.call-update) | async-done | bytes 6291472 | tf_op jit(solution)/shard_map/all_gather | solution.py:280
  97.0 2.5 %fusion = f32[256,1024]{1,0:T(8,128)S(1)} fusion(bf16[256,1024]{1,0:T(8,128)(2,1)S(1)} %copy-done.1, bf16[1024,3072]{1,0:T(8,128)(2,1)} %all-gather.2.cloned.1.call-done), kind=kOutput, calls=%fused_computation.2 | convolution fusion | flops 536870912 | bytes 3670016 | tf_op jit(solution)/shard_map/dot_general | solution.py:286
  99.5 2.4 %fusion.2 = f32[256,1024]{1,0:T(8,128)S(1)} fusion(bf16[1024,3072]{1,0:T(8,128)(2,1)} %all-gather.2.cloned.1.call-done, bf16[32,8,1024]{2,0,1:T(8,128)(2,1)S(1)} %pad_maximum_fusion), kind=kOutput, calls=%fused_computation.4 | convolution fusion | flops 536870912 | bytes 3670016 | tf_op jit(solution)/shard_map/dot_general | solution.py:286
  102.0 0.9 fusion.14
  102.9 1.0 fusion.23
  104.7 1.8 convolution_bitcast_fusion
  106.5 1.3 fusion.47
  108.7 1.0 fusion.20
  110.2 1.7 copy.31
  111.9 6.9 %all-to-all-start.2 = ((f32[32,8,1024]{2,1,0:T(8,128)}), f32[32,8,1024]{2,1,0:T(8,128)}, u32[]{:S(2)}, u32[]{:S(2)}) async-start(f32[32,8,1024]{2,1,0:T(8,128)} %copy.31), calls=%async_computation.2 | async-start | bytes 2097152 | tf_op jit(solution)/shard_map/all_to_all | solution.py:336
  118.8 1.1 copy.61
  119.9 1.1 copy.62
  121.0 1.1 copy.36
  122.3 5.7 %convolution_convert_fusion = bf16[1024,3072]{1,0:T(8,128)(2,1)} fusion(bf16[256,1024]{0,1:T(8,128)(2,1)S(1)} %bitcast.57, bf16[256,1024]{1,0:T(8,128)(2,1)S(1)} %copy-done.2, bf16[256,1024]{1,0:T(8,128)(2,1)} %bitcast.54, bf16[256,1024]{1,0:T(8,128)(2,1)} %bitcast.55), kind=kOutput, calls=%fused_computation | convolution fusion | flops 1618477056 | bytes 8388608 | tf_op jit(solution)/shard_map/dot_general | solution.py:315
  128.0 90.7 %shard_map.72 = f32[2,16,3072]{2,1,0:T(8,128)S(1)} custom-call(bf16[2,4,128,3072]{3,2,1,0:T(8,128)(2,1)} %bitcast.49), custom_call_target="tpu_custom_call" | custom-call | tf_op jit(solution)/shard_map/pallas_call | solution.py:222
  218.7 3.0 %fusion.17 = bf16[32,8,1024]{2,0,1:T(8,128)(2,1)S(1)} fusion(f32[32,16,1024]{2,0,1:T(8,128)S(1)} %fusion.20, f32[32,8,1024]{2,1,0:T(8,128)S(1)} %copy-done, f32[32,8,1024]{2,1,0:T(8,128)} %all-to-all-done.2, s32[32,1,32]{2,0,1:T(8,128)S(1)} %bitcast.59), kind=kOutput, calls=%fused_computation.18 | convolution fusion | flops 101450752 | bytes 3674112 | tf_op jit(solution)/shard_map/ns,nlc->slc/dot_general | solution.py:337
  221.7 1.1 copy.60
  222.7 0.7 copy.65
  (28 shorter events, 4.2 us)
Async XLA Ops:
  7.2 31.6 %copy-start.6 = (s32[1,32]{1,0:T(1,128)S(1)}, s32[1,32]{1,0:T(1,128)}, u32[]{:S(2)}) copy-start(s32[1,32]{1,0:T(1,128)} %param.17) | copy-start | bytes 388
  7.2 31.3 %copy-start.1 = (bf16[256,1024]{1,0:T(8,128)(2,1)S(1)}, bf16[256,1024]{1,0:T(8,128)(2,1)}, u32[]{:S(2)}) copy-start(bf16[256,1024]{1,0:T(8,128)(2,1)} %param.14) | copy-start | bytes 1572868
  7.2 89.8 %all-gather.2.cloned.1.call-start = ((), (), s32[]{:S(2)}) async-start(), calls=%async_computation.3 | async-start | bytes 6488064 | tf_op jit(solution)/shard_map/all_gather | solution.py:280
  32.7 24.0 %all-to-all-start.1 = ((bf16[32,8,1024]{2,1,0:T(8,128)(2,1)}), bf16[32,8,1024]{2,1,0:T(8,128)(2,1)S(1)}, u32[]{:S(2)}, u32[]{:S(2)}) async-start(bf16[32,8,1024]{2,1,0:T(8,128)(2,1)} %copy.22), calls=%async_computation.1 | async-start | bytes 1048576 | tf_op jit(solution)/shard_map/all_to_all | solution.py:275
  97.0 4.9 %copy-start.4 = (bf16[1024,3072]{1,0:T(8,128)(2,1)S(1)}, bf16[1024,3072]{1,0:T(8,128)(2,1)}, u32[]{:S(2)}) copy-start(bf16[1024,3072]{1,0:T(8,128)(2,1)} %all-gather.2.cloned.1.call-done) | copy-start | bytes 18874372
  102.0 1.0 copy-start.5
  104.0 0.7 copy-start.3
  111.9 106.7 %all-to-all-start.2 = ((f32[32,8,1024]{2,1,0:T(8,128)}), f32[32,8,1024]{2,1,0:T(8,128)}, u32[]{:S(2)}, u32[]{:S(2)}) async-start(f32[32,8,1024]{2,1,0:T(8,128)} %copy.31), calls=%async_computation.2 | async-start | bytes 2097152 | tf_op jit(solution)/shard_map/all_to_all | solution.py:336
  119.9 2.4 %copy-start.2 = (bf16[256,1024]{1,0:T(8,128)(2,1)S(1)}, bf16[256,1024]{1,0:T(8,128)(2,1)}, u32[]{:S(2)}) copy-start(bf16[256,1024]{1,0:T(8,128)(2,1)} %param.14) | copy-start | bytes 1572868
  128.0 90.7 %copy-start = (f32[32,8,1024]{2,1,0:T(8,128)S(1)}, f32[32,8,1024]{2,1,0:T(8,128)}, u32[]{:S(2)}) copy-start(f32[32,8,1024]{2,1,0:T(8,128)} %get-tuple-element.59) | copy-start | bytes 3145732
Sparse Core Ops, SparseCore 0:
  11.1 85.8 all-gather.1

commit v4 on v3

--- a/solution.py
+++ b/solution.py
@@ -105,7 +105,8 @@
 
 
 def grad_reduce_kernel(z_hi, scale, p_ref, out_ref, recv_c, s1b, recv_x, s2, own, recv_z, s3, recv_y, g16,
-                       core_sems, x_send, x_recv, z_send, z_recv, y_send, y_recv, g_send, g_recv, pair_sems):
+                       core_sems, x_send, x_recv, z_send, z_recv, y_send, y_recv, g_send, g_recv, pair_sems,
+                       relay, relay_sems):
     n_x = recv_x.shape[0]
     n_z = 2 * z_hi
     n_y = recv_y.shape[0]
@@ -169,8 +170,47 @@
         return carry
 
     lax.fori_loop(0, n_x * chunks, round_two_sums, 0)
-    exchange(lambda p: s1b.at[p], lambda p: recv_x.at[p], x_send, x_recv, x_peers, x,
-             lambda p: device(p, zh, c, y, zl))
+    if n_x == 4:
+        right, across, left = x_peers
+        split = band // 2
+        head, tail = pl.ds(0, split), pl.ds(split, split)
+        sends = []
+        for p in (right, left):
+            copy = pltpu.make_async_remote_copy(
+                src_ref=s1b.at[p], dst_ref=recv_x.at[x], send_sem=x_send.at[p],
+                recv_sem=x_recv.at[x], device_id=device(p, zh, c, y, zl), device_id_type=MESH)
+            copy.start()
+            sends.append(copy)
+        for slot, (p, rows_) in enumerate(((right, head), (left, tail))):
+            copy = pltpu.make_async_remote_copy(
+                src_ref=s1b.at[across, rows_], dst_ref=relay.at[slot], send_sem=relay_sems.at[0, slot],
+                recv_sem=relay_sems.at[1, slot], device_id=device(p, zh, c, y, zl), device_id_type=MESH)
+            copy.start()
+            sends.append(copy)
+        for slot, (p, q, rows_) in enumerate(((right, left, head), (left, right, tail))):
+            pltpu.make_async_remote_copy(
+                src_ref=s1b.at[across, rows_], dst_ref=relay.at[slot], send_sem=relay_sems.at[0, slot],
+                recv_sem=relay_sems.at[1, slot], device_id=device(p, zh, c, y, zl),
+                device_id_type=MESH).wait_recv()
+            copy = pltpu.make_async_remote_copy(
+                src_ref=relay.at[slot], dst_ref=recv_x.at[q, rows_], send_sem=relay_sems.at[2, slot],
+                recv_sem=relay_sems.at[3, slot], device_id=device(p, zh, c, y, zl), device_id_type=MESH)
+            copy.start()
+            sends.append(copy)
+        for p in (right, left):
+            pltpu.make_async_remote_copy(
+                src_ref=s1b.at[p], dst_ref=recv_x.at[p], send_sem=x_send.at[p],
+                recv_sem=x_recv.at[p], device_id=device(p, zh, c, y, zl), device_id_type=MESH).wait_recv()
+        for slot, rows_ in enumerate((head, tail)):
+            pltpu.make_async_remote_copy(
+                src_ref=relay.at[slot], dst_ref=recv_x.at[across, rows_], send_sem=relay_sems.at[2, slot],
+                recv_sem=relay_sems.at[3, slot], device_id=device(across, zh, c, y, zl),
+                device_id_type=MESH).wait_recv()
+        for copy in sends:
+            copy.wait_send()
+    else:
+        exchange(lambda p: s1b.at[p], lambda p: recv_x.at[p], x_send, x_recv, x_peers, x,
+                 lambda p: device(p, zh, c, y, zl))
 
     def sum_x(j, carry):
         at = pl.ds(pl.multiple_of(j * half, half), half)
@@ -244,6 +284,8 @@
             pltpu.SemaphoreType.DMA((n_y,)),
             pltpu.SemaphoreType.DMA((n_y,)),
             pltpu.SemaphoreType.DMA((2,)),
+            pltpu.VMEM((2, band // 2, cols), partial_rows.dtype),
+            pltpu.SemaphoreType.DMA((4, 2)),
         ],
         compiler_params=pltpu.CompilerParams(
             collective_id=1, has_side_effects=True, vmem_limit_bytes=48 * 1024 * 1024),

time: 235 us -> 235 us (level); the launches traced: 230 us -> 234 us
  Pallas kernels: 90.7 us -> 94.4 us
    pallas_call x1, Pallas kernels: 90.7 us -> 94.4 us  [grad_reduce(): pl.pallas_call(functools.partial(grad_reduce_kernel, z_hi, scale), out_sh...]
  transfers between devices with their start and end apart: 3 -> 3, of which waited for: 2 -> 2; matrix products, arithmetic and copies ran while one was open for 6% -> 6% of each run, Pallas kernels for 39% -> 40%
where the time goes in v4:
time: 235 us; the launch traced here: 234 us
  Pallas kernels  94.4 us (40%)
  waiting for transfers between devices  58.1 us (25%)
  blocking collectives  21.1 us (9%)
  matrix products  19.4 us (8%)
  between operations  14.3 us (6%)
  starting transfers between devices  12.7 us (5%)
  local copies, waits for them, and re-layouts  11.3 us (5%)
  other arithmetic  2.78 us (1%)
    pallas_call x1, Pallas kernels, grad_reduce(): pl.pallas_call(functools.partial(grad_reduce_kernel, z_hi, scale), out_sh...  94.4 us
    all_gather x1, waiting for transfers between devices, per_device(): full_weight = lax.all_gather(conv_weight, 'fsdp', axis=0, tiled=True)  39.5 us
    all_to_all x1, blocking collectives, per_device(): lax.all_to_all(request_mask, 'fsdp', split_axis=0, concat_axis=0, tiled=T...  21.1 us
    all_to_all x1, waiting for transfers between devices, per_device(): lax.all_to_all(outgoing, 'fsdp', split_axis=0, concat_axis=0, tiled=True)  17.9 us
    all_to_all x1, starting transfers between devices, per_device(): lax.all_to_all(outgoing_grad, 'fsdp', split_axis=0, concat_axis=0, tiled=...  6.86 us
    dot_general x3, matrix products, per_device(): lax.dot_general(windows[selected_index], full_weight[:, selected_index *...  5.83 us
    all_to_all x1, starting transfers between devices, per_device(): lax.all_to_all(outgoing, 'fsdp', split_axis=0, concat_axis=0, tiled=True)  5.78 us
    dot_general x1, matrix products, per_device(): lax.dot_general(routed, stacked, contract_first, preferred_element_type=j...  5.66 us
  transfers between devices with their start and end apart: 3, of which 2 were waited for; matrix products, arithmetic and copies ran while one was open for 6% of the time, Pallas kernels for 40%

profile of v4, /device:TPU:6, one launch (start us, length us, event | category | flops | bytes accessed | tf_op | source)
XLA Modules:
  0.0 234.1 jit_solution(14810724903770520101)
XLA Ops:
  8.6 21.1 %all_to_all.16 = s32[32,1,32]{2,1,0:T(1,128)S(1)} all-to-all(s32[32,1,32]{2,1,0:T(1,128)S(1)} %compare_convert_fusion), channel_id=1, replica_groups=mesh['dp'=16,'fsdp'=32] {'fsdp'}, dimensions={0} | all-to-all | bytes 8192 | tf_op jit(solution)/shard_map/all_to_all | solution.py:311
  29.7 1.8 convolution_convert_fusion.2
  31.6 1.1 copy.22
  32.7 5.8 %all-to-all-start.1 = ((bf16[32,8,1024]{2,1,0:T(8,128)(2,1)}), bf16[32,8,1024]{2,1,0:T(8,128)(2,1)S(1)}, u32[]{:S(2)}, u32[]{:S(2)}) async-start(bf16[32,8,1024]{2,1,0:T(8,128)(2,1)} %copy.22), calls=%async_computation.1 | async-start | bytes 1048576 | tf_op jit(solution)/shard_map/all_to_all | solution.py:317
  38.8 17.9 %all-to-all-done.1 = bf16[32,8,1024]{2,1,0:T(8,128)(2,1)S(1)} async-done(((bf16[32,8,1024]{2,1,0:T(8,128)(2,1)}), bf16[32,8,1024]{2,1,0:T(8,128)(2,1)S(1)}, u32[]{:S(2)}, u32[]{:S(2)}) %all-to-all-start.1) | async-done | bytes 524320 | tf_op jit(solution)/shard_map/all_to_all | solution.py:317
  56.7 0.8 convolution_convert_fusion.1
  57.5 39.5 %all-gather.2.cloned.1.call-done = bf16[1024,3072]{1,0:T(8,128)(2,1)} async-done(((bf16[32,3072]{1,0:T(8,128)(2,1)}), bf16[1024,3072]{1,0:T(8,128)(2,1)}) %all-gather.2.cloned.1.call-update) | async-done | bytes 6291472 | tf_op jit(solution)/shard_map/all_gather | solution.py:322
  97.0 2.5 %fusion = f32[256,1024]{1,0:T(8,128)S(1)} fusion(bf16[256,1024]{1,0:T(8,128)(2,1)S(1)} %copy-done.1, bf16[1024,3072]{1,0:T(8,128)(2,1)} %all-gather.2.cloned.1.call-done), kind=kOutput, calls=%fused_computation.2 | convolution fusion | flops 536870912 | bytes 3670016 | tf_op jit(solution)/shard_map/dot_general | solution.py:328
  99.5 2.4 %fusion.2 = f32[256,1024]{1,0:T(8,128)S(1)} fusion(bf16[1024,3072]{1,0:T(8,128)(2,1)} %all-gather.2.cloned.1.call-done, bf16[32,8,1024]{2,0,1:T(8,128)(2,1)S(1)} %pad_maximum_fusion), kind=kOutput, calls=%fused_computation.4 | convolution fusion | flops 536870912 | bytes 3670016 | tf_op jit(solution)/shard_map/dot_general | solution.py:328
  102.0 0.9 fusion.14
  102.9 1.0 fusion.23
  104.7 1.8 convolution_bitcast_fusion
  106.5 1.3 fusion.47
  108.7 1.0 fusion.20
  110.2 1.7 copy.31
  111.9 6.9 %all-to-all-start.2 = ((f32[32,8,1024]{2,1,0:T(8,128)}), f32[32,8,1024]{2,1,0:T(8,128)}, u32[]{:S(2)}, u32[]{:S(2)}) async-start(f32[32,8,1024]{2,1,0:T(8,128)} %copy.31), calls=%async_computation.2 | async-start | bytes 2097152 | tf_op jit(solution)/shard_map/all_to_all | solution.py:378
  118.8 1.1 copy.61
  119.9 1.1 copy.62
  121.0 1.1 copy.36
  122.3 5.7 %convolution_convert_fusion = bf16[1024,3072]{1,0:T(8,128)(2,1)} fusion(bf16[256,1024]{0,1:T(8,128)(2,1)S(1)} %bitcast.57, bf16[256,1024]{1,0:T(8,128)(2,1)S(1)} %copy-done.2, bf16[256,1024]{1,0:T(8,128)(2,1)} %bitcast.54, bf16[256,1024]{1,0:T(8,128)(2,1)} %bitcast.55), kind=kOutput, calls=%fused_computation | convolution fusion | flops 1618477056 | bytes 8388608 | tf_op jit(solution)/shard_map/dot_general | solution.py:357
  128.0 94.4 %shard_map.72 = f32[2,16,3072]{2,1,0:T(8,128)S(1)} custom-call(bf16[2,4,128,3072]{3,2,1,0:T(8,128)(2,1)} %bitcast.49), custom_call_target="tpu_custom_call" | custom-call | tf_op jit(solution)/shard_map/pallas_call | solution.py:262
  222.4 3.0 %fusion.17 = bf16[32,8,1024]{2,0,1:T(8,128)(2,1)S(1)} fusion(f32[32,16,1024]{2,0,1:T(8,128)S(1)} %fusion.20, f32[32,8,1024]{2,1,0:T(8,128)S(1)} %copy-done, f32[32,8,1024]{2,1,0:T(8,128)} %all-to-all-done.2, s32[32,1,32]{2,0,1:T(8,128)S(1)} %bitcast.59), kind=kOutput, calls=%fused_computation.18 | convolution fusion | flops 101450752 | bytes 3674112 | tf_op jit(solution)/shard_map/ns,nlc->slc/dot_general | solution.py:379
  225.4 1.1 copy.60
  226.5 0.7 copy.65
  (28 shorter events, 4.2 us)
Async XLA Ops:
  7.2 31.6 %copy-start.6 = (s32[1,32]{1,0:T(1,128)S(1)}, s32[1,32]{1,0:T(1,128)}, u32[]{:S(2)}) copy-start(s32[1,32]{1,0:T(1,128)} %param.17) | copy-start | bytes 388
  7.2 31.3 %copy-start.1 = (bf16[256,1024]{1,0:T(8,128)(2,1)S(1)}, bf16[256,1024]{1,0:T(8,128)(2,1)}, u32[]{:S(2)}) copy-start(bf16[256,1024]{1,0:T(8,128)(2,1)} %param.14) | copy-start | bytes 1572868
  7.2 89.8 %all-gather.2.cloned.1.call-start = ((), (), s32[]{:S(2)}) async-start(), calls=%async_computation.3 | async-start | bytes 6488064 | tf_op jit(solution)/shard_map/all_gather | solution.py:322
  32.7 24.0 %all-to-all-start.1 = ((bf16[32,8,1024]{2,1,0:T(8,128)(2,1)}), bf16[32,8,1024]{2,1,0:T(8,128)(2,1)S(1)}, u32[]{:S(2)}, u32[]{:S(2)}) async-start(bf16[32,8,1024]{2,1,0:T(8,128)(2,1)} %copy.22), calls=%async_computation.1 | async-start | bytes 1048576 | tf_op jit(solution)/shard_map/all_to_all | solution.py:317
  97.0 4.9 %copy-start.4 = (bf16[1024,3072]{1,0:T(8,128)(2,1)S(1)}, bf16[1024,3072]{1,0:T(8,128)(2,1)}, u32[]{:S(2)}) copy-start(bf16[1024,3072]{1,0:T(8,128)(2,1)} %all-gather.2.cloned.1.call-done) | copy-start | bytes 18874372
  102.0 1.0 copy-start.5
  104.0 0.7 copy-start.3
  111.9 110.5 %all-to-all-start.2 = ((f32[32,8,1024]{2,1,0:T(8,128)}), f32[32,8,1024]{2,1,0:T(8,128)}, u32[]{:S(2)}, u32[]{:S(2)}) async-start(f32[32,8,1024]{2,1,0:T(8,128)} %copy.31), calls=%async_computation.2 | async-start | bytes 2097152 | tf_op jit(solution)/shard_map/all_to_all | solution.py:378
  119.9 2.4 %copy-start.2 = (bf16[256,1024]{1,0:T(8,128)(2,1)S(1)}, bf16[256,1024]{1,0:T(8,128)(2,1)}, u32[]{:S(2)}) copy-start(bf16[256,1024]{1,0:T(8,128)(2,1)} %param.14) | copy-start | bytes 1572868
  128.0 94.5 %copy-start = (f32[32,8,1024]{2,1,0:T(8,128)S(1)}, f32[32,8,1024]{2,1,0:T(8,128)}, u32[]{:S(2)}) copy-start(f32[32,8,1024]{2,1,0:T(8,128)} %get-tuple-element.59) | copy-start | bytes 3145732
Sparse Core Ops, SparseCore 0:
  11.1 85.8 all-gather.1

commit v5 on v3

--- a/solution.py
+++ b/solution.py
@@ -14,6 +14,7 @@
 H = 512
 DILATION_SIZE = 4
 Z_HI = 4
+PIECES = 2
 
 
 def all_reduce_kernel(axis, n, x_ref, out_ref, gathered, summed, send_sems, recv_sems, out_send, out_recv):
@@ -137,20 +138,28 @@
         pl.semaphore_signal(barrier, inc=1, device_id=peer, device_id_type=MESH)
     pl.semaphore_wait(barrier, len(everyone))
 
-    def exchange(src_of, dst_of, send_sems, recv_sems, peers, mine, device_of):
-        sends = []
+    def start_exchange(src_of, dst_of, send_sems, recv_sems, peers, mine, device_of):
+        sends, arrivals = [], []
         for p in peers:
             copy = pltpu.make_async_remote_copy(
                 src_ref=src_of(p), dst_ref=dst_of(mine), send_sem=send_sems.at[p],
                 recv_sem=recv_sems.at[mine], device_id=device_of(p), device_id_type=MESH)
             copy.start()
             sends.append(copy)
-        for p in peers:
-            pltpu.make_async_remote_copy(
+            arrivals.append(pltpu.make_async_remote_copy(
                 src_ref=src_of(p), dst_ref=dst_of(p), send_sem=send_sems.at[p],
-                recv_sem=recv_sems.at[p], device_id=device_of(p), device_id_type=MESH).wait_recv()
+                recv_sem=recv_sems.at[p], device_id=device_of(p), device_id_type=MESH))
+        return sends, arrivals
+
+    def finish_exchange(pending):
+        sends, arrivals = pending
+        for copy in arrivals:
+            copy.wait_recv()
         for copy in sends:
             copy.wait_send()
+
+    def exchange(*args):
+        finish_exchange(start_exchange(*args))
 
     core_copy = pltpu.make_async_remote_copy(
         src_ref=p_ref.at[1 - c], dst_ref=recv_c, send_sem=core_sems.at[0],
@@ -169,21 +178,43 @@
         return carry
 
     lax.fori_loop(0, n_x * chunks, round_two_sums, 0)
-    exchange(lambda p: s1b.at[p], lambda p: recv_x.at[p], x_send, x_recv, x_peers, x,
-             lambda p: device(p, zh, c, y, zl))
-
-    def sum_x(j, carry):
-        at = pl.ds(pl.multiple_of(j * half, half), half)
-        total = p_ref[c, x, at, :].astype(jnp.float32) + recv_c[x, at, :].astype(jnp.float32)
-        for p in x_peers:
-            total = total + recv_x[p, at, :].astype(jnp.float32)
-        s2[j] = total.astype(s2.dtype)
-        own[j] = total
-        return carry
-
-    lax.fori_loop(0, n_z, sum_x, 0)
-    exchange(lambda p: s2.at[p], lambda p: recv_z.at[p], z_send, z_recv, z_peers, z,
-             lambda p: device(x, p // 2, c, y, lax.rem(p, 2)))
+    pieces = x_send.shape[0]
+    span = s1b.shape[2] // pieces
+
+    def piece(k):
+        return pl.ds(k * span, span)
+
+    def x_stage(k):
+        return start_exchange(lambda p: s1b.at[p, :, piece(k)], lambda p: recv_x.at[p, :, piece(k)],
+                              x_send.at[k], x_recv.at[k], x_peers, x, lambda p: device(p, zh, c, y, zl))
+
+    def z_stage(k):
+        return start_exchange(lambda p: s2.at[p, :, piece(k)], lambda p: recv_z.at[p, :, piece(k)],
+                              z_send.at[k], z_recv.at[k], z_peers, z,
+                              lambda p: device(x, p // 2, c, y, lax.rem(p, 2)))
+
+    def sum_x(k):
+        def body(j, carry):
+            at = pl.ds(pl.multiple_of(j * half, half), half)
+            total = (p_ref[c, x, at, piece(k)].astype(jnp.float32)
+                     + recv_c[x, at, piece(k)].astype(jnp.float32))
+            for p in x_peers:
+                total = total + recv_x[p, at, piece(k)].astype(jnp.float32)
+            s2[j, :, piece(k)] = total.astype(s2.dtype)
+            own[j, :, piece(k)] = total
+            return carry
+        lax.fori_loop(0, n_z, body, 0)
+
+    x_pending = x_stage(0)
+    z_pending = []
+    for k in range(pieces):
+        finish_exchange(x_pending)
+        sum_x(k)
+        z_pending.append(z_stage(k))
+        if k + 1 < pieces:
+            x_pending = x_stage(k + 1)
+    for pending in z_pending:
+        finish_exchange(pending)
     total = own[z]
     for p in z_peers:
         total = total + recv_z[p].astype(jnp.float32)
@@ -235,10 +266,10 @@
             pltpu.VMEM((n_y, half, cols // n_y), f32),
             pltpu.VMEM((half, cols), f32),
             pltpu.SemaphoreType.DMA((2,)),
-            pltpu.SemaphoreType.DMA((n_x,)),
-            pltpu.SemaphoreType.DMA((n_x,)),
-            pltpu.SemaphoreType.DMA((2 * z_hi,)),
-            pltpu.SemaphoreType.DMA((2 * z_hi,)),
+            pltpu.SemaphoreType.DMA((PIECES, n_x)),
+            pltpu.SemaphoreType.DMA((PIECES, n_x)),
+            pltpu.SemaphoreType.DMA((PIECES, 2 * z_hi)),
+            pltpu.SemaphoreType.DMA((PIECES, 2 * z_hi)),
             pltpu.SemaphoreType.DMA((n_y,)),
             pltpu.SemaphoreType.DMA((n_y,)),
             pltpu.SemaphoreType.DMA((n_y,)),

time: 235 us -> 227 us (0.966); the launches traced: 230 us -> 226 us
  Pallas kernels: 90.7 us -> 86.1 us
    pallas_call x1, Pallas kernels: 90.7 us -> 86.1 us  [grad_reduce(): pl.pallas_call(functools.partial(grad_reduce_kernel, z_hi, scale), out_sh...]
  transfers between devices with their start and end apart: 3 -> 3, of which waited for: 2 -> 2; matrix products, arithmetic and copies ran while one was open for 6% -> 6% of each run, Pallas kernels for 39% -> 38%
where the time goes in v5:
time: 227 us; the launch traced here: 226 us
  Pallas kernels  86.1 us (38%)
  waiting for transfers between devices  58.1 us (26%)
  blocking collectives  21.1 us (9%)
  matrix products  19.4 us (9%)
  between operations  14.3 us (6%)
  starting transfers between devices  12.7 us (6%)
  local copies, waits for them, and re-layouts  11.3 us (5%)
  other arithmetic  2.78 us (1%)
    pallas_call x1, Pallas kernels, grad_reduce(): pl.pallas_call(functools.partial(grad_reduce_kernel, z_hi, scale), out_sh...  86.1 us
    all_gather x1, waiting for transfers between devices, per_device(): full_weight = lax.all_gather(conv_weight, 'fsdp', axis=0, tiled=True)  39.5 us
    all_to_all x1, blocking collectives, per_device(): lax.all_to_all(request_mask, 'fsdp', split_axis=0, concat_axis=0, tiled=T...  21.1 us
    all_to_all x1, waiting for transfers between devices, per_device(): lax.all_to_all(outgoing, 'fsdp', split_axis=0, concat_axis=0, tiled=True)  17.9 us
    all_to_all x1, starting transfers between devices, per_device(): lax.all_to_all(outgoing_grad, 'fsdp', split_axis=0, concat_axis=0, tiled=...  6.86 us
    dot_general x3, matrix products, per_device(): lax.dot_general(windows[selected_index], full_weight[:, selected_index *...  5.83 us
    all_to_all x1, starting transfers between devices, per_device(): lax.all_to_all(outgoing, 'fsdp', split_axis=0, concat_axis=0, tiled=True)  5.78 us
    dot_general x1, matrix products, per_device(): lax.dot_general(routed, stacked, contract_first, preferred_element_type=j...  5.66 us
  transfers between devices with their start and end apart: 3, of which 2 were waited for; matrix products, arithmetic and copies ran while one was open for 6% of the time, Pallas kernels for 38%

profile of v5, /device:TPU:6, one launch (start us, length us, event | category | flops | bytes accessed | tf_op | source)
XLA Modules:
  0.0 225.7 jit_solution(9427570051093771993)
XLA Ops:
  8.6 21.1 %all_to_all.16 = s32[32,1,32]{2,1,0:T(1,128)S(1)} all-to-all(s32[32,1,32]{2,1,0:T(1,128)S(1)} %compare_convert_fusion), channel_id=1, replica_groups=mesh['dp'=16,'fsdp'=32] {'fsdp'}, dimensions={0} | all-to-all | bytes 8192 | tf_op jit(solution)/shard_map/all_to_all | solution.py:300
  29.7 1.8 convolution_convert_fusion.2
  31.6 1.1 copy.22
  32.7 5.8 %all-to-all-start.1 = ((bf16[32,8,1024]{2,1,0:T(8,128)(2,1)}), bf16[32,8,1024]{2,1,0:T(8,128)(2,1)S(1)}, u32[]{:S(2)}, u32[]{:S(2)}) async-start(bf16[32,8,1024]{2,1,0:T(8,128)(2,1)} %copy.22), calls=%async_computation.1 | async-start | bytes 1048576 | tf_op jit(solution)/shard_map/all_to_all | solution.py:306
  38.8 17.9 %all-to-all-done.1 = bf16[32,8,1024]{2,1,0:T(8,128)(2,1)S(1)} async-done(((bf16[32,8,1024]{2,1,0:T(8,128)(2,1)}), bf16[32,8,1024]{2,1,0:T(8,128)(2,1)S(1)}, u32[]{:S(2)}, u32[]{:S(2)}) %all-to-all-start.1) | async-done | bytes 524320 | tf_op jit(solution)/shard_map/all_to_all | solution.py:306
  56.7 0.8 convolution_convert_fusion.1
  57.5 39.5 %all-gather.2.cloned.1.call-done = bf16[1024,3072]{1,0:T(8,128)(2,1)} async-done(((bf16[32,3072]{1,0:T(8,128)(2,1)}), bf16[1024,3072]{1,0:T(8,128)(2,1)}) %all-gather.2.cloned.1.call-update) | async-done | bytes 6291472 | tf_op jit(solution)/shard_map/all_gather | solution.py:311
  97.0 2.5 %fusion = f32[256,1024]{1,0:T(8,128)S(1)} fusion(bf16[256,1024]{1,0:T(8,128)(2,1)S(1)} %copy-done.1, bf16[1024,3072]{1,0:T(8,128)(2,1)} %all-gather.2.cloned.1.call-done), kind=kOutput, calls=%fused_computation.2 | convolution fusion | flops 536870912 | bytes 3670016 | tf_op jit(solution)/shard_map/dot_general | solution.py:317
  99.5 2.4 %fusion.2 = f32[256,1024]{1,0:T(8,128)S(1)} fusion(bf16[1024,3072]{1,0:T(8,128)(2,1)} %all-gather.2.cloned.1.call-done, bf16[32,8,1024]{2,0,1:T(8,128)(2,1)S(1)} %pad_maximum_fusion), kind=kOutput, calls=%fused_computation.4 | convolution fusion | flops 536870912 | bytes 3670016 | tf_op jit(solution)/shard_map/dot_general | solution.py:317
  102.0 0.9 fusion.14
  102.9 1.0 fusion.23
  104.7 1.8 convolution_bitcast_fusion
  106.5 1.3 fusion.47
  108.7 1.0 fusion.20
  110.2 1.7 copy.31
  111.9 6.9 %all-to-all-start.2 = ((f32[32,8,1024]{2,1,0:T(8,128)}), f32[32,8,1024]{2,1,0:T(8,128)}, u32[]{:S(2)}, u32[]{:S(2)}) async-start(f32[32,8,1024]{2,1,0:T(8,128)} %copy.31), calls=%async_computation.2 | async-start | bytes 2097152 | tf_op jit(solution)/shard_map/all_to_all | solution.py:367
  118.8 1.1 copy.61
  119.9 1.1 copy.62
  121.0 1.1 copy.36
  122.3 5.7 %convolution_convert_fusion = bf16[1024,3072]{1,0:T(8,128)(2,1)} fusion(bf16[256,1024]{0,1:T(8,128)(2,1)S(1)} %bitcast.57, bf16[256,1024]{1,0:T(8,128)(2,1)S(1)} %copy-done.2, bf16[256,1024]{1,0:T(8,128)(2,1)} %bitcast.54, bf16[256,1024]{1,0:T(8,128)(2,1)} %bitcast.55), kind=kOutput, calls=%fused_computation | convolution fusion | flops 1618477056 | bytes 8388608 | tf_op jit(solution)/shard_map/dot_general | solution.py:346
  128.0 86.1 %shard_map.72 = f32[2,16,3072]{2,1,0:T(8,128)S(1)} custom-call(bf16[2,4,128,3072]{3,2,1,0:T(8,128)(2,1)} %bitcast.49), custom_call_target="tpu_custom_call" | custom-call | tf_op jit(solution)/shard_map/pallas_call | solution.py:253
  214.1 3.0 %fusion.17 = bf16[32,8,1024]{2,0,1:T(8,128)(2,1)S(1)} fusion(f32[32,16,1024]{2,0,1:T(8,128)S(1)} %fusion.20, f32[32,8,1024]{2,1,0:T(8,128)S(1)} %copy-done, f32[32,8,1024]{2,1,0:T(8,128)} %all-to-all-done.2, s32[32,1,32]{2,0,1:T(8,128)S(1)} %bitcast.59), kind=kOutput, calls=%fused_computation.18 | convolution fusion | flops 101450752 | bytes 3674112 | tf_op jit(solution)/shard_map/ns,nlc->slc/dot_general | solution.py:368
  217.1 1.1 copy.60
  218.1 0.7 copy.65
  (28 shorter events, 4.2 us)
Async XLA Ops:
  7.2 31.6 %copy-start.6 = (s32[1,32]{1,0:T(1,128)S(1)}, s32[1,32]{1,0:T(1,128)}, u32[]{:S(2)}) copy-start(s32[1,32]{1,0:T(1,128)} %param.17) | copy-start | bytes 388
  7.2 31.3 %copy-start.1 = (bf16[256,1024]{1,0:T(8,128)(2,1)S(1)}, bf16[256,1024]{1,0:T(8,128)(2,1)}, u32[]{:S(2)}) copy-start(bf16[256,1024]{1,0:T(8,128)(2,1)} %param.14) | copy-start | bytes 1572868
  7.2 89.8 %all-gather.2.cloned.1.call-start = ((), (), s32[]{:S(2)}) async-start(), calls=%async_computation.3 | async-start | bytes 6488064 | tf_op jit(solution)/shard_map/all_gather | solution.py:311
  32.7 24.0 %all-to-all-start.1 = ((bf16[32,8,1024]{2,1,0:T(8,128)(2,1)}), bf16[32,8,1024]{2,1,0:T(8,128)(2,1)S(1)}, u32[]{:S(2)}, u32[]{:S(2)}) async-start(bf16[32,8,1024]{2,1,0:T(8,128)(2,1)} %copy.22), calls=%async_computation.1 | async-start | bytes 1048576 | tf_op jit(solution)/shard_map/all_to_all | solution.py:306
  97.0 4.9 %copy-start.4 = (bf16[1024,3072]{1,0:T(8,128)(2,1)S(1)}, bf16[1024,3072]{1,0:T(8,128)(2,1)}, u32[]{:S(2)}) copy-start(bf16[1024,3072]{1,0:T(8,128)(2,1)} %all-gather.2.cloned.1.call-done) | copy-start | bytes 18874372
  102.0 1.0 copy-start.5
  104.0 0.7 copy-start.3
  111.9 102.1 %all-to-all-start.2 = ((f32[32,8,1024]{2,1,0:T(8,128)}), f32[32,8,1024]{2,1,0:T(8,128)}, u32[]{:S(2)}, u32[]{:S(2)}) async-start(f32[32,8,1024]{2,1,0:T(8,128)} %copy.31), calls=%async_computation.2 | async-start | bytes 2097152 | tf_op jit(solution)/shard_map/all_to_all | solution.py:367
  119.9 2.4 %copy-start.2 = (bf16[256,1024]{1,0:T(8,128)(2,1)S(1)}, bf16[256,1024]{1,0:T(8,128)(2,1)}, u32[]{:S(2)}) copy-start(bf16[256,1024]{1,0:T(8,128)(2,1)} %param.14) | copy-start | bytes 1572868
  128.0 86.1 %copy-start = (f32[32,8,1024]{2,1,0:T(8,128)S(1)}, f32[32,8,1024]{2,1,0:T(8,128)}, u32[]{:S(2)}) copy-start(f32[32,8,1024]{2,1,0:T(8,128)} %get-tuple-element.59) | copy-start | bytes 3145732
Sparse Core Ops, SparseCore 0:
  11.1 85.8 all-gather.1

commit v6 on v5

--- a/solution.py
+++ b/solution.py
@@ -14,7 +14,7 @@
 H = 512
 DILATION_SIZE = 4
 Z_HI = 4
-PIECES = 2
+PIECES = 4
 
 
 def all_reduce_kernel(axis, n, x_ref, out_ref, gathered, summed, send_sems, recv_sems, out_send, out_recv):

time: 227 us -> 227 us (level)
  no operation moved by 1% of the time
where the time goes in v6:
time: 227 us; the launch traced here: 226 us
  Pallas kernels  86.5 us (38%)
  waiting for transfers between devices  58.1 us (26%)
  blocking collectives  21.1 us (9%)
  matrix products  19.4 us (9%)
  between operations  14.3 us (6%)
  starting transfers between devices  12.7 us (6%)
  local copies, waits for them, and re-layouts  11.3 us (5%)
  other arithmetic  2.78 us (1%)
    pallas_call x1, Pallas kernels, grad_reduce(): pl.pallas_call(functools.partial(grad_reduce_kernel, z_hi, scale), out_sh...  86.5 us
    all_gather x1, waiting for transfers between devices, per_device(): full_weight = lax.all_gather(conv_weight, 'fsdp', axis=0, tiled=True)  39.5 us
    all_to_all x1, blocking collectives, per_device(): lax.all_to_all(request_mask, 'fsdp', split_axis=0, concat_axis=0, tiled=T...  21.1 us
    all_to_all x1, waiting for transfers between devices, per_device(): lax.all_to_all(outgoing, 'fsdp', split_axis=0, concat_axis=0, tiled=True)  17.9 us
    all_to_all x1, starting transfers between devices, per_device(): lax.all_to_all(outgoing_grad, 'fsdp', split_axis=0, concat_axis=0, tiled=...  6.86 us
    dot_general x3, matrix products, per_device(): lax.dot_general(windows[selected_index], full_weight[:, selected_index *...  5.83 us
    all_to_all x1, starting transfers between devices, per_device(): lax.all_to_all(outgoing, 'fsdp', split_axis=0, concat_axis=0, tiled=True)  5.78 us
    dot_general x1, matrix products, per_device(): lax.dot_general(routed, stacked, contract_first, preferred_element_type=j...  5.66 us
  transfers between devices with their start and end apart: 3, of which 2 were waited for; matrix products, arithmetic and copies ran while one was open for 6% of the time, Pallas kernels for 38%

profile of v6, /device:TPU:6, one launch (start us, length us, event | category | flops | bytes accessed | tf_op | source)
XLA Modules:
  0.0 226.2 jit_solution(4152089590527233729)
XLA Ops:
  8.6 21.1 %all_to_all.16 = s32[32,1,32]{2,1,0:T(1,128)S(1)} all-to-all(s32[32,1,32]{2,1,0:T(1,128)S(1)} %compare_convert_fusion), channel_id=1, replica_groups=mesh['dp'=16,'fsdp'=32] {'fsdp'}, dimensions={0} | all-to-all | bytes 8192 | tf_op jit(solution)/shard_map/all_to_all | solution.py:300
  29.7 1.8 convolution_convert_fusion.2
  31.6 1.1 copy.22
  32.7 5.8 %all-to-all-start.1 = ((bf16[32,8,1024]{2,1,0:T(8,128)(2,1)}), bf16[32,8,1024]{2,1,0:T(8,128)(2,1)S(1)}, u32[]{:S(2)}, u32[]{:S(2)}) async-start(bf16[32,8,1024]{2,1,0:T(8,128)(2,1)} %copy.22), calls=%async_computation.1 | async-start | bytes 1048576 | tf_op jit(solution)/shard_map/all_to_all | solution.py:306
  38.8 17.9 %all-to-all-done.1 = bf16[32,8,1024]{2,1,0:T(8,128)(2,1)S(1)} async-done(((bf16[32,8,1024]{2,1,0:T(8,128)(2,1)}), bf16[32,8,1024]{2,1,0:T(8,128)(2,1)S(1)}, u32[]{:S(2)}, u32[]{:S(2)}) %all-to-all-start.1) | async-done | bytes 524320 | tf_op jit(solution)/shard_map/all_to_all | solution.py:306
  56.7 0.8 convolution_convert_fusion.1
  57.5 39.5 %all-gather.2.cloned.1.call-done = bf16[1024,3072]{1,0:T(8,128)(2,1)} async-done(((bf16[32,3072]{1,0:T(8,128)(2,1)}), bf16[1024,3072]{1,0:T(8,128)(2,1)}) %all-gather.2.cloned.1.call-update) | async-done | bytes 6291472 | tf_op jit(solution)/shard_map/all_gather | solution.py:311
  97.0 2.5 %fusion = f32[256,1024]{1,0:T(8,128)S(1)} fusion(bf16[256,1024]{1,0:T(8,128)(2,1)S(1)} %copy-done.1, bf16[1024,3072]{1,0:T(8,128)(2,1)} %all-gather.2.cloned.1.call-done), kind=kOutput, calls=%fused_computation.2 | convolution fusion | flops 536870912 | bytes 3670016 | tf_op jit(solution)/shard_map/dot_general | solution.py:317
  99.5 2.4 %fusion.2 = f32[256,1024]{1,0:T(8,128)S(1)} fusion(bf16[1024,3072]{1,0:T(8,128)(2,1)} %all-gather.2.cloned.1.call-done, bf16[32,8,1024]{2,0,1:T(8,128)(2,1)S(1)} %pad_maximum_fusion), kind=kOutput, calls=%fused_computation.4 | convolution fusion | flops 536870912 | bytes 3670016 | tf_op jit(solution)/shard_map/dot_general | solution.py:317
  102.0 0.9 fusion.14
  102.9 1.0 fusion.23
  104.7 1.8 convolution_bitcast_fusion
  106.5 1.3 fusion.47
  108.7 1.0 fusion.20
  110.2 1.7 copy.31
  111.9 6.9 %all-to-all-start.2 = ((f32[32,8,1024]{2,1,0:T(8,128)}), f32[32,8,1024]{2,1,0:T(8,128)}, u32[]{:S(2)}, u32[]{:S(2)}) async-start(f32[32,8,1024]{2,1,0:T(8,128)} %copy.31), calls=%async_computation.2 | async-start | bytes 2097152 | tf_op jit(solution)/shard_map/all_to_all | solution.py:367
  118.8 1.1 copy.61
  119.9 1.1 copy.62
  121.0 1.1 copy.36
  122.3 5.7 %convolution_convert_fusion = bf16[1024,3072]{1,0:T(8,128)(2,1)} fusion(bf16[256,1024]{0,1:T(8,128)(2,1)S(1)} %bitcast.57, bf16[256,1024]{1,0:T(8,128)(2,1)S(1)} %copy-done.2, bf16[256,1024]{1,0:T(8,128)(2,1)} %bitcast.54, bf16[256,1024]{1,0:T(8,128)(2,1)} %bitcast.55), kind=kOutput, calls=%fused_computation | convolution fusion | flops 1618477056 | bytes 8388608 | tf_op jit(solution)/shard_map/dot_general | solution.py:346
  128.0 86.5 %shard_map.72 = f32[2,16,3072]{2,1,0:T(8,128)S(1)} custom-call(bf16[2,4,128,3072]{3,2,1,0:T(8,128)(2,1)} %bitcast.49), custom_call_target="tpu_custom_call" | custom-call | tf_op jit(solution)/shard_map/pallas_call | solution.py:253
  214.5 3.0 %fusion.17 = bf16[32,8,1024]{2,0,1:T(8,128)(2,1)S(1)} fusion(f32[32,16,1024]{2,0,1:T(8,128)S(1)} %fusion.20, f32[32,8,1024]{2,1,0:T(8,128)S(1)} %copy-done, f32[32,8,1024]{2,1,0:T(8,128)} %all-to-all-done.2, s32[32,1,32]{2,0,1:T(8,128)S(1)} %bitcast.59), kind=kOutput, calls=%fused_computation.18 | convolution fusion | flops 101450752 | bytes 3674112 | tf_op jit(solution)/shard_map/ns,nlc->slc/dot_general | solution.py:368
  217.5 1.1 copy.60
  218.6 0.7 copy.65
  (28 shorter events, 4.2 us)
Async XLA Ops:
  7.2 31.6 %copy-start.6 = (s32[1,32]{1,0:T(1,128)S(1)}, s32[1,32]{1,0:T(1,128)}, u32[]{:S(2)}) copy-start(s32[1,32]{1,0:T(1,128)} %param.17) | copy-start | bytes 388
  7.2 31.3 %copy-start.1 = (bf16[256,1024]{1,0:T(8,128)(2,1)S(1)}, bf16[256,1024]{1,0:T(8,128)(2,1)}, u32[]{:S(2)}) copy-start(bf16[256,1024]{1,0:T(8,128)(2,1)} %param.14) | copy-start | bytes 1572868
  7.2 89.8 %all-gather.2.cloned.1.call-start = ((), (), s32[]{:S(2)}) async-start(), calls=%async_computation.3 | async-start | bytes 6488064 | tf_op jit(solution)/shard_map/all_gather | solution.py:311
  32.7 24.0 %all-to-all-start.1 = ((bf16[32,8,1024]{2,1,0:T(8,128)(2,1)}), bf16[32,8,1024]{2,1,0:T(8,128)(2,1)S(1)}, u32[]{:S(2)}, u32[]{:S(2)}) async-start(bf16[32,8,1024]{2,1,0:T(8,128)(2,1)} %copy.22), calls=%async_computation.1 | async-start | bytes 1048576 | tf_op jit(solution)/shard_map/all_to_all | solution.py:306
  97.0 4.9 %copy-start.4 = (bf16[1024,3072]{1,0:T(8,128)(2,1)S(1)}, bf16[1024,3072]{1,0:T(8,128)(2,1)}, u32[]{:S(2)}) copy-start(bf16[1024,3072]{1,0:T(8,128)(2,1)} %all-gather.2.cloned.1.call-done) | copy-start | bytes 18874372
  102.0 1.0 copy-start.5
  104.0 0.7 copy-start.3
  111.9 102.6 %all-to-all-start.2 = ((f32[32,8,1024]{2,1,0:T(8,128)}), f32[32,8,1024]{2,1,0:T(8,128)}, u32[]{:S(2)}, u32[]{:S(2)}) async-start(f32[32,8,1024]{2,1,0:T(8,128)} %copy.31), calls=%async_computation.2 | async-start | bytes 2097152 | tf_op jit(solution)/shard_map/all_to_all | solution.py:367
  119.9 2.4 %copy-start.2 = (bf16[256,1024]{1,0:T(8,128)(2,1)S(1)}, bf16[256,1024]{1,0:T(8,128)(2,1)}, u32[]{:S(2)}) copy-start(bf16[256,1024]{1,0:T(8,128)(2,1)} %param.14) | copy-start | bytes 1572868
  128.0 86.6 %copy-start = (f32[32,8,1024]{2,1,0:T(8,128)S(1)}, f32[32,8,1024]{2,1,0:T(8,128)}, u32[]{:S(2)}) copy-start(f32[32,8,1024]{2,1,0:T(8,128)} %get-tuple-element.59) | copy-start | bytes 3145732
Sparse Core Ops, SparseCore 0:
  11.1 85.8 all-gather.1

commit v7 on v5

--- a/solution.py
+++ b/solution.py
@@ -360,16 +360,16 @@
         )
     outgoing_grad = jnp.einsum(
         "sn,slc->nlc",
-        recv_table.astype(jnp.float32),
-        grad_ext[:, :context_row_block, :],
-        precision=lax.Precision.HIGHEST,
-    )
+        recv_table,
+        grad_ext[:, :context_row_block, :].astype(jnp.bfloat16),
+        preferred_element_type=jnp.float32,
+    ).astype(jnp.bfloat16)
     incoming_grad = lax.all_to_all(outgoing_grad, "fsdp", split_axis=0, concat_axis=0, tiled=True)
     tail_grad = jnp.einsum(
         "ns,nlc->slc",
-        send_table.astype(jnp.float32),
+        send_table,
         incoming_grad,
-        precision=lax.Precision.HIGHEST,
+        preferred_element_type=jnp.float32,
     )
     grad_in = (
         grad_ext[:, context_row_block:, :].at[:, seg_rows - context_row_block :, :].add(tail_grad)

time: 227 us -> 226 us (level)
  no operation moved by 1% of the time
where the time goes in v7:
time: 226 us; the launch traced here: 224 us
  Pallas kernels  85.6 us (38%)
  waiting for transfers between devices  58.1 us (26%)
  blocking collectives  21.1 us (9%)
  matrix products  18.5 us (8%)
  between operations  14.3 us (6%)
  starting transfers between devices  12.7 us (6%)
  local copies, waits for them, and re-layouts  10.8 us (5%)
  other arithmetic  2.78 us (1%)
    pallas_call x1, Pallas kernels, grad_reduce(): pl.pallas_call(functools.partial(grad_reduce_kernel, z_hi, scale), out_sh...  85.6 us
    all_gather x1, waiting for transfers between devices, per_device(): full_weight = lax.all_gather(conv_weight, 'fsdp', axis=0, tiled=True)  39.5 us
    all_to_all x1, blocking collectives, per_device(): lax.all_to_all(request_mask, 'fsdp', split_axis=0, concat_axis=0, tiled=T...  21.1 us
    all_to_all x1, waiting for transfers between devices, per_device(): lax.all_to_all(outgoing, 'fsdp', split_axis=0, concat_axis=0, tiled=True)  17.9 us
    all_to_all x1, starting transfers between devices, per_device(): lax.all_to_all(outgoing_grad, 'fsdp', split_axis=0, concat_axis=0, tiled=...  6.86 us
    dot_general x3, matrix products, per_device(): lax.dot_general(windows[selected_index], full_weight[:, selected_index *...  5.83 us
    all_to_all x1, starting transfers between devices, per_device(): lax.all_to_all(outgoing, 'fsdp', split_axis=0, concat_axis=0, tiled=True)  5.78 us
    dot_general x1, matrix products, per_device(): lax.dot_general(routed, stacked, contract_first, preferred_element_type=j...  5.66 us
  transfers between devices with their start and end apart: 3, of which 2 were waited for; matrix products, arithmetic and copies ran while one was open for 6% of the time, Pallas kernels for 38%

profile of v7, /device:TPU:6, one launch (start us, length us, event | category | flops | bytes accessed | tf_op | source)
XLA Modules:
  0.0 223.7 jit_solution(2203448400042967496)
XLA Ops:
  8.6 21.1 %all_to_all.16 = s32[32,1,32]{2,1,0:T(1,128)S(1)} all-to-all(s32[32,1,32]{2,1,0:T(1,128)S(1)} %compare_convert_fusion), channel_id=1, replica_groups=mesh['dp'=16,'fsdp'=32] {'fsdp'}, dimensions={0} | all-to-all | bytes 8192 | tf_op jit(solution)/shard_map/all_to_all | solution.py:300
  29.7 1.8 convolution_convert_fusion.3
  31.6 1.1 copy.22
  32.7 5.8 %all-to-all-start.1 = ((bf16[32,8,1024]{2,1,0:T(8,128)(2,1)}), bf16[32,8,1024]{2,1,0:T(8,128)(2,1)S(1)}, u32[]{:S(2)}, u32[]{:S(2)}) async-start(bf16[32,8,1024]{2,1,0:T(8,128)(2,1)} %copy.22), calls=%async_computation.1 | async-start | bytes 1048576 | tf_op jit(solution)/shard_map/all_to_all | solution.py:306
  38.8 17.9 %all-to-all-done.1 = bf16[32,8,1024]{2,1,0:T(8,128)(2,1)S(1)} async-done(((bf16[32,8,1024]{2,1,0:T(8,128)(2,1)}), bf16[32,8,1024]{2,1,0:T(8,128)(2,1)S(1)}, u32[]{:S(2)}, u32[]{:S(2)}) %all-to-all-start.1) | async-done | bytes 524320 | tf_op jit(solution)/shard_map/all_to_all | solution.py:306
  56.7 0.8 convolution_convert_fusion.2
  57.5 39.5 %all-gather.2.cloned.1.call-done = bf16[1024,3072]{1,0:T(8,128)(2,1)} async-done(((bf16[32,3072]{1,0:T(8,128)(2,1)}), bf16[1024,3072]{1,0:T(8,128)(2,1)}) %all-gather.2.cloned.1.call-update) | async-done | bytes 6291472 | tf_op jit(solution)/shard_map/all_gather | solution.py:311
  97.0 2.5 %fusion = f32[256,1024]{1,0:T(8,128)S(1)} fusion(bf16[256,1024]{1,0:T(8,128)(2,1)S(1)} %copy-done.1, bf16[1024,3072]{1,0:T(8,128)(2,1)} %all-gather.2.cloned.1.call-done), kind=kOutput, calls=%fused_computation.2 | convolution fusion | flops 536870912 | bytes 3670016 | tf_op jit(solution)/shard_map/dot_general | solution.py:317
  99.5 2.4 %fusion.2 = f32[256,1024]{1,0:T(8,128)S(1)} fusion(bf16[1024,3072]{1,0:T(8,128)(2,1)} %all-gather.2.cloned.1.call-done, bf16[32,8,1024]{2,0,1:T(8,128)(2,1)S(1)} %pad_maximum_fusion), kind=kOutput, calls=%fused_computation.4 | convolution fusion | flops 536870912 | bytes 3670016 | tf_op jit(solution)/shard_map/dot_general | solution.py:317
  102.0 0.9 fusion.14
  102.9 1.0 fusion.20
  104.7 1.8 convolution_bitcast_fusion
  106.5 1.3 fusion.45
  108.7 1.0 fusion.18
  109.9 1.1 copy.31
  111.0 6.9 %all-to-all-start.2 = ((bf16[32,8,1024]{2,1,0:T(8,128)(2,1)}), bf16[32,8,1024]{2,1,0:T(8,128)(2,1)}, u32[]{:S(2)}, u32[]{:S(2)}) async-start(bf16[32,8,1024]{2,1,0:T(8,128)(2,1)} %copy.31), calls=%async_computation.2 | async-start | bytes 1048576 | tf_op jit(solution)/shard_map/all_to_all | solution.py:367
  117.9 1.1 copy.61
  119.0 1.1 copy.62
  120.1 1.1 copy.36
  121.5 5.7 %convolution_convert_fusion = bf16[1024,3072]{1,0:T(8,128)(2,1)} fusion(bf16[256,1024]{0,1:T(8,128)(2,1)S(1)} %bitcast.57, bf16[256,1024]{1,0:T(8,128)(2,1)S(1)} %copy-done.2, bf16[256,1024]{1,0:T(8,128)(2,1)} %bitcast.54, bf16[256,1024]{1,0:T(8,128)(2,1)} %bitcast.55), kind=kOutput, calls=%fused_computation | convolution fusion | flops 1618477056 | bytes 8388608 | tf_op jit(solution)/shard_map/dot_general | solution.py:346
  127.1 85.6 %shard_map.72 = f32[2,16,3072]{2,1,0:T(8,128)S(1)} custom-call(bf16[2,4,128,3072]{3,2,1,0:T(8,128)(2,1)} %bitcast.49), custom_call_target="tpu_custom_call" | custom-call | tf_op jit(solution)/shard_map/pallas_call | solution.py:253
  212.7 2.3 %fusion.17 = bf16[32,8,1024]{2,0,1:T(8,128)(2,1)S(1)} fusion(f32[32,16,1024]{2,0,1:T(8,128)S(1)} %fusion.18, f32[32,8,1024]{2,1,0:T(8,128)S(1)} %copy-done, bf16[32,8,1024]{2,1,0:T(8,128)(2,1)} %all-to-all-done.2, s32[32,1,32]{2,0,1:T(8,128)S(1)} %bitcast.59), kind=kOutput, calls=%fused_computation.16 | convolution fusion | flops 17564672 | bytes 3149824 | tf_op jit(solution)/shard_map/ns,nlc->slc/dot_general | solution.py:368
  215.0 1.1 copy.60
  216.1 0.7 copy.65
  (28 shorter events, 3.9 us)
Async XLA Ops:
  7.2 31.6 %copy-start.6 = (s32[1,32]{1,0:T(1,128)S(1)}, s32[1,32]{1,0:T(1,128)}, u32[]{:S(2)}) copy-start(s32[1,32]{1,0:T(1,128)} %param.17) | copy-start | bytes 388
  7.2 31.3 %copy-start.1 = (bf16[256,1024]{1,0:T(8,128)(2,1)S(1)}, bf16[256,1024]{1,0:T(8,128)(2,1)}, u32[]{:S(2)}) copy-start(bf16[256,1024]{1,0:T(8,128)(2,1)} %param.14) | copy-start | bytes 1572868
  7.2 89.8 %all-gather.2.cloned.1.call-start = ((), (), s32[]{:S(2)}) async-start(), calls=%async_computation.3 | async-start | bytes 6488064 | tf_op jit(solution)/shard_map/all_gather | solution.py:311
  32.7 24.0 %all-to-all-start.1 = ((bf16[32,8,1024]{2,1,0:T(8,128)(2,1)}), bf16[32,8,1024]{2,1,0:T(8,128)(2,1)S(1)}, u32[]{:S(2)}, u32[]{:S(2)}) async-start(bf16[32,8,1024]{2,1,0:T(8,128)(2,1)} %copy.22), calls=%async_computation.1 | async-start | bytes 1048576 | tf_op jit(solution)/shard_map/all_to_all | solution.py:306
  97.0 4.9 %copy-start.4 = (bf16[1024,3072]{1,0:T(8,128)(2,1)S(1)}, bf16[1024,3072]{1,0:T(8,128)(2,1)}, u32[]{:S(2)}) copy-start(bf16[1024,3072]{1,0:T(8,128)(2,1)} %all-gather.2.cloned.1.call-done) | copy-start | bytes 18874372
  102.0 1.0 copy-start.5
  104.0 0.7 copy-start.3
  111.0 101.7 %all-to-all-start.2 = ((bf16[32,8,1024]{2,1,0:T(8,128)(2,1)}), bf16[32,8,1024]{2,1,0:T(8,128)(2,1)}, u32[]{:S(2)}, u32[]{:S(2)}) async-start(bf16[32,8,1024]{2,1,0:T(8,128)(2,1)} %copy.31), calls=%async_computation.2 | async-start | bytes 1048576 | tf_op jit(solution)/shard_map/all_to_all | solution.py:367
  119.0 2.5 %copy-start.2 = (bf16[256,1024]{1,0:T(8,128)(2,1)S(1)}, bf16[256,1024]{1,0:T(8,128)(2,1)}, u32[]{:S(2)}) copy-start(bf16[256,1024]{1,0:T(8,128)(2,1)} %param.14) | copy-start | bytes 1572868
  127.1 85.6 %copy-start = (f32[32,8,1024]{2,1,0:T(8,128)S(1)}, f32[32,8,1024]{2,1,0:T(8,128)}, u32[]{:S(2)}) copy-start(f32[32,8,1024]{2,1,0:T(8,128)} %get-tuple-element.59) | copy-start | bytes 3145732
Sparse Core Ops, SparseCore 0:
  11.1 85.8 all-gather.1

commit v8 on v7

--- a/solution.py
+++ b/solution.py
@@ -105,8 +105,9 @@
     return out.reshape(shape)
 
 
-def grad_reduce_kernel(z_hi, scale, p_ref, out_ref, recv_c, s1b, recv_x, s2, own, recv_z, s3, recv_y, g16,
-                       core_sems, x_send, x_recv, z_send, z_recv, y_send, y_recv, g_send, g_recv, pair_sems):
+def grad_reduce_kernel(z_hi, scale, p_ref, back_ref, out_ref, back_out, recv_c, s1b, recv_x, s2, own, recv_z, s3, recv_y, g16,
+                       core_sems, x_send, x_recv, z_send, z_recv, y_send, y_recv, g_send, g_recv, pair_sems,
+                       back_sems):
     n_x = recv_x.shape[0]
     n_z = 2 * z_hi
     n_y = recv_y.shape[0]
@@ -129,9 +130,10 @@
     x_peers = [lax.rem(x + k, n_x) for k in range(1, n_x)]
     z_peers = [lax.rem(z + k, n_z) for k in range(1, n_z)]
     y_peers = [lax.rem(y + k, n_y) for k in range(1, n_y)]
-    everyone = [partner]
-    everyone += [device(xp, zh, c, y, zl) for xp in x_peers]
-    everyone += [device(x, zp // 2, c, y, lax.rem(zp, 2)) for zp in z_peers]
+    n_f = back_ref.shape[0]
+    f_peers = [lax.rem(f + k, n_f) for k in range(1, n_f)]
+    everyone = [{"dp": d, "fsdp": fp} for fp in f_peers]
+    everyone += [device(x, zp // 2, c, y, lax.rem(zp, 2)) for k, zp in enumerate(z_peers, 1) if k % 2]
     everyone += [device(x, zh, c, yp, zl) for yp in y_peers]
     barrier = pltpu.get_barrier_semaphore()
     for peer in everyone:
@@ -161,6 +163,9 @@
     def exchange(*args):
         finish_exchange(start_exchange(*args))
 
+    back_pending = start_exchange(lambda p: back_ref.at[p], lambda p: back_out.at[p], back_sems.at[0],
+                                  back_sems.at[1], f_peers, f, lambda p: {"dp": d, "fsdp": p})
+    back_out[f] = back_ref[f]
     core_copy = pltpu.make_async_remote_copy(
         src_ref=p_ref.at[1 - c], dst_ref=recv_c, send_sem=core_sems.at[0],
         recv_sem=core_sems.at[1], device_id=partner, device_id_type=MESH)
@@ -240,9 +245,10 @@
         src_ref=g16, dst_ref=out_ref.at[1 - zl], send_sem=pair_sems.at[0], recv_sem=pair_sems.at[1],
         device_id=device(x, zh, c, y, 1 - zl), device_id_type=MESH).wait_recv()
     pair_copy.wait_send()
-
-
-def grad_reduce(partial_rows, z_hi, scale):
+    finish_exchange(back_pending)
+
+
+def grad_reduce(partial_rows, back, z_hi, scale):
     n_x = partial_rows.shape[1]
     n_y = lax.axis_size("dp") // 2
     cols = partial_rows.shape[3]
@@ -252,9 +258,9 @@
     f32 = jnp.float32
     return pl.pallas_call(
         functools.partial(grad_reduce_kernel, z_hi, scale),
-        out_shape=jax.ShapeDtypeStruct((2, half, cols), f32),
-        in_specs=[pl.BlockSpec(memory_space=pltpu.VMEM)],
-        out_specs=pl.BlockSpec(memory_space=pltpu.VMEM),
+        out_shape=(jax.ShapeDtypeStruct((2, half, cols), f32), jax.ShapeDtypeStruct(back.shape, back.dtype)),
+        in_specs=[pl.BlockSpec(memory_space=pltpu.VMEM)] * 2,
+        out_specs=(pl.BlockSpec(memory_space=pltpu.VMEM),) * 2,
         scratch_shapes=[
             pltpu.VMEM((n_x, band, cols), partial_rows.dtype),
             pltpu.VMEM((n_x, band, cols), partial_rows.dtype),
@@ -275,10 +281,11 @@
             pltpu.SemaphoreType.DMA((n_y,)),
             pltpu.SemaphoreType.DMA((n_y,)),
             pltpu.SemaphoreType.DMA((2,)),
+            pltpu.SemaphoreType.DMA((2, back.shape[0])),
         ],
         compiler_params=pltpu.CompilerParams(
             collective_id=1, has_side_effects=True, vmem_limit_bytes=48 * 1024 * 1024),
-    )(partial_rows)
+    )(partial_rows, back)
 
 
 def tap_starts(context_row_block):
@@ -346,11 +353,6 @@
     partial_value = lax.dot_general(
         routed, stacked, contract_first, preferred_element_type=jnp.float32
     ).astype(jnp.bfloat16)
-    total_token_count = row_count * peer_count * lax.axis_size("dp")
-    reduced = grad_reduce(
-        partial_value.reshape(2, n_x, z_hi * shard, 3 * C), z_hi, 1.0 / math.sqrt(total_token_count)
-    )
-    grad_weight = reduced.reshape(shard, 3 * C)
     back_proj = jnp.dot(grad_pre, full_weight, preferred_element_type=jnp.float32)
     back_proj = back_proj.reshape(seg_count, seg_rows, 3 * C)
     grad_ext = jnp.zeros((seg_count, context_row_block + seg_rows, C), jnp.float32)
@@ -364,7 +366,14 @@
         grad_ext[:, :context_row_block, :].astype(jnp.bfloat16),
         preferred_element_type=jnp.float32,
     ).astype(jnp.bfloat16)
-    incoming_grad = lax.all_to_all(outgoing_grad, "fsdp", split_axis=0, concat_axis=0, tiled=True)
+    total_token_count = row_count * peer_count * lax.axis_size("dp")
+    reduced, incoming_grad = grad_reduce(
+        partial_value.reshape(2, n_x, z_hi * shard, 3 * C),
+        outgoing_grad,
+        z_hi,
+        1.0 / math.sqrt(total_token_count),
+    )
+    grad_weight = reduced.reshape(shard, 3 * C)
     tail_grad = jnp.einsum(
         "ns,nlc->slc",
         send_table,

time: 226 us -> 216 us (0.956)
  starting transfers between devices: 12.7 us -> 5.81 us
  local copies, waits for them, and re-layouts: 10.8 us -> 5.58 us
    all_to_all x1 -> x0, starting transfers between devices: 6.86 us -> none  [per_device(): lax.all_to_all(outgoing_grad, 'fsdp', split_axis=0, concat_axis=0, tiled=...]
    dot_general x1, matrix products: 1.79 us -> 4.57 us  [per_device(): jnp.dot(grad_pre, full_weight, preferred_element_type=jnp.float32)]
  transfers between devices with their start and end apart: 3 -> 2, of which waited for: 2 -> 2; matrix products, arithmetic and copies ran while one was open for 6% -> 2% of each run, Pallas kernels for 38% -> 0%
where the time goes in v8:
time: 216 us; the launch traced here: 215 us
  Pallas kernels  87 us (40%)
  waiting for transfers between devices  57.5 us (27%)
  blocking collectives  21.1 us (10%)
  matrix products  20.5 us (9%)
  between operations  14.2 us (7%)
  starting transfers between devices  5.81 us (3%)
  local copies, waits for them, and re-layouts  5.58 us (3%)
  other arithmetic  2.78 us (1%)
    pallas_call x1, Pallas kernels, grad_reduce(): pl.pallas_call(functools.partial(grad_reduce_kernel, z_hi, scale), out_sh...  87 us
    all_gather x1, waiting for transfers between devices, per_device(): full_weight = lax.all_gather(conv_weight, 'fsdp', axis=0, tiled=True)  39 us
    all_to_all x1, blocking collectives, per_device(): lax.all_to_all(request_mask, 'fsdp', split_axis=0, concat_axis=0, tiled=T...  21.1 us
    all_to_all x1, waiting for transfers between devices, per_device(): lax.all_to_all(outgoing, 'fsdp', split_axis=0, concat_axis=0, tiled=True)  17.9 us
    dot_general x3, matrix products, per_device(): lax.dot_general(windows[selected_index], full_weight[:, selected_index *...  7.28 us
    all_to_all x1, starting transfers between devices, per_device(): lax.all_to_all(outgoing, 'fsdp', split_axis=0, concat_axis=0, tiled=True)  5.78 us
    dot_general x1, matrix products, per_device(): jnp.dot(grad_pre, full_weight, preferred_element_type=jnp.float32)  4.57 us
    dot_general x1, matrix products, per_device(): lax.dot_general(routed, stacked, contract_first, preferred_element_type=j...  4.47 us
  transfers between devices with their start and end apart: 2, of which 2 were waited for; matrix products, arithmetic and copies ran while one was open for 2% of the time, Pallas kernels for 0%

profile of v8, /device:TPU:6, one launch (start us, length us, event | category | flops | bytes accessed | tf_op | source)
XLA Modules:
  0.0 214.5 jit_solution(3744820154232310707)
XLA Ops:
  7.2 0.7 all-gather.2.cloned.1.call-update
  7.9 0.7 fusion.42
  8.6 21.1 %all_to_all.11 = s32[32,1,32]{2,1,0:T(1,128)S(1)} all-to-all(s32[32,1,32]{2,1,0:T(1,128)S(1)} %compare_convert_fusion), channel_id=1, replica_groups=mesh['dp'=16,'fsdp'=32] {'fsdp'}, dimensions={0} | all-to-all | bytes 8192 | tf_op jit(solution)/shard_map/all_to_all | solution.py:307
  29.7 1.8 convolution_convert_fusion.2
  31.6 1.1 copy.28
  32.7 5.8 %all-to-all-start.1 = ((bf16[32,8,1024]{2,1,0:T(8,128)(2,1)}), bf16[32,8,1024]{2,1,0:T(8,128)(2,1)S(1)}, u32[]{:S(2)}, u32[]{:S(2)}) async-start(bf16[32,8,1024]{2,1,0:T(8,128)(2,1)} %copy.28), calls=%async_computation.1 | async-start | bytes 1048576 | tf_op jit(solution)/shard_map/all_to_all | solution.py:313
  38.8 17.9 %all-to-all-done.1 = bf16[32,8,1024]{2,1,0:T(8,128)(2,1)S(1)} async-done(((bf16[32,8,1024]{2,1,0:T(8,128)(2,1)}), bf16[32,8,1024]{2,1,0:T(8,128)(2,1)S(1)}, u32[]{:S(2)}, u32[]{:S(2)}) %all-to-all-start.1) | async-done | bytes 524320 | tf_op jit(solution)/shard_map/all_to_all | solution.py:313
  56.7 0.8 convolution_convert_fusion.1
  57.5 0.6 copy_bitcast_fusion.1
  58.1 39.0 %all-gather.2.cloned.1.call-done = bf16[1024,3072]{1,0:T(8,128)(2,1)} async-done(((bf16[32,3072]{1,0:T(8,128)(2,1)}), bf16[1024,3072]{1,0:T(8,128)(2,1)}) %all-gather.2.cloned.1.call-update) | async-done | bytes 6291472 | tf_op jit(solution)/shard_map/all_gather | solution.py:318
  97.0 2.3 %fusion = f32[256,1024]{1,0:T(8,128)S(1)} fusion(bf16[256,1024]{1,0:T(8,128)(2,1)S(1)} %copy-done, bf16[1024,3072]{1,0:T(8,128)(2,1)} %all-gather.2.cloned.1.call-done), kind=kOutput, calls=%fused_computation.2 | convolution fusion | flops 536870912 | bytes 3670016 | tf_op jit(solution)/shard_map/dot_general | solution.py:324
  99.4 2.4 %fusion.2 = f32[256,1024]{1,0:T(8,128)S(1)} fusion(bf16[1024,3072]{1,0:T(8,128)(2,1)} %all-gather.2.cloned.1.call-done, bf16[32,8,1024]{2,0,1:T(8,128)(2,1)S(1)} %pad_maximum_fusion), kind=kOutput, calls=%fused_computation.4 | convolution fusion | flops 536870912 | bytes 3670016 | tf_op jit(solution)/shard_map/dot_general | solution.py:324
  101.8 2.5 %fusion.14 = f32[256,1024]{1,0:T(8,128)S(1)} fusion(f32[256,1024]{1,0:T(8,128)S(1)} %fusion, f32[256,1024]{1,0:T(8,128)S(1)} %fusion.2, bf16[1024,3072]{1,0:T(8,128)(2,1)} %all-gather.2.cloned.1.call-done, bf16[32,8,1024]{2,0,1:T(8,128)(2,1)S(1)} %convolution_convert_fusion.1), kind=kOutput, calls=%fused_computation.15 | convolution fusion | flops 537395200 | bytes 5767168 | tf_op jit(solution)/shard_map/dot_general | solution.py:324
  104.4 1.0 fusion.20
  105.7 4.6 %convolution_bitcast_fusion = f32[32,8,3072]{2,1,0:T(8,128)S(1)} fusion(bf16[1024,3072]{1,0:T(8,128)(2,1)} %all-gather.2.cloned.1.call-done, bf16[256,512]{1,0:T(8,128)(2,1)S(1)} %get-tuple-element.67, bf16[256,512]{1,0:T(8,128)(2,1)S(1)} %get-tuple-element.66), kind=kOutput, calls=%fused_computation.1 | convolution fusion | flops 1611661312 | bytes 9961472 | tf_op jit(solution)/shard_map/dot_general | solution.py:356
  110.2 0.3 fusion.46
  110.6 0.6 copy.48
  111.5 1.0 fusion.18
  112.8 0.3 copy.67.back_ref
  113.1 4.5 %convolution_convert_fusion = bf16[1024,3072]{1,0:T(8,128)(2,1)} fusion(bf16[256,1024]{0,1:T(8,128)(2,1)S(1)} %bitcast.52, bf16[256,1024]{1,0:T(8,128)(2,1)S(1)} %copy-done, bf16[256,1024]{1,0:T(8,128)(2,1)S(1)} %get-tuple-element.69, bf16[256,1024]{1,0:T(8,128)(2,1)S(1)} %get-tuple-element.70), kind=kOutput, calls=%fused_computation | convolution fusion | flops 1618477056 | bytes 8388608 | tf_op jit(solution)/shard_map/dot_general | solution.py:353
  117.6 87.0 %shard_map.72 = (f32[2,16,3072]{2,1,0:T(8,128)S(1)}, bf16[32,8,1024]{2,1,0:T(8,128)(2,1)S(1)}) custom-call(bf16[2,4,128,3072]{3,2,1,0:T(8,128)(2,1)} %bitcast.47, bf16[32,8,1024]{2,1,0:T(8,128)(2,1)S(1)} %copy.67.back_ref), custom_call_target="tpu_custom_call" | custom-call | tf_op jit(solution)/shard_map/pallas_call | solution.py:259
  204.6 1.3 fusion.17
  205.8 1.1 copy.68
  206.9 0.7 copy.71
  (17 shorter events, 1.3 us)
Async XLA Ops:
  7.2 31.6 %copy-start.2 = (s32[1,32]{1,0:T(1,128)S(1)}, s32[1,32]{1,0:T(1,128)}, u32[]{:S(2)}) copy-start(s32[1,32]{1,0:T(1,128)} %param.17) | copy-start | bytes 388
  7.2 31.3 %copy-start = (bf16[256,1024]{1,0:T(8,128)(2,1)S(1)}, bf16[256,1024]{1,0:T(8,128)(2,1)}, u32[]{:S(2)}) copy-start(bf16[256,1024]{1,0:T(8,128)(2,1)} %param.14) | copy-start | bytes 1572868
  7.2 89.9 %all-gather.2.cloned.1.call-start = ((), (), s32[]{:S(2)}) async-start(), calls=%async_computation.2 | async-start | bytes 6488064 | tf_op jit(solution)/shard_map/all_gather | solution.py:318
  32.7 24.0 %all-to-all-start.1 = ((bf16[32,8,1024]{2,1,0:T(8,128)(2,1)}), bf16[32,8,1024]{2,1,0:T(8,128)(2,1)S(1)}, u32[]{:S(2)}, u32[]{:S(2)}) async-start(bf16[32,8,1024]{2,1,0:T(8,128)(2,1)} %copy.28), calls=%async_computation.1 | async-start | bytes 1048576 | tf_op jit(solution)/shard_map/all_to_all | solution.py:313
  101.8 2.5 %copy-start.1 = (bf16[256,512]{1,0:T(8,128)(2,1)S(1)}, bf16[256,512]{1,0:T(8,128)(2,1)}, u32[]{:S(2)}) copy-start(bf16[256,512]{1,0:T(8,128)(2,1)} %param.15) | copy-start | bytes 786436
Sparse Core Ops, SparseCore 0:
  11.1 85.8 all-gather.1

commit v9 on v8

--- a/solution.py
+++ b/solution.py
@@ -135,6 +135,7 @@
     everyone = [{"dp": d, "fsdp": fp} for fp in f_peers]
     everyone += [device(x, zp // 2, c, y, lax.rem(zp, 2)) for k, zp in enumerate(z_peers, 1) if k % 2]
     everyone += [device(x, zh, c, yp, zl) for yp in y_peers]
+    everyone += [device(x, zh, c, yp, 1 - zl) for yp in y_peers]
     barrier = pltpu.get_barrier_semaphore()
     for peer in everyone:
         pl.semaphore_signal(barrier, inc=1, device_id=peer, device_id_type=MESH)
@@ -233,18 +234,12 @@
     total = s3[:, cols(y)]
     for p in y_peers:
         total = total + recv_y[p]
-    g16[:, cols(y)] = total * scale
-    exchange(lambda p: g16.at[:, cols(y)], lambda p: g16.at[:, cols(p)], g_send, g_recv, y_peers, y,
-             lambda p: device(x, zh, c, p, zl))
-    out_ref[zl] = g16[...]
-    pair_copy = pltpu.make_async_remote_copy(
-        src_ref=g16, dst_ref=out_ref.at[zl], send_sem=pair_sems.at[0], recv_sem=pair_sems.at[1],
-        device_id=device(x, zh, c, y, 1 - zl), device_id_type=MESH)
-    pair_copy.start()
-    pltpu.make_async_remote_copy(
-        src_ref=g16, dst_ref=out_ref.at[1 - zl], send_sem=pair_sems.at[0], recv_sem=pair_sems.at[1],
-        device_id=device(x, zh, c, y, 1 - zl), device_id_type=MESH).wait_recv()
-    pair_copy.wait_send()
+    n_dp = g_send.shape[0]
+    out_ref[zl, :, cols(y)] = total * scale
+    g16[...] = total * scale
+    dp_peers = [lax.rem(d + k, n_dp) for k in range(1, n_dp)]
+    exchange(lambda q: g16, lambda q: out_ref.at[lax.rem(q, 2), :, cols(q // 2)], g_send, g_recv, dp_peers, d,
+             lambda q: {"dp": q, "fsdp": f})
     finish_exchange(back_pending)
 
 
@@ -270,7 +265,7 @@
             pltpu.VMEM((2 * z_hi, half, cols), partial_rows.dtype),
             pltpu.VMEM((half, cols), f32),
             pltpu.VMEM((n_y, half, cols // n_y), f32),
-            pltpu.VMEM((half, cols), f32),
+            pltpu.VMEM((half, cols // n_y), f32),
             pltpu.SemaphoreType.DMA((2,)),
             pltpu.SemaphoreType.DMA((PIECES, n_x)),
             pltpu.SemaphoreType.DMA((PIECES, n_x)),
@@ -278,8 +273,8 @@
             pltpu.SemaphoreType.DMA((PIECES, 2 * z_hi)),
             pltpu.SemaphoreType.DMA((n_y,)),
             pltpu.SemaphoreType.DMA((n_y,)),
-            pltpu.SemaphoreType.DMA((n_y,)),
-            pltpu.SemaphoreType.DMA((n_y,)),
+            pltpu.SemaphoreType.DMA((2 * n_y,)),
+            pltpu.SemaphoreType.DMA((2 * n_y,)),
             pltpu.SemaphoreType.DMA((2,)),
             pltpu.SemaphoreType.DMA((2, back.shape[0])),
         ],

time: 216 us -> 218 us (level)
  Pallas kernels: 87 us -> 90.3 us
    pallas_call x1, Pallas kernels: 87 us -> 90.3 us  [grad_reduce(): pl.pallas_call(functools.partial(grad_reduce_kernel, z_hi, scale), out_sh...]
where the time goes in v9:
time: 218 us
  Pallas kernels  90.3 us (41%)
  waiting for transfers between devices  57.5 us (26%)
  blocking collectives  21.1 us (10%)
  matrix products  20.5 us (9%)
  between operations  14.2 us (7%)
  starting transfers between devices  5.82 us (3%)
  local copies, waits for them, and re-layouts  5.58 us (3%)
  other arithmetic  2.78 us (1%)
    pallas_call x1, Pallas kernels, grad_reduce(): pl.pallas_call(functools.partial(grad_reduce_kernel, z_hi, scale), out_sh...  90.3 us
    all_gather x1, waiting for transfers between devices, per_device(): full_weight = lax.all_gather(conv_weight, 'fsdp', axis=0, tiled=True)  39 us
    all_to_all x1, blocking collectives, per_device(): lax.all_to_all(request_mask, 'fsdp', split_axis=0, concat_axis=0, tiled=T...  21.1 us
    all_to_all x1, waiting for transfers between devices, per_device(): lax.all_to_all(outgoing, 'fsdp', split_axis=0, concat_axis=0, tiled=True)  17.9 us
    dot_general x3, matrix products, per_device(): lax.dot_general(windows[selected_index], full_weight[:, selected_index *...  7.28 us
    all_to_all x1, starting transfers between devices, per_device(): lax.all_to_all(outgoing, 'fsdp', split_axis=0, concat_axis=0, tiled=True)  5.78 us
    dot_general x1, matrix products, per_device(): jnp.dot(grad_pre, full_weight, preferred_element_type=jnp.float32)  4.57 us
    dot_general x1, matrix products, per_device(): lax.dot_general(routed, stacked, contract_first, preferred_element_type=j...  4.47 us
  transfers between devices with their start and end apart: 2, of which 2 were waited for; matrix products, arithmetic and copies ran while one was open for 2% of the time, Pallas kernels for 0%

profile of v9, /device:TPU:6, one launch (start us, length us, event | category | flops | bytes accessed | tf_op | source)
XLA Modules:
  0.0 217.8 jit_solution(14700975399597076100)
XLA Ops:
  7.2 0.7 all-gather.2.cloned.1.call-update
  7.9 0.7 fusion.42
  8.6 21.1 %all_to_all.11 = s32[32,1,32]{2,1,0:T(1,128)S(1)} all-to-all(s32[32,1,32]{2,1,0:T(1,128)S(1)} %compare_convert_fusion), channel_id=1, replica_groups=mesh['dp'=16,'fsdp'=32] {'fsdp'}, dimensions={0} | all-to-all | bytes 8192 | tf_op jit(solution)/shard_map/all_to_all | solution.py:302
  29.7 1.8 convolution_convert_fusion.2
  31.6 1.1 copy.28
  32.7 5.8 %all-to-all-start.1 = ((bf16[32,8,1024]{2,1,0:T(8,128)(2,1)}), bf16[32,8,1024]{2,1,0:T(8,128)(2,1)S(1)}, u32[]{:S(2)}, u32[]{:S(2)}) async-start(bf16[32,8,1024]{2,1,0:T(8,128)(2,1)} %copy.28), calls=%async_computation.1 | async-start | bytes 1048576 | tf_op jit(solution)/shard_map/all_to_all | solution.py:308
  38.5 0.3 copy.27
  38.8 17.9 %all-to-all-done.1 = bf16[32,8,1024]{2,1,0:T(8,128)(2,1)S(1)} async-done(((bf16[32,8,1024]{2,1,0:T(8,128)(2,1)}), bf16[32,8,1024]{2,1,0:T(8,128)(2,1)S(1)}, u32[]{:S(2)}, u32[]{:S(2)}) %all-to-all-start.1) | async-done | bytes 524320 | tf_op jit(solution)/shard_map/all_to_all | solution.py:308
  56.7 0.8 convolution_convert_fusion.1
  57.5 0.6 copy_bitcast_fusion.1
  58.1 39.0 %all-gather.2.cloned.1.call-done = bf16[1024,3072]{1,0:T(8,128)(2,1)} async-done(((bf16[32,3072]{1,0:T(8,128)(2,1)}), bf16[1024,3072]{1,0:T(8,128)(2,1)}) %all-gather.2.cloned.1.call-update) | async-done | bytes 6291472 | tf_op jit(solution)/shard_map/all_gather | solution.py:313
  97.0 2.3 %fusion = f32[256,1024]{1,0:T(8,128)S(1)} fusion(bf16[256,1024]{1,0:T(8,128)(2,1)S(1)} %copy-done, bf16[1024,3072]{1,0:T(8,128)(2,1)} %all-gather.2.cloned.1.call-done), kind=kOutput, calls=%fused_computation.2 | convolution fusion | flops 536870912 | bytes 3670016 | tf_op jit(solution)/shard_map/dot_general | solution.py:319
  99.4 2.4 %fusion.2 = f32[256,1024]{1,0:T(8,128)S(1)} fusion(bf16[1024,3072]{1,0:T(8,128)(2,1)} %all-gather.2.cloned.1.call-done, bf16[32,8,1024]{2,0,1:T(8,128)(2,1)S(1)} %pad_maximum_fusion), kind=kOutput, calls=%fused_computation.4 | convolution fusion | flops 536870912 | bytes 3670016 | tf_op jit(solution)/shard_map/dot_general | solution.py:319
  101.8 2.5 %fusion.14 = f32[256,1024]{1,0:T(8,128)S(1)} fusion(f32[256,1024]{1,0:T(8,128)S(1)} %fusion, f32[256,1024]{1,0:T(8,128)S(1)} %fusion.2, bf16[1024,3072]{1,0:T(8,128)(2,1)} %all-gather.2.cloned.1.call-done, bf16[32,8,1024]{2,0,1:T(8,128)(2,1)S(1)} %convolution_convert_fusion.1), kind=kOutput, calls=%fused_computation.15 | convolution fusion | flops 537395200 | bytes 5767168 | tf_op jit(solution)/shard_map/dot_general | solution.py:319
  104.4 1.0 fusion.20
  105.7 4.6 %convolution_bitcast_fusion = f32[32,8,3072]{2,1,0:T(8,128)S(1)} fusion(bf16[1024,3072]{1,0:T(8,128)(2,1)} %all-gather.2.cloned.1.call-done, bf16[256,512]{1,0:T(8,128)(2,1)S(1)} %get-tuple-element.67, bf16[256,512]{1,0:T(8,128)(2,1)S(1)} %get-tuple-element.66), kind=kOutput, calls=%fused_computation.1 | convolution fusion | flops 1611661312 | bytes 9961472 | tf_op jit(solution)/shard_map/dot_general | solution.py:351
  110.3 0.3 fusion.46
  110.6 0.6 copy.48
  111.6 1.0 fusion.18
  113.1 4.5 %convolution_convert_fusion = bf16[1024,3072]{1,0:T(8,128)(2,1)} fusion(bf16[256,1024]{0,1:T(8,128)(2,1)S(1)} %bitcast.52, bf16[256,1024]{1,0:T(8,128)(2,1)S(1)} %copy-done, bf16[256,1024]{1,0:T(8,128)(2,1)S(1)} %get-tuple-element.69, bf16[256,1024]{1,0:T(8,128)(2,1)S(1)} %get-tuple-element.70), kind=kOutput, calls=%fused_computation | convolution fusion | flops 1618477056 | bytes 8388608 | tf_op jit(solution)/shard_map/dot_general | solution.py:348
  117.6 90.3 %shard_map.72 = (f32[2,16,3072]{2,1,0:T(8,128)S(1)}, bf16[32,8,1024]{2,1,0:T(8,128)(2,1)S(1)}) custom-call(bf16[2,4,128,3072]{3,2,1,0:T(8,128)(2,1)} %bitcast.47, bf16[32,8,1024]{2,1,0:T(8,128)(2,1)S(1)} %copy.67.back_ref), custom_call_target="tpu_custom_call" | custom-call | tf_op jit(solution)/shard_map/pallas_call | solution.py:254
  207.9 1.3 fusion.17
  209.1 1.1 copy.68
  210.2 0.7 copy.71
  (17 shorter events, 1.3 us)
Async XLA Ops:
  7.2 31.6 %copy-start.2 = (s32[1,32]{1,0:T(1,128)S(1)}, s32[1,32]{1,0:T(1,128)}, u32[]{:S(2)}) copy-start(s32[1,32]{1,0:T(1,128)} %param.17) | copy-start | bytes 388
  7.2 31.3 %copy-start = (bf16[256,1024]{1,0:T(8,128)(2,1)S(1)}, bf16[256,1024]{1,0:T(8,128)(2,1)}, u32[]{:S(2)}) copy-start(bf16[256,1024]{1,0:T(8,128)(2,1)} %param.14) | copy-start | bytes 1572868
  7.2 89.9 %all-gather.2.cloned.1.call-start = ((), (), s32[]{:S(2)}) async-start(), calls=%async_computation.2 | async-start | bytes 6488064 | tf_op jit(solution)/shard_map/all_gather | solution.py:313
  32.7 24.0 %all-to-all-start.1 = ((bf16[32,8,1024]{2,1,0:T(8,128)(2,1)}), bf16[32,8,1024]{2,1,0:T(8,128)(2,1)S(1)}, u32[]{:S(2)}, u32[]{:S(2)}) async-start(bf16[32,8,1024]{2,1,0:T(8,128)(2,1)} %copy.28), calls=%async_computation.1 | async-start | bytes 1048576 | tf_op jit(solution)/shard_map/all_to_all | solution.py:308
  101.8 2.5 %copy-start.1 = (bf16[256,512]{1,0:T(8,128)(2,1)S(1)}, bf16[256,512]{1,0:T(8,128)(2,1)}, u32[]{:S(2)}) copy-start(bf16[256,512]{1,0:T(8,128)(2,1)} %param.15) | copy-start | bytes 786436
Sparse Core Ops, SparseCore 0:
  11.1 85.8 all-gather.1

commit v10 on v8

--- a/solution.py
+++ b/solution.py
@@ -319,16 +319,9 @@
     contract_final_axis = (((1,), (1,)), ((), ()))
     contract_first = (((0,), (0,)), ((), ()))
     windows = [extended[:, start : start + seg_rows, :].reshape(row_count, C) for start in starts]
-    preact = sum(
-        (
-            lax.dot_general(
-                windows[selected_index],
-                full_weight[:, selected_index * C : (selected_index + 1) * C],
-                contract_final_axis,
-                preferred_element_type=jnp.float32,
-            )
-            for selected_index in range(3)
-        )
+    stacked = jnp.concatenate(windows, axis=1)
+    preact = lax.dot_general(
+        stacked, full_weight, contract_final_axis, preferred_element_type=jnp.float32
     )
     filter_act = jnp.tanh(preact[:, :H])
     gate_act = jax.nn.sigmoid(preact[:, H:])
@@ -349,7 +342,6 @@
         .transpose(0, 3, 1, 2, 4)
         .reshape(row_count, 2 * H)
     )
-    stacked = jnp.concatenate(windows, axis=1)
     partial_value = lax.dot_general(
         routed, stacked, contract_first, preferred_element_type=jnp.float32
     ).astype(jnp.bfloat16)

time: 216 us -> 214 us (level)
  matrix products: 20.5 us -> 18.1 us
    dot_general x3 -> x1, matrix products: 7.28 us -> 4.77 us  [per_device(): lax.dot_general(stacked, full_weight, contract_final_axis, preferred_elem...]
where the time goes in v10:
time: 214 us; the launch traced here: 212 us
  Pallas kernels  86.8 us (41%)
  waiting for transfers between devices  57.5 us (27%)
  blocking collectives  21.1 us (10%)
  matrix products  18.1 us (8%)
  between operations  14.2 us (7%)
  starting transfers between devices  5.81 us (3%)
  local copies, waits for them, and re-layouts  5.66 us (3%)
  other arithmetic  2.8 us (1%)
    pallas_call x1, Pallas kernels, grad_reduce(): pl.pallas_call(functools.partial(grad_reduce_kernel, z_hi, scale), out_sh...  86.8 us
    all_gather x1, waiting for transfers between devices, per_device(): full_weight = lax.all_gather(conv_weight, 'fsdp', axis=0, tiled=True)  39 us
    all_to_all x1, blocking collectives, per_device(): lax.all_to_all(request_mask, 'fsdp', split_axis=0, concat_axis=0, tiled=T...  21.1 us
    all_to_all x1, waiting for transfers between devices, per_device(): lax.all_to_all(outgoing, 'fsdp', split_axis=0, concat_axis=0, tiled=True)  17.9 us
    all_to_all x1, starting transfers between devices, per_device(): lax.all_to_all(outgoing, 'fsdp', split_axis=0, concat_axis=0, tiled=True)  5.78 us
    dot_general x1, matrix products, per_device(): lax.dot_general(stacked, full_weight, contract_final_axis, preferred_elem...  4.77 us
    dot_general x1, matrix products, per_device(): jnp.dot(grad_pre, full_weight, preferred_element_type=jnp.float32)  4.68 us
    dot_general x1, matrix products, per_device(): lax.dot_general(routed, stacked, contract_first, preferred_element_type=j...  4.47 us
  transfers between devices with their start and end apart: 2, of which 2 were waited for; matrix products, arithmetic and copies ran while one was open for 2% of the time, Pallas kernels for 0%

profile of v10, /device:TPU:6, one launch (start us, length us, event | category | flops | bytes accessed | tf_op | source)
XLA Modules:
  0.0 212.0 jit_solution(1399391110570267445)
XLA Ops:
  7.2 0.7 all-gather.2.cloned.1.call-update
  7.9 0.7 fusion.26
  8.6 21.1 %all_to_all.11 = s32[32,1,32]{2,1,0:T(1,128)S(1)} all-to-all(s32[32,1,32]{2,1,0:T(1,128)S(1)} %compare_convert_fusion), channel_id=1, replica_groups=mesh['dp'=16,'fsdp'=32] {'fsdp'}, dimensions={0} | all-to-all | bytes 8192 | tf_op jit(solution)/shard_map/all_to_all | solution.py:307
  29.7 1.8 convolution_convert_fusion.2
  31.6 1.1 copy.28
  32.7 5.8 %all-to-all-start.1 = ((bf16[32,8,1024]{2,1,0:T(8,128)(2,1)}), bf16[32,8,1024]{2,1,0:T(8,128)(2,1)S(1)}, u32[]{:S(2)}, u32[]{:S(2)}) async-start(bf16[32,8,1024]{2,1,0:T(8,128)(2,1)} %copy.28), calls=%async_computation.1 | async-start | bytes 1048576 | tf_op jit(solution)/shard_map/all_to_all | solution.py:313
  38.4 0.3 copy.27
  38.8 17.9 %all-to-all-done.1 = bf16[32,8,1024]{2,1,0:T(8,128)(2,1)S(1)} async-done(((bf16[32,8,1024]{2,1,0:T(8,128)(2,1)}), bf16[32,8,1024]{2,1,0:T(8,128)(2,1)S(1)}, u32[]{:S(2)}, u32[]{:S(2)}) %all-to-all-start.1) | async-done | bytes 524320 | tf_op jit(solution)/shard_map/all_to_all | solution.py:313
  56.7 0.8 convolution_convert_fusion.1
  57.5 0.6 copy_bitcast_fusion.1
  58.1 39.0 %all-gather.2.cloned.1.call-done = bf16[1024,3072]{1,0:T(8,128)(2,1)} async-done(((bf16[32,3072]{1,0:T(8,128)(2,1)}), bf16[1024,3072]{1,0:T(8,128)(2,1)}) %all-gather.2.cloned.1.call-update) | async-done | bytes 6291472 | tf_op jit(solution)/shard_map/all_gather | solution.py:318
  97.0 4.8 %fusion.2 = f32[256,1024]{1,0:T(8,128)S(1)} fusion(bf16[1024,3072]{1,0:T(8,128)(2,1)} %all-gather.2.cloned.1.call-done, bf16[256,1024]{1,0:T(8,128)(2,1)S(1)} %copy-done, bf16[256,1024]{1,0:T(8,128)(2,1)S(1)} %get-tuple-element.69, bf16[256,1024]{1,0:T(8,128)(2,1)S(1)} %get-tuple-element.70), kind=kOutput, calls=%fused_computation.14 | convolution fusion | flops 1615331328 | bytes 8912896 | tf_op jit(solution)/shard_map/dot_general | solution.py:323
  101.8 1.0 fusion.4
  103.1 4.7 %convolution_bitcast_fusion = f32[32,8,3072]{2,1,0:T(8,128)S(1)} fusion(bf16[1024,3072]{1,0:T(8,128)(2,1)} %all-gather.2.cloned.1.call-done, bf16[256,512]{1,0:T(8,128)(2,1)S(1)} %get-tuple-element.67, bf16[256,512]{1,0:T(8,128)(2,1)S(1)} %get-tuple-element.66), kind=kOutput, calls=%fused_computation.1 | convolution fusion | flops 1611661312 | bytes 9961472 | tf_op jit(solution)/shard_map/dot_general | solution.py:348
  107.8 0.4 fusion.31
  108.2 0.6 copy.48
  109.0 4.5 %convolution_convert_fusion = bf16[1024,3072]{1,0:T(8,128)(2,1)} fusion(bf16[256,1024]{0,1:T(8,128)(2,1)S(1)} %bitcast.51, bf16[256,1024]{1,0:T(8,128)(2,1)S(1)} %copy-done, bf16[256,1024]{1,0:T(8,128)(2,1)S(1)} %get-tuple-element.69, bf16[256,1024]{1,0:T(8,128)(2,1)S(1)} %get-tuple-element.70), kind=kOutput, calls=%fused_computation | convolution fusion | flops 1618477056 | bytes 8388608 | tf_op jit(solution)/shard_map/dot_general | solution.py:345
  113.7 1.0 fusion.1
  114.6 0.3 fusion.8
  114.9 0.3 copy.65.back_ref
  115.2 86.8 %shard_map.72 = (f32[2,16,3072]{2,1,0:T(8,128)S(1)}, bf16[32,8,1024]{2,1,0:T(8,128)(2,1)S(1)}) custom-call(bf16[2,4,128,3072]{3,2,1,0:T(8,128)(2,1)} %bitcast.45, bf16[32,8,1024]{2,1,0:T(8,128)(2,1)S(1)} %copy.65.back_ref), custom_call_target="tpu_custom_call" | custom-call | tf_op jit(solution)/shard_map/pallas_call | solution.py:259
  202.0 1.3 fusion
  203.3 1.1 copy.66
  204.4 0.7 copy.69
  (15 shorter events, 0.7 us)
Async XLA Ops:
  7.2 31.6 %copy-start.2 = (s32[1,32]{1,0:T(1,128)S(1)}, s32[1,32]{1,0:T(1,128)}, u32[]{:S(2)}) copy-start(s32[1,32]{1,0:T(1,128)} %param.17) | copy-start | bytes 388
  7.2 31.3 %copy-start = (bf16[256,1024]{1,0:T(8,128)(2,1)S(1)}, bf16[256,1024]{1,0:T(8,128)(2,1)}, u32[]{:S(2)}) copy-start(bf16[256,1024]{1,0:T(8,128)(2,1)} %param.14) | copy-start | bytes 1572868
  7.2 89.9 %all-gather.2.cloned.1.call-start = ((), (), s32[]{:S(2)}) async-start(), calls=%async_computation.2 | async-start | bytes 6488064 | tf_op jit(solution)/shard_map/all_gather | solution.py:318
  32.7 24.0 %all-to-all-start.1 = ((bf16[32,8,1024]{2,1,0:T(8,128)(2,1)}), bf16[32,8,1024]{2,1,0:T(8,128)(2,1)S(1)}, u32[]{:S(2)}, u32[]{:S(2)}) async-start(bf16[32,8,1024]{2,1,0:T(8,128)(2,1)} %copy.28), calls=%async_computation.1 | async-start | bytes 1048576 | tf_op jit(solution)/shard_map/all_to_all | solution.py:313
  97.0 4.8 %copy-start.1 = (bf16[256,512]{1,0:T(8,128)(2,1)S(1)}, bf16[256,512]{1,0:T(8,128)(2,1)}, u32[]{:S(2)}) copy-start(bf16[256,512]{1,0:T(8,128)(2,1)} %param.15) | copy-start | bytes 786436
Sparse Core Ops, SparseCore 0:
  11.1 85.8 all-gather.1

commit v11 on v10

--- a/solution.py
+++ b/solution.py
@@ -166,28 +166,32 @@
     back_pending = start_exchange(lambda p: back_ref.at[p], lambda p: back_out.at[p], back_sems.at[0],
                                   back_sems.at[1], f_peers, f, lambda p: {"dp": d, "fsdp": p})
     back_out[f] = back_ref[f]
-    core_copy = pltpu.make_async_remote_copy(
-        src_ref=p_ref.at[1 - c], dst_ref=recv_c, send_sem=core_sems.at[0],
-        recv_sem=core_sems.at[1], device_id=partner, device_id_type=MESH)
-    core_copy.start()
-    core_copy.wait()
-
     rows = 32
     chunks = band // rows
 
-    def round_two_sums(i, carry):
-        xi, r = i // chunks, lax.rem(i, chunks)
-        at = pl.ds(pl.multiple_of(r * rows, rows), rows)
-        both = p_ref[c, xi, at, :].astype(jnp.float32) + recv_c[xi, at, :].astype(jnp.float32)
-        s1b[xi, at, :] = both.astype(s1b.dtype)
-        return carry
-
-    lax.fori_loop(0, n_x * chunks, round_two_sums, 0)
     pieces = x_send.shape[0]
     span = s1b.shape[2] // pieces
 
     def piece(k):
         return pl.ds(k * span, span)
+
+    def core_stage(k):
+        copy = pltpu.make_async_remote_copy(
+            src_ref=p_ref.at[1 - c, :, :, piece(k)], dst_ref=recv_c.at[:, :, piece(k)],
+            send_sem=core_sems.at[0, k], recv_sem=core_sems.at[1, k], device_id=partner,
+            device_id_type=MESH)
+        copy.start()
+        return copy
+
+    def round_two_sums(k):
+        def body(i, carry):
+            xi, r = i // chunks, lax.rem(i, chunks)
+            at = pl.ds(pl.multiple_of(r * rows, rows), rows)
+            both = (p_ref[c, xi, at, piece(k)].astype(jnp.float32)
+                    + recv_c[xi, at, piece(k)].astype(jnp.float32))
+            s1b[xi, at, piece(k)] = both.astype(s1b.dtype)
+            return carry
+        lax.fori_loop(0, n_x * chunks, body, 0)
 
     def x_stage(k):
         return start_exchange(lambda p: s1b.at[p, :, piece(k)], lambda p: recv_x.at[p, :, piece(k)],
@@ -210,14 +214,24 @@
             return carry
         lax.fori_loop(0, n_z, body, 0)
 
+    core_copy = core_stage(0)
+    core_copy.wait()
+    round_two_sums(0)
     x_pending = x_stage(0)
+    if pieces > 1:
+        core_copy = core_stage(1)
     z_pending = []
     for k in range(pieces):
+        if k + 1 < pieces:
+            core_copy.wait()
+            round_two_sums(k + 1)
         finish_exchange(x_pending)
         sum_x(k)
         z_pending.append(z_stage(k))
         if k + 1 < pieces:
             x_pending = x_stage(k + 1)
+            if k + 2 < pieces:
+                core_copy = core_stage(k + 2)
     for pending in z_pending:
         finish_exchange(pending)
     total = own[z]
@@ -271,7 +285,7 @@
             pltpu.VMEM((half, cols), f32),
             pltpu.VMEM((n_y, half, cols // n_y), f32),
             pltpu.VMEM((half, cols), f32),
-            pltpu.SemaphoreType.DMA((2,)),
+            pltpu.SemaphoreType.DMA((2, PIECES)),
             pltpu.SemaphoreType.DMA((PIECES, n_x)),
             pltpu.SemaphoreType.DMA((PIECES, n_x)),
             pltpu.SemaphoreType.DMA((PIECES, 2 * z_hi)),

time: 214 us -> 213 us (level)
  no operation moved by 1% of the time
where the time goes in v11:
time: 213 us
  Pallas kernels  87.5 us (41%)
  waiting for transfers between devices  57.5 us (27%)
  blocking collectives  21.1 us (10%)
  matrix products  18.1 us (8%)
  between operations  14.2 us (7%)
  starting transfers between devices  5.81 us (3%)
  local copies, waits for them, and re-layouts  5.66 us (3%)
  other arithmetic  2.8 us (1%)
    pallas_call x1, Pallas kernels, grad_reduce(): pl.pallas_call(functools.partial(grad_reduce_kernel, z_hi, scale), out_sh...  87.5 us
    all_gather x1, waiting for transfers between devices, per_device(): full_weight = lax.all_gather(conv_weight, 'fsdp', axis=0, tiled=True)  39 us
    all_to_all x1, blocking collectives, per_device(): lax.all_to_all(request_mask, 'fsdp', split_axis=0, concat_axis=0, tiled=T...  21.1 us
    all_to_all x1, waiting for transfers between devices, per_device(): lax.all_to_all(outgoing, 'fsdp', split_axis=0, concat_axis=0, tiled=True)  17.9 us
    all_to_all x1, starting transfers between devices, per_device(): lax.all_to_all(outgoing, 'fsdp', split_axis=0, concat_axis=0, tiled=True)  5.78 us
    dot_general x1, matrix products, per_device(): lax.dot_general(stacked, full_weight, contract_final_axis, preferred_elem...  4.77 us
    dot_general x1, matrix products, per_device(): jnp.dot(grad_pre, full_weight, preferred_element_type=jnp.float32)  4.68 us
    dot_general x1, matrix products, per_device(): lax.dot_general(routed, stacked, contract_first, preferred_element_type=j...  4.47 us
  transfers between devices with their start and end apart: 2, of which 2 were waited for; matrix products, arithmetic and copies ran while one was open for 2% of the time, Pallas kernels for 0%

profile of v11, /device:TPU:6, one launch (start us, length us, event | category | flops | bytes accessed | tf_op | source)
XLA Modules:
  0.0 212.7 jit_solution(4207473043415433418)
XLA Ops:
  7.2 0.7 all-gather.2.cloned.1.call-update
  7.9 0.7 fusion.26
  8.6 21.1 %all_to_all.11 = s32[32,1,32]{2,1,0:T(1,128)S(1)} all-to-all(s32[32,1,32]{2,1,0:T(1,128)S(1)} %compare_convert_fusion), channel_id=1, replica_groups=mesh['dp'=16,'fsdp'=32] {'fsdp'}, dimensions={0} | all-to-all | bytes 8192 | tf_op jit(solution)/shard_map/all_to_all | solution.py:321
  29.7 1.8 convolution_convert_fusion.2
  31.6 1.1 copy.28
  32.7 5.8 %all-to-all-start.1 = ((bf16[32,8,1024]{2,1,0:T(8,128)(2,1)}), bf16[32,8,1024]{2,1,0:T(8,128)(2,1)S(1)}, u32[]{:S(2)}, u32[]{:S(2)}) async-start(bf16[32,8,1024]{2,1,0:T(8,128)(2,1)} %copy.28), calls=%async_computation.1 | async-start | bytes 1048576 | tf_op jit(solution)/shard_map/all_to_all | solution.py:327
  38.4 0.3 copy.27
  38.8 17.9 %all-to-all-done.1 = bf16[32,8,1024]{2,1,0:T(8,128)(2,1)S(1)} async-done(((bf16[32,8,1024]{2,1,0:T(8,128)(2,1)}), bf16[32,8,1024]{2,1,0:T(8,128)(2,1)S(1)}, u32[]{:S(2)}, u32[]{:S(2)}) %all-to-all-start.1) | async-done | bytes 524320 | tf_op jit(solution)/shard_map/all_to_all | solution.py:327
  56.7 0.8 convolution_convert_fusion.1
  57.5 0.6 copy_bitcast_fusion.1
  58.1 39.0 %all-gather.2.cloned.1.call-done = bf16[1024,3072]{1,0:T(8,128)(2,1)} async-done(((bf16[32,3072]{1,0:T(8,128)(2,1)}), bf16[1024,3072]{1,0:T(8,128)(2,1)}) %all-gather.2.cloned.1.call-update) | async-done | bytes 6291472 | tf_op jit(solution)/shard_map/all_gather | solution.py:332
  97.0 4.8 %fusion.2 = f32[256,1024]{1,0:T(8,128)S(1)} fusion(bf16[1024,3072]{1,0:T(8,128)(2,1)} %all-gather.2.cloned.1.call-done, bf16[256,1024]{1,0:T(8,128)(2,1)S(1)} %copy-done, bf16[256,1024]{1,0:T(8,128)(2,1)S(1)} %get-tuple-element.69, bf16[256,1024]{1,0:T(8,128)(2,1)S(1)} %get-tuple-element.70), kind=kOutput, calls=%fused_computation.14 | convolution fusion | flops 1615331328 | bytes 8912896 | tf_op jit(solution)/shard_map/dot_general | solution.py:337
  101.8 1.0 fusion.4
  103.1 4.7 %convolution_bitcast_fusion = f32[32,8,3072]{2,1,0:T(8,128)S(1)} fusion(bf16[1024,3072]{1,0:T(8,128)(2,1)} %all-gather.2.cloned.1.call-done, bf16[256,512]{1,0:T(8,128)(2,1)S(1)} %get-tuple-element.67, bf16[256,512]{1,0:T(8,128)(2,1)S(1)} %get-tuple-element.66), kind=kOutput, calls=%fused_computation.1 | convolution fusion | flops 1611661312 | bytes 9961472 | tf_op jit(solution)/shard_map/dot_general | solution.py:362
  107.8 0.4 fusion.31
  108.2 0.6 copy.48
  109.0 4.5 %convolution_convert_fusion = bf16[1024,3072]{1,0:T(8,128)(2,1)} fusion(bf16[256,1024]{0,1:T(8,128)(2,1)S(1)} %bitcast.51, bf16[256,1024]{1,0:T(8,128)(2,1)S(1)} %copy-done, bf16[256,1024]{1,0:T(8,128)(2,1)S(1)} %get-tuple-element.69, bf16[256,1024]{1,0:T(8,128)(2,1)S(1)} %get-tuple-element.70), kind=kOutput, calls=%fused_computation | convolution fusion | flops 1618477056 | bytes 8388608 | tf_op jit(solution)/shard_map/dot_general | solution.py:359
  113.7 1.0 fusion.1
  114.6 0.3 fusion.8
  114.9 0.3 copy.65.back_ref
  115.2 87.5 %shard_map.72 = (f32[2,16,3072]{2,1,0:T(8,128)S(1)}, bf16[32,8,1024]{2,1,0:T(8,128)(2,1)S(1)}) custom-call(bf16[2,4,128,3072]{3,2,1,0:T(8,128)(2,1)} %bitcast.45, bf16[32,8,1024]{2,1,0:T(8,128)(2,1)S(1)} %copy.65.back_ref), custom_call_target="tpu_custom_call" | custom-call | tf_op jit(solution)/shard_map/pallas_call | solution.py:273
  202.8 1.3 fusion
  204.0 1.1 copy.66
  205.1 0.7 copy.69
  (15 shorter events, 0.7 us)
Async XLA Ops:
  7.2 31.6 %copy-start.2 = (s32[1,32]{1,0:T(1,128)S(1)}, s32[1,32]{1,0:T(1,128)}, u32[]{:S(2)}) copy-start(s32[1,32]{1,0:T(1,128)} %param.17) | copy-start | bytes 388
  7.2 31.3 %copy-start = (bf16[256,1024]{1,0:T(8,128)(2,1)S(1)}, bf16[256,1024]{1,0:T(8,128)(2,1)}, u32[]{:S(2)}) copy-start(bf16[256,1024]{1,0:T(8,128)(2,1)} %param.14) | copy-start | bytes 1572868
  7.2 89.9 %all-gather.2.cloned.1.call-start = ((), (), s32[]{:S(2)}) async-start(), calls=%async_computation.2 | async-start | bytes 6488064 | tf_op jit(solution)/shard_map/all_gather | solution.py:332
  32.7 24.0 %all-to-all-start.1 = ((bf16[32,8,1024]{2,1,0:T(8,128)(2,1)}), bf16[32,8,1024]{2,1,0:T(8,128)(2,1)S(1)}, u32[]{:S(2)}, u32[]{:S(2)}) async-start(bf16[32,8,1024]{2,1,0:T(8,128)(2,1)} %copy.28), calls=%async_computation.1 | async-start | bytes 1048576 | tf_op jit(solution)/shard_map/all_to_all | solution.py:327
  97.0 4.8 %copy-start.1 = (bf16[256,512]{1,0:T(8,128)(2,1)S(1)}, bf16[256,512]{1,0:T(8,128)(2,1)}, u32[]{:S(2)}) copy-start(bf16[256,512]{1,0:T(8,128)(2,1)} %param.15) | copy-start | bytes 786436
Sparse Core Ops, SparseCore 0:
  11.1 85.8 all-gather.1

commit v12 on v11

--- a/solution.py
+++ b/solution.py
@@ -232,18 +232,32 @@
             x_pending = x_stage(k + 1)
             if k + 2 < pieces:
                 core_copy = core_stage(k + 2)
-    for pending in z_pending:
-        finish_exchange(pending)
-    total = own[z]
-    for p in z_peers:
-        total = total + recv_z[p].astype(jnp.float32)
-    s3[...] = total
-
     def cols(p):
         return pl.ds(pl.multiple_of(p * width, 128), width)
 
-    exchange(lambda p: s3.at[:, cols(p)], lambda p: recv_y.at[p], y_send, y_recv, y_peers, y,
-             lambda p: device(x, zh, c, p, zl))
+    per_piece = span // width
+    for k in range(pieces):
+        finish_exchange(z_pending[k])
+        total = own[z, :, piece(k)]
+        for p in z_peers:
+            total = total + recv_z[p, :, piece(k)].astype(jnp.float32)
+        s3[:, piece(k)] = total
+        for b in range(k * per_piece, (k + 1) * per_piece):
+            @pl.when(b != y)
+            def _():
+                pltpu.make_async_remote_copy(
+                    src_ref=s3.at[:, pl.ds(b * width, width)], dst_ref=recv_y.at[y], send_sem=y_send.at[b],
+                    recv_sem=y_recv.at[y], device_id=device(x, zh, c, b, zl), device_id_type=MESH).start()
+    for p in y_peers:
+        pltpu.make_async_remote_copy(
+            src_ref=s3.at[:, cols(p)], dst_ref=recv_y.at[p], send_sem=y_send.at[p],
+            recv_sem=y_recv.at[p], device_id=device(x, zh, c, p, zl), device_id_type=MESH).wait_recv()
+    for b in range(n_y):
+        @pl.when(b != y)
+        def _():
+            pltpu.make_async_remote_copy(
+                src_ref=s3.at[:, pl.ds(b * width, width)], dst_ref=recv_y.at[y], send_sem=y_send.at[b],
+                recv_sem=y_recv.at[y], device_id=device(x, zh, c, b, zl), device_id_type=MESH).wait_send()
     total = s3[:, cols(y)]
     for p in y_peers:
         total = total + recv_y[p]

time: 213 us -> 212 us (level)
  transfers between devices with their start and end apart: 2 -> 2, of which waited for: 2 -> 2; matrix products, arithmetic and copies ran while one was open for 2% -> 3% of each run, Pallas kernels for 0% -> 0%
where the time goes in v12:
time: 212 us
  Pallas kernels  86.5 us (41%)
  waiting for transfers between devices  57.5 us (27%)
  blocking collectives  21.1 us (10%)
  matrix products  18.1 us (9%)
  between operations  14.2 us (7%)
  starting transfers between devices  5.81 us (3%)
  local copies, waits for them, and re-layouts  5.66 us (3%)
  other arithmetic  2.8 us (1%)
    pallas_call x1, Pallas kernels, grad_reduce(): pl.pallas_call(functools.partial(grad_reduce_kernel, z_hi, scale), out_sh...  86.5 us
    all_gather x1, waiting for transfers between devices, per_device(): full_weight = lax.all_gather(conv_weight, 'fsdp', axis=0, tiled=True)  39 us
    all_to_all x1, blocking collectives, per_device(): lax.all_to_all(request_mask, 'fsdp', split_axis=0, concat_axis=0, tiled=T...  21.1 us
    all_to_all x1, waiting for transfers between devices, per_device(): lax.all_to_all(outgoing, 'fsdp', split_axis=0, concat_axis=0, tiled=True)  17.9 us
    all_to_all x1, starting transfers between devices, per_device(): lax.all_to_all(outgoing, 'fsdp', split_axis=0, concat_axis=0, tiled=True)  5.78 us
    dot_general x1, matrix products, per_device(): lax.dot_general(stacked, full_weight, contract_final_axis, preferred_elem...  4.77 us
    dot_general x1, matrix products, per_device(): jnp.dot(grad_pre, full_weight, preferred_element_type=jnp.float32)  4.68 us
    dot_general x1, matrix products, per_device(): lax.dot_general(routed, stacked, contract_first, preferred_element_type=j...  4.47 us
  transfers between devices with their start and end apart: 2, of which 2 were waited for; matrix products, arithmetic and copies ran while one was open for 3% of the time, Pallas kernels for 0%

profile of v12, /device:TPU:6, one launch (start us, length us, event | category | flops | bytes accessed | tf_op | source)
XLA Modules:
  0.0 211.7 jit_solution(2953543169746008120)
XLA Ops:
  7.2 0.7 all-gather.2.cloned.1.call-update
  7.9 0.7 fusion.26
  8.6 21.1 %all_to_all.11 = s32[32,1,32]{2,1,0:T(1,128)S(1)} all-to-all(s32[32,1,32]{2,1,0:T(1,128)S(1)} %compare_convert_fusion), channel_id=1, replica_groups=mesh['dp'=16,'fsdp'=32] {'fsdp'}, dimensions={0} | all-to-all | bytes 8192 | tf_op jit(solution)/shard_map/all_to_all | solution.py:335
  29.7 1.8 convolution_convert_fusion.2
  31.6 1.1 copy.28
  32.7 5.8 %all-to-all-start.1 = ((bf16[32,8,1024]{2,1,0:T(8,128)(2,1)}), bf16[32,8,1024]{2,1,0:T(8,128)(2,1)S(1)}, u32[]{:S(2)}, u32[]{:S(2)}) async-start(bf16[32,8,1024]{2,1,0:T(8,128)(2,1)} %copy.28), calls=%async_computation.1 | async-start | bytes 1048576 | tf_op jit(solution)/shard_map/all_to_all | solution.py:341
  38.4 0.3 copy.27
  38.8 17.9 %all-to-all-done.1 = bf16[32,8,1024]{2,1,0:T(8,128)(2,1)S(1)} async-done(((bf16[32,8,1024]{2,1,0:T(8,128)(2,1)}), bf16[32,8,1024]{2,1,0:T(8,128)(2,1)S(1)}, u32[]{:S(2)}, u32[]{:S(2)}) %all-to-all-start.1) | async-done | bytes 524320 | tf_op jit(solution)/shard_map/all_to_all | solution.py:341
  56.7 0.8 convolution_convert_fusion.1
  57.5 0.6 copy_bitcast_fusion.1
  58.1 39.0 %all-gather.2.cloned.1.call-done = bf16[1024,3072]{1,0:T(8,128)(2,1)} async-done(((bf16[32,3072]{1,0:T(8,128)(2,1)}), bf16[1024,3072]{1,0:T(8,128)(2,1)}) %all-gather.2.cloned.1.call-update) | async-done | bytes 6291472 | tf_op jit(solution)/shard_map/all_gather | solution.py:346
  97.0 4.8 %fusion.2 = f32[256,1024]{1,0:T(8,128)S(1)} fusion(bf16[1024,3072]{1,0:T(8,128)(2,1)} %all-gather.2.cloned.1.call-done, bf16[256,1024]{1,0:T(8,128)(2,1)S(1)} %copy-done, bf16[256,1024]{1,0:T(8,128)(2,1)S(1)} %get-tuple-element.69, bf16[256,1024]{1,0:T(8,128)(2,1)S(1)} %get-tuple-element.70), kind=kOutput, calls=%fused_computation.14 | convolution fusion | flops 1615331328 | bytes 8912896 | tf_op jit(solution)/shard_map/dot_general | solution.py:351
  101.8 1.0 fusion.4
  103.1 4.7 %convolution_bitcast_fusion = f32[32,8,3072]{2,1,0:T(8,128)S(1)} fusion(bf16[1024,3072]{1,0:T(8,128)(2,1)} %all-gather.2.cloned.1.call-done, bf16[256,512]{1,0:T(8,128)(2,1)S(1)} %get-tuple-element.67, bf16[256,512]{1,0:T(8,128)(2,1)S(1)} %get-tuple-element.66), kind=kOutput, calls=%fused_computation.1 | convolution fusion | flops 1611661312 | bytes 9961472 | tf_op jit(solution)/shard_map/dot_general | solution.py:376
  107.8 0.4 fusion.31
  108.2 0.6 copy.48
  109.0 4.5 %convolution_convert_fusion = bf16[1024,3072]{1,0:T(8,128)(2,1)} fusion(bf16[256,1024]{0,1:T(8,128)(2,1)S(1)} %bitcast.51, bf16[256,1024]{1,0:T(8,128)(2,1)S(1)} %copy-done, bf16[256,1024]{1,0:T(8,128)(2,1)S(1)} %get-tuple-element.69, bf16[256,1024]{1,0:T(8,128)(2,1)S(1)} %get-tuple-element.70), kind=kOutput, calls=%fused_computation | convolution fusion | flops 1618477056 | bytes 8388608 | tf_op jit(solution)/shard_map/dot_general | solution.py:373
  113.7 1.0 fusion.1
  114.6 0.3 fusion.8
  114.9 0.3 copy.65.back_ref
  115.2 86.5 %shard_map.72 = (f32[2,16,3072]{2,1,0:T(8,128)S(1)}, bf16[32,8,1024]{2,1,0:T(8,128)(2,1)S(1)}) custom-call(bf16[2,4,128,3072]{3,2,1,0:T(8,128)(2,1)} %bitcast.45, bf16[32,8,1024]{2,1,0:T(8,128)(2,1)S(1)} %copy.65.back_ref), custom_call_target="tpu_custom_call" | custom-call | tf_op jit(solution)/shard_map/pallas_call | solution.py:287
  201.7 1.3 fusion
  203.0 1.1 copy.66
  204.1 0.7 copy.69
  (15 shorter events, 0.7 us)
Async XLA Ops:
  7.2 31.6 %copy-start.2 = (s32[1,32]{1,0:T(1,128)S(1)}, s32[1,32]{1,0:T(1,128)}, u32[]{:S(2)}) copy-start(s32[1,32]{1,0:T(1,128)} %param.17) | copy-start | bytes 388
  7.2 31.3 %copy-start = (bf16[256,1024]{1,0:T(8,128)(2,1)S(1)}, bf16[256,1024]{1,0:T(8,128)(2,1)}, u32[]{:S(2)}) copy-start(bf16[256,1024]{1,0:T(8,128)(2,1)} %param.14) | copy-start | bytes 1572868
  7.2 89.9 %all-gather.2.cloned.1.call-start = ((), (), s32[]{:S(2)}) async-start(), calls=%async_computation.2 | async-start | bytes 6488064 | tf_op jit(solution)/shard_map/all_gather | solution.py:346
  32.7 24.0 %all-to-all-start.1 = ((bf16[32,8,1024]{2,1,0:T(8,128)(2,1)}), bf16[32,8,1024]{2,1,0:T(8,128)(2,1)S(1)}, u32[]{:S(2)}, u32[]{:S(2)}) async-start(bf16[32,8,1024]{2,1,0:T(8,128)(2,1)} %copy.28), calls=%async_computation.1 | async-start | bytes 1048576 | tf_op jit(solution)/shard_map/all_to_all | solution.py:341
  97.0 4.8 %copy-start.1 = (bf16[256,512]{1,0:T(8,128)(2,1)S(1)}, bf16[256,512]{1,0:T(8,128)(2,1)}, u32[]{:S(2)}) copy-start(bf16[256,512]{1,0:T(8,128)(2,1)} %param.15) | copy-start | bytes 786436
Sparse Core Ops, SparseCore 0:
  11.1 85.8 all-gather.1

commit v13 on v12

--- a/solution.py
+++ b/solution.py
@@ -343,13 +343,24 @@
         "sn,nlc->slc", recv_table, incoming, preferred_element_type=jnp.float32
     ).astype(jnp.bfloat16)
     extended = jnp.concatenate([carries, segments], axis=1)
-    full_weight = lax.all_gather(conv_weight, "fsdp", axis=0, tiled=True)
+    half_cols = conv_weight.shape[1] // 2
+    weight_halves = [
+        lax.all_gather(conv_weight[:, :half_cols], "fsdp", axis=0, tiled=True),
+        lax.all_gather(conv_weight[:, half_cols:], "fsdp", axis=0, tiled=True),
+    ]
+    full_weight = jnp.concatenate(weight_halves, axis=1)
     contract_final_axis = (((1,), (1,)), ((), ()))
     contract_first = (((0,), (0,)), ((), ()))
     windows = [extended[:, start : start + seg_rows, :].reshape(row_count, C) for start in starts]
     stacked = jnp.concatenate(windows, axis=1)
-    preact = lax.dot_general(
-        stacked, full_weight, contract_final_axis, preferred_element_type=jnp.float32
+    preact = sum(
+        lax.dot_general(
+            stacked[:, k * half_cols : (k + 1) * half_cols],
+            weight_halves[k],
+            contract_final_axis,
+            preferred_element_type=jnp.float32,
+        )
+        for k in range(2)
     )
     filter_act = jnp.tanh(preact[:, :H])
     gate_act = jax.nn.sigmoid(preact[:, H:])

time: 212 us -> 264 us (1.25)
  waiting for transfers between devices: 57.5 us -> 105 us
    all_gather x1 -> x2, waiting for transfers between devices: 39 us -> 88.6 us  [the longest x1 61.3 us: per_device(): lax.all_gather(conv_weight[:, half_cols:], 'fsdp', axis=0, tiled=True)]
    all_to_all x1, waiting for transfers between devices: 17.9 us -> 15.2 us  [per_device(): lax.all_to_all(outgoing, 'fsdp', split_axis=0, concat_axis=0, tiled=True)]
    dot_general x1 -> x2, matrix products: 4.77 us -> 5.85 us  [per_device(): lax.dot_general(stacked[:, k * half_cols:(k + 1) * half_cols], weight_hal...]
  transfers between devices with their start and end apart: 2 -> 3, of which waited for: 2 -> 3; matrix products, arithmetic and copies ran while one was open for 3% -> 3% of each run, Pallas kernels for 0% -> 0%
where the time goes in v13:
time: 264 us; the launch traced here: 262 us
  waiting for transfers between devices  105 us (40%)
  Pallas kernels  86.8 us (33%)
  blocking collectives  21.1 us (8%)
  matrix products  19.2 us (7%)
  between operations  14.2 us (5%)
  local copies, waits for them, and re-layouts  7.34 us (3%)
  starting transfers between devices  5.86 us (2%)
  other arithmetic  2.78 us (1%)
    pallas_call x1, Pallas kernels, grad_reduce(): pl.pallas_call(functools.partial(grad_reduce_kernel, z_hi, scale), out_sh...  86.8 us
    all_gather x1, waiting for transfers between devices, per_device(): lax.all_gather(conv_weight[:, half_cols:], 'fsdp', axis=0, tiled=True)  61.3 us
    all_gather x1, waiting for transfers between devices, per_device(): lax.all_gather(conv_weight[:, :half_cols], 'fsdp', axis=0, tiled=True)  27.4 us
    all_to_all x1, blocking collectives, per_device(): lax.all_to_all(request_mask, 'fsdp', split_axis=0, concat_axis=0, tiled=T...  21.1 us
    all_to_all x1, waiting for transfers between devices, per_device(): lax.all_to_all(outgoing, 'fsdp', split_axis=0, concat_axis=0, tiled=True)  15.2 us
    dot_general x2, matrix products, per_device(): lax.dot_general(stacked[:, k * half_cols:(k + 1) * half_cols], weight_hal...  5.85 us
    all_to_all x1, starting transfers between devices, per_device(): lax.all_to_all(outgoing, 'fsdp', split_axis=0, concat_axis=0, tiled=True)  5.78 us
  transfers between devices with their start and end apart: 3, of which 3 were waited for; matrix products, arithmetic and copies ran while one was open for 3% of the time, Pallas kernels for 0%

profile of v13, /device:TPU:6, one launch (start us, length us, event | category | flops | bytes accessed | tf_op | source)
XLA Modules:
  0.0 261.9 jit_solution(14317005083554801522)
XLA Ops:
  7.2 1.7 fusion.47
  9.0 0.7 all-gather.5.cloned.1.call-update
  9.7 0.7 fusion.40
  10.4 21.1 %all_to_all.11 = s32[32,1,32]{2,1,0:T(1,128)S(1)} all-to-all(s32[32,1,32]{2,1,0:T(1,128)S(1)} %compare_convert_fusion), channel_id=1, replica_groups=mesh['dp'=16,'fsdp'=32] {'fsdp'}, dimensions={0} | all-to-all | bytes 8192 | tf_op jit(solution)/shard_map/all_to_all | solution.py:335
  31.5 1.8 convolution_convert_fusion.2
  33.3 1.1 copy.28
  34.4 5.8 %all-to-all-start.1 = ((bf16[32,8,1024]{2,1,0:T(8,128)(2,1)}), bf16[32,8,1024]{2,1,0:T(8,128)(2,1)S(1)}, u32[]{:S(2)}, u32[]{:S(2)}) async-start(bf16[32,8,1024]{2,1,0:T(8,128)(2,1)} %copy.28), calls=%async_computation.1 | async-start | bytes 1048576 | tf_op jit(solution)/shard_map/all_to_all | solution.py:341
  40.5 15.2 %all-to-all-done.1 = bf16[32,8,1024]{2,1,0:T(8,128)(2,1)S(1)} async-done(((bf16[32,8,1024]{2,1,0:T(8,128)(2,1)}), bf16[32,8,1024]{2,1,0:T(8,128)(2,1)S(1)}, u32[]{:S(2)}, u32[]{:S(2)}) %all-to-all-start.1) | async-done | bytes 524320 | tf_op jit(solution)/shard_map/all_to_all | solution.py:341
  55.7 0.8 convolution_convert_fusion.1
  56.5 0.6 copy_bitcast_fusion.1
  57.1 27.4 %all-gather.3.cloned.1.call-done = bf16[1024,1536]{1,0:T(8,128)(2,1)} async-done(((bf16[32,1536]{1,0:T(8,128)(2,1)}), bf16[1024,1536]{1,0:T(8,128)(2,1)}) %all-gather.3.cloned.1.call-update) | async-done | bytes 3145744 | tf_op jit(solution)/shard_map/all_gather | solution.py:348
  84.5 2.9 %fusion.15 = f32[256,1024]{1,0:T(8,128)S(1)} fusion(bf16[1024,1536]{1,0:T(8,128)(2,1)} %all-gather.3.cloned.1.call-done, bf16[256,1024]{1,0:T(8,128)(2,1)S(1)} %get-tuple-element.71, bf16[256,1024]{1,0:T(8,128)(2,1)S(1)} %get-tuple-element.72), kind=kOutput, calls=%fused_computation.24 | convolution fusion | flops 806879232 | bytes 5242880 | tf_op jit(solution)/shard_map/dot_general | solution.py:357
  87.4 61.3 %all-gather.5.cloned.1.call-done = bf16[1024,1536]{1,0:T(8,128)(2,1)} async-done(((bf16[32,1536]{1,0:T(8,128)(2,1)}), bf16[1024,1536]{1,0:T(8,128)(2,1)}) %all-gather.5.cloned.1.call-update) | async-done | bytes 3145744 | tf_op jit(solution)/shard_map/all_gather | solution.py:349
  148.7 2.9 %convolution_add_fusion.1 = f32[256,1024]{1,0:T(8,128)S(1)} fusion(f32[256,1024]{1,0:T(8,128)S(1)} %fusion.15, bf16[1024,1536]{1,0:T(8,128)(2,1)} %all-gather.5.cloned.1.call-done, bf16[256,1024]{1,0:T(8,128)(2,1)S(1)} %copy-done, bf16[256,1024]{1,0:T(8,128)(2,1)S(1)} %get-tuple-element.71), kind=kOutput, calls=%fused_computation.12 | convolution fusion | flops 807141376 | bytes 6291456 | tf_op jit(solution)/shard_map/dot_general | solution.py:357
  151.7 1.0 fusion.18
  152.9 4.7 %fusion.4 = f32[32,8,3072]{2,1,0:T(8,128)S(1)} fusion(bf16[1024,1536]{1,0:T(8,128)(2,1)} %all-gather.5.cloned.1.call-done, bf16[1024,1536]{1,0:T(8,128)(2,1)} %all-gather.3.cloned.1.call-done, bf16[256,512]{1,0:T(8,128)(2,1)S(1)} %get-tuple-element.67, bf16[256,512]{1,0:T(8,128)(2,1)S(1)} %get-tuple-element.66), kind=kOutput, calls=%fused_computation.5 | convolution fusion | flops 1624244224 | bytes 9961472 | tf_op jit(solution)/shard_map/dot_general | solution.py:387
  157.7 0.4 fusion.46
  158.1 0.6 copy.48
  158.8 4.5 %convolution_convert_fusion = bf16[1024,3072]{1,0:T(8,128)(2,1)} fusion(bf16[256,1024]{0,1:T(8,128)(2,1)S(1)} %bitcast.51, bf16[256,1024]{1,0:T(8,128)(2,1)S(1)} %copy-done, bf16[256,1024]{1,0:T(8,128)(2,1)S(1)} %get-tuple-element.71, bf16[256,1024]{1,0:T(8,128)(2,1)S(1)} %get-tuple-element.72), kind=kOutput, calls=%fused_computation.4 | convolution fusion | flops 1618477056 | bytes 8388608 | tf_op jit(solution)/shard_map/dot_general | solution.py:384
  163.5 1.0 fusion.13
  165.1 86.8 %shard_map.72 = (f32[2,16,3072]{2,1,0:T(8,128)S(1)}, bf16[32,8,1024]{2,1,0:T(8,128)(2,1)S(1)}) custom-call(bf16[2,4,128,3072]{3,2,1,0:T(8,128)(2,1)} %bitcast.45, bf16[32,8,1024]{2,1,0:T(8,128)(2,1)S(1)} %copy.65.back_ref), custom_call_target="tpu_custom_call" | custom-call | tf_op jit(solution)/shard_map/pallas_call | solution.py:287
  251.9 1.3 fusion.12
  253.2 1.1 copy.66
  254.3 0.7 copy.69
  (20 shorter events, 1.6 us)
Async XLA Ops:
  7.2 33.3 %copy-start.2 = (s32[1,32]{1,0:T(1,128)S(1)}, s32[1,32]{1,0:T(1,128)}, u32[]{:S(2)}) copy-start(s32[1,32]{1,0:T(1,128)} %param.17) | copy-start | bytes 388
  7.2 33.0 %copy-start = (bf16[256,1024]{1,0:T(8,128)(2,1)S(1)}, bf16[256,1024]{1,0:T(8,128)(2,1)}, u32[]{:S(2)}) copy-start(bf16[256,1024]{1,0:T(8,128)(2,1)} %param.14) | copy-start | bytes 1572868
  7.2 77.3 %all-gather.3.cloned.1.call-start = ((), (), s32[]{:S(2)}) async-start(), calls=%async_computation.2 | async-start | bytes 3244032 | tf_op jit(solution)/shard_map/all_gather | solution.py:348
  8.9 139.8 %all-gather.5.cloned.1.call-start = ((), (), s32[]{:S(2)}) async-start(), calls=%async_computation.3 | async-start | bytes 3244032 | tf_op jit(solution)/shard_map/all_gather | solution.py:349
  34.4 21.3 %all-to-all-start.1 = ((bf16[32,8,1024]{2,1,0:T(8,128)(2,1)}), bf16[32,8,1024]{2,1,0:T(8,128)(2,1)S(1)}, u32[]{:S(2)}, u32[]{:S(2)}) async-start(bf16[32,8,1024]{2,1,0:T(8,128)(2,1)} %copy.28), calls=%async_computation.1 | async-start | bytes 1048576 | tf_op jit(solution)/shard_map/all_to_all | solution.py:341
  87.4 64.2 %copy-start.1 = (bf16[256,512]{1,0:T(8,128)(2,1)S(1)}, bf16[256,512]{1,0:T(8,128)(2,1)}, u32[]{:S(2)}) copy-start(bf16[256,512]{1,0:T(8,128)(2,1)} %param.15) | copy-start | bytes 786436
Sparse Core Ops, SparseCore 0:
  11.7 72.7 all-gather.2
  88.2 60.5 all-gather.4

commit v14 on v12

--- a/solution.py
+++ b/solution.py
@@ -374,16 +374,27 @@
         routed, stacked, contract_first, preferred_element_type=jnp.float32
     ).astype(jnp.bfloat16)
     back_proj = jnp.dot(grad_pre, full_weight, preferred_element_type=jnp.float32)
-    back_proj = back_proj.reshape(seg_count, seg_rows, 3 * C)
-    grad_ext = jnp.zeros((seg_count, context_row_block + seg_rows, C), jnp.float32)
-    for selected_index, start in enumerate(starts):
-        grad_ext = grad_ext.at[:, start : start + seg_rows, :].add(
-            back_proj[:, :, selected_index * C : (selected_index + 1) * C]
-        )
+    row_in_seg = lax.rem(lax.broadcasted_iota(jnp.int32, (row_count, 1), 0), seg_rows)
+    taps = [back_proj[:, selected_index * C : (selected_index + 1) * C] for selected_index in range(3)]
+
+    def extended_rows(first):
+        total = None
+        for selected_index, start in enumerate(starts):
+            shift = first - start
+            if shift <= -seg_rows or shift >= seg_rows:
+                continue
+            term = taps[selected_index]
+            if shift != 0:
+                inside = (row_in_seg + shift >= 0) & (row_in_seg + shift < seg_rows)
+                term = jnp.where(inside, jnp.roll(term, -shift, axis=0), 0.0)
+            total = term if total is None else total + term
+        return total
+
+    carry_rows = extended_rows(0).reshape(seg_count, seg_rows, C)
     outgoing_grad = jnp.einsum(
         "sn,slc->nlc",
         recv_table,
-        grad_ext[:, :context_row_block, :].astype(jnp.bfloat16),
+        carry_rows.astype(jnp.bfloat16),
         preferred_element_type=jnp.float32,
     ).astype(jnp.bfloat16)
     total_token_count = row_count * peer_count * lax.axis_size("dp")
@@ -400,10 +411,8 @@
         incoming_grad,
         preferred_element_type=jnp.float32,
     )
-    grad_in = (
-        grad_ext[:, context_row_block:, :].at[:, seg_rows - context_row_block :, :].add(tail_grad)
-    )
-    grad_in = grad_in.reshape(row_count, C).astype(jnp.bfloat16)
+    grad_in = extended_rows(context_row_block) + tail_grad.reshape(row_count, C)
+    grad_in = grad_in.astype(jnp.bfloat16)
     return (gated_out, grad_in, grad_weight)
 
 

time: 212 us -> 215 us (1.014)
  matrix products: 18.1 us -> 15.4 us
  other arithmetic: 2.8 us -> 5.01 us
    convert_element_type x0 -> x2, other arithmetic: none -> 3.19 us  [the longest x1 1.61 us: per_device(): grad_in = grad_in.astype(jnp.bfloat16)]
    dot_general x1, matrix products: 4.68 us -> 1.79 us  [per_device(): jnp.dot(grad_pre, full_weight, preferred_element_type=jnp.float32)]
    another operation x2, local copies, waits for them, and re-layouts: 0.26 us -> 2.87 us
  transfers between devices with their start and end apart: 2 -> 2, of which waited for: 2 -> 2; matrix products, arithmetic and copies ran while one was open for 3% -> 2% of each run, Pallas kernels for 0% -> 0%
where the time goes in v14:
time: 215 us; the launch traced here: 213 us
  Pallas kernels  86.8 us (40%)
  waiting for transfers between devices  57.5 us (27%)
  blocking collectives  21.1 us (10%)
  matrix products  15.4 us (7%)
  between operations  14.3 us (7%)
  local copies, waits for them, and re-layouts  7.49 us (3%)
  starting transfers between devices  5.81 us (3%)
  other arithmetic  5.01 us (2%)
    pallas_call x1, Pallas kernels, grad_reduce(): pl.pallas_call(functools.partial(grad_reduce_kernel, z_hi, scale), out_sh...  86.8 us
    all_gather x1, waiting for transfers between devices, per_device(): full_weight = lax.all_gather(conv_weight, 'fsdp', axis=0, tiled=True)  38.9 us
    all_to_all x1, blocking collectives, per_device(): lax.all_to_all(request_mask, 'fsdp', split_axis=0, concat_axis=0, tiled=T...  21.1 us
    all_to_all x1, waiting for transfers between devices, per_device(): lax.all_to_all(outgoing, 'fsdp', split_axis=0, concat_axis=0, tiled=True)  17.9 us
    all_to_all x1, starting transfers between devices, per_device(): lax.all_to_all(outgoing, 'fsdp', split_axis=0, concat_axis=0, tiled=True)  5.78 us
    dot_general x1, matrix products, per_device(): lax.dot_general(stacked, full_weight, contract_final_axis, preferred_elem...  4.94 us
    dot_general x1, matrix products, per_device(): lax.dot_general(routed, stacked, contract_first, preferred_element_type=j...  4.46 us
  transfers between devices with their start and end apart: 2, of which 2 were waited for; matrix products, arithmetic and copies ran while one was open for 2% of the time, Pallas kernels for 0%

profile of v14, /device:TPU:6, one launch (start us, length us, event | category | flops | bytes accessed | tf_op | source)
XLA Modules:
  0.0 213.4 jit_solution(8458468025577541419)
XLA Ops:
  7.2 0.7 all-gather.2.cloned.1.call-update
  7.9 0.7 fusion.31
  8.6 21.1 %all_to_all.11 = s32[32,1,32]{2,1,0:T(1,128)S(1)} all-to-all(s32[32,1,32]{2,1,0:T(1,128)S(1)} %compare_convert_fusion), channel_id=1, replica_groups=mesh['dp'=16,'fsdp'=32] {'fsdp'}, dimensions={0} | all-to-all | bytes 8192 | tf_op jit(solution)/shard_map/all_to_all | solution.py:335
  29.7 1.8 convolution_convert_fusion.2
  31.6 1.1 copy.25
  32.7 5.8 %all-to-all-start.1 = ((bf16[32,8,1024]{2,1,0:T(8,128)(2,1)}), bf16[32,8,1024]{2,1,0:T(8,128)(2,1)S(1)}, u32[]{:S(2)}, u32[]{:S(2)}) async-start(bf16[32,8,1024]{2,1,0:T(8,128)(2,1)} %copy.25), calls=%async_computation.1 | async-start | bytes 1048576 | tf_op jit(solution)/shard_map/all_to_all | solution.py:341
  38.4 0.3 copy.24
  38.8 17.9 %all-to-all-done.1 = bf16[32,8,1024]{2,1,0:T(8,128)(2,1)S(1)} async-done(((bf16[32,8,1024]{2,1,0:T(8,128)(2,1)}), bf16[32,8,1024]{2,1,0:T(8,128)(2,1)S(1)}, u32[]{:S(2)}, u32[]{:S(2)}) %all-to-all-start.1) | async-done | bytes 524320 | tf_op jit(solution)/shard_map/all_to_all | solution.py:341
  56.7 0.8 convolution_convert_fusion.1
  57.5 0.6 copy_bitcast_fusion
  58.1 38.9 %all-gather.2.cloned.1.call-done = bf16[1024,3072]{1,0:T(8,128)(2,1)} async-done(((bf16[32,3072]{1,0:T(8,128)(2,1)}), bf16[1024,3072]{1,0:T(8,128)(2,1)}) %all-gather.2.cloned.1.call-update) | async-done | bytes 6291472 | tf_op jit(solution)/shard_map/all_gather | solution.py:346
  97.0 4.9 %fusion.3 = f32[256,1024]{1,0:T(8,128)S(1)} fusion(bf16[1024,3072]{1,0:T(8,128)(2,1)} %all-gather.2.cloned.1.call-done, bf16[256,1024]{1,0:T(8,128)(2,1)S(1)} %copy-done.1, bf16[256,1024]{1,0:T(8,128)(2,1)S(1)} %get-tuple-element.14, bf16[256,1024]{1,0:T(8,128)(2,1)S(1)} %get-tuple-element.15), kind=kOutput, calls=%fused_computation.14 | convolution fusion | flops 1615331328 | bytes 8912896 | tf_op jit(solution)/shard_map/dot_general | solution.py:351
  102.0 1.0 fusion.5
  103.0 1.8 fusion.13
  104.8 1.5 fusion.37
  106.4 1.1 copy.31
  107.5 1.8 copy.32
  109.3 1.6 fusion.9
  110.9 0.8 fusion.19
  112.1 4.5 %convolution_convert_fusion = bf16[1024,3072]{1,0:T(8,128)(2,1)} fusion(bf16[256,1024]{0,1:T(8,128)(2,1)S(1)} %bitcast.49, bf16[256,1024]{1,0:T(8,128)(2,1)S(1)} %copy-done.2, bf16[256,1024]{1,0:T(8,128)(2,1)S(1)} %copy-done.7, bf16[256,1024]{1,0:T(8,128)(2,1)S(1)} %copy-done.9), kind=kOutput, calls=%fused_computation | convolution fusion | flops 1618477056 | bytes 8388608 | tf_op jit(solution)/shard_map/dot_general | solution.py:373
  116.5 86.8 %shard_map.67 = (f32[2,16,3072]{2,1,0:T(8,128)S(1)}, bf16[32,8,1024]{2,1,0:T(8,128)(2,1)S(1)}) custom-call(bf16[2,4,128,3072]{3,2,1,0:T(8,128)(2,1)} %bitcast.44, bf16[32,8,1024]{2,1,0:T(8,128)(2,1)S(1)} %copy.55.back_ref), custom_call_target="tpu_custom_call" | custom-call | tf_op jit(solution)/shard_map/pallas_call | solution.py:287
  203.3 0.8 fusion.17
  204.2 1.6 fusion.2
  205.8 0.7 copy.57
  (36 shorter events, 0.6 us)
Async XLA Ops:
  7.2 31.6 %copy-start.12 = (s32[1,32]{1,0:T(1,128)S(1)}, s32[1,32]{1,0:T(1,128)}, u32[]{:S(2)}) copy-start(s32[1,32]{1,0:T(1,128)} %param.7) | copy-start | bytes 388
  7.2 31.3 %copy-start.1 = (bf16[256,1024]{1,0:T(8,128)(2,1)S(1)}, bf16[256,1024]{1,0:T(8,128)(2,1)}, u32[]{:S(2)}) copy-start(bf16[256,1024]{1,0:T(8,128)(2,1)} %param.4) | copy-start | bytes 1572868
  7.2 89.8 %all-gather.2.cloned.1.call-start = ((), (), s32[]{:S(2)}) async-start(), calls=%async_computation.2 | async-start | bytes 6488064 | tf_op jit(solution)/shard_map/all_gather | solution.py:346
  32.7 24.0 %all-to-all-start.1 = ((bf16[32,8,1024]{2,1,0:T(8,128)(2,1)}), bf16[32,8,1024]{2,1,0:T(8,128)(2,1)S(1)}, u32[]{:S(2)}, u32[]{:S(2)}) async-start(bf16[32,8,1024]{2,1,0:T(8,128)(2,1)} %copy.25), calls=%async_computation.1 | async-start | bytes 1048576 | tf_op jit(solution)/shard_map/all_to_all | solution.py:341
  58.1 43.9 %copy-start.6 = (bf16[256,1024]{1,0:T(8,128)(2,1)}, bf16[256,1024]{1,0:T(8,128)(2,1)S(1)}, u32[]{:S(2)}) copy-start(bf16[256,1024]{1,0:T(8,128)(2,1)S(1)} %get-tuple-element.14) | copy-start | bytes 1572868
  58.1 43.9 %copy-start.8 = (bf16[256,1024]{1,0:T(8,128)(2,1)}, bf16[256,1024]{1,0:T(8,128)(2,1)S(1)}, u32[]{:S(2)}) copy-start(bf16[256,1024]{1,0:T(8,128)(2,1)S(1)} %get-tuple-element.15) | copy-start | bytes 1572868
  97.0 5.0 %copy-start.10 = (bf16[256,512]{1,0:T(8,128)(2,1)S(1)}, bf16[256,512]{1,0:T(8,128)(2,1)}, u32[]{:S(2)}) copy-start(bf16[256,512]{1,0:T(8,128)(2,1)} %param.5) | copy-start | bytes 786436
  97.0 6.0 %copy-start.11 = (bf16[1024,3072]{1,0:T(8,128)(2,1)S(1)}, bf16[1024,3072]{1,0:T(8,128)(2,1)}, u32[]{:S(2)}) copy-start(bf16[1024,3072]{1,0:T(8,128)(2,1)} %all-gather.2.cloned.1.call-done) | copy-start | bytes 18874372
  103.0 1.8 copy-start.4
  103.0 1.8 copy-start.5
  109.3 2.7 %copy-start.3 = (bf16[256,512]{0,1:T(8,128)(2,1)S(1)}, bf16[256,512]{0,1:T(8,128)(2,1)}, u32[]{:S(2)}) copy-start(bf16[256,512]{0,1:T(8,128)(2,1)} %copy.32) | copy-start | bytes 786436
  109.3 2.8 %copy-start.2 = (bf16[256,1024]{1,0:T(8,128)(2,1)S(1)}, bf16[256,1024]{1,0:T(8,128)(2,1)}, u32[]{:S(2)}) copy-start(bf16[256,1024]{1,0:T(8,128)(2,1)} %param.4) | copy-start | bytes 1572868
  109.3 2.8 %copy-start.7 = (bf16[256,1024]{1,0:T(8,128)(2,1)S(1)}, bf16[256,1024]{1,0:T(8,128)(2,1)}, u32[]{:S(2)}) copy-start(bf16[256,1024]{1,0:T(8,128)(2,1)} %copy-done.6) | copy-start | bytes 1572868
  109.3 2.8 %copy-start.9 = (bf16[256,1024]{1,0:T(8,128)(2,1)S(1)}, bf16[256,1024]{1,0:T(8,128)(2,1)}, u32[]{:S(2)}) copy-start(bf16[256,1024]{1,0:T(8,128)(2,1)} %copy-done.8) | copy-start | bytes 1572868
  116.5 87.6 %copy-start = (f32[252,1024]{1,0:T(8,128)S(1)}, f32[252,1024]{1,0:T(8,128)}, u32[]{:S(2)}) copy-start(f32[252,1024]{1,0:T(8,128)} %get-tuple-element.10) | copy-start | bytes 3096580
Sparse Core Ops, SparseCore 0:
  11.1 85.8 all-gather.1
